TPU v7x, 32 devices: a whole 2x2x4 slice. The times are simulated.
32 devices in a mesh: dp: 8 (over y, x, core), tensor: 4 (over z).
Axes of the slice: x: 2, y: 2, z: 4, core: 2. Of those that a mesh axis runs over, the one named last changes fastest.
Arguments:
- tokens_in: bfloat16 [18464, 1024], P('dp', 'tensor'), may hold values from -6 to 6
- cotangent: bfloat16 [18464, 1024], P('dp', 'tensor'), may hold values from -6 to 6
- slot_mask: int32 [32], P('dp'), may hold values 0 or 1
- norm1_gain: float32 [4, 256], P('tensor', 'dp'), may hold values from 0.1 to 1.9
- norm1_bias: float32 [4, 256], P('tensor', 'dp'), may hold values from -4 to 4
- w_qkv: float32 [1024, 3, 1024], P('dp', None, 'tensor')
- b_qkv: float32 [2, 4, 256], P(None, 'tensor', 'dp'), may hold values from -6 to 6
- w_out: float32 [1024, 1024], P('tensor', 'dp'), may hold values from -1.5 to 1.5
- b_out: float32 [4, 256], P('tensor', 'dp'), may hold values from -4 to 4
- norm2_gain: float32 [4, 256], P('tensor', 'dp'), may hold values from 0.1 to 1.9
- norm2_bias: float32 [4, 256], P('tensor', 'dp'), may hold values from -4 to 4
- w_fc1: float32 [1024, 4096], P('dp', 'tensor')
- b_fc1: float32 [4, 1024], P('tensor', 'dp'), may hold values from -6 to 6
- w_fc2: float32 [4096, 1024], P('tensor', 'dp'), may hold values from -0.09375 to 0.09375
- b_fc2: float32 [4, 256], P('tensor', 'dp'), may hold values from -4 to 4
Outputs:
- block_out: bfloat16 [18464, 1024], P('dp', 'tensor')
- grad_tokens: bfloat16 [18464, 1024], P('dp', 'tensor')
- grad_norm1_gain: float32 [4, 256], P('tensor', 'dp')
- grad_norm1_bias: float32 [4, 256], P('tensor', 'dp')
- grad_w_qkv: float32 [1024, 3, 1024], P('dp', None, 'tensor')
- grad_b_qkv: float32 [2, 4, 256], P(None, 'tensor', 'dp')
- grad_w_out: float32 [1024, 1024], P('tensor', 'dp')
- grad_b_out: float32 [4, 256], P('tensor', 'dp')
- grad_norm2_gain: float32 [4, 256], P('tensor', 'dp')
- grad_norm2_bias: float32 [4, 256], P('tensor', 'dp')
- grad_w_fc1: float32 [1024, 4096], P('dp', 'tensor')
- grad_b_fc1: float32 [4, 1024], P('tensor', 'dp')
- grad_w_fc2: float32 [4096, 1024], P('tensor', 'dp')
- grad_b_fc2: float32 [4, 256], P('tensor', 'dp')
All inputs are finite; a program needn't handle non-finite values. No bound on the sum of `slot_mask` on one device may be relied on, other than what follows from the above.
Results may differ from a plain program's by a relative error of at most 0.025.
Values may be sent and summed in bfloat16 or wider, within the bound.
A program may use at most 192 MiB of HBM per device.

v0:
```python
import jax
import jax.numpy as jnp
from jax import lax
from jax.sharding import PartitionSpec as P

D = 1024
HD = 64
SEQ = 577


def row_total(partial_sum):
    return lax.psum(partial_sum, "tensor")


def grad_total(first_sum, second_sum):
    return lax.psum((first_sum, second_sum), "tensor")


def layer_norm_slice(values):
    mean_row = row_total(jnp.sum(values, axis=1, keepdims=True)) / D
    centered = values - mean_row
    variance = row_total(jnp.sum(centered * centered, axis=1, keepdims=True)) / D
    inv_std = lax.rsqrt(variance + 1e-05)
    return (centered * inv_std, inv_std)


def norm_backward(grad_normed, normed, inv_std, gain):
    scaled = grad_normed * gain
    first_sum, second_sum = grad_total(
        jnp.sum(scaled, axis=1, keepdims=True), jnp.sum(scaled * normed, axis=1, keepdims=True)
    )
    grad_input = inv_std * (scaled - first_sum / D - normed * (second_sum / D))
    grad_gain = jnp.sum(grad_normed * normed, axis=0, keepdims=True)
    grad_shift = jnp.sum(grad_normed, axis=0, keepdims=True)
    return (grad_input, grad_gain, grad_shift)


def attend(image_entry):
    queries, key_rows, value_rows = image_entry
    scale_factor = queries.shape[-1] ** (-0.5)
    scores = (
        jnp.einsum("qhe,khe->hqk", queries, key_rows, preferred_element_type=jnp.float32)
        * scale_factor
    )
    top_score = jnp.max(scores, axis=2, keepdims=True)
    shifted = jnp.exp(scores - top_score)
    exp_total = jnp.sum(shifted, axis=2, keepdims=True)
    attn_probs = (shifted / exp_total).astype(jnp.bfloat16)
    context = jnp.einsum(
        "hqk,khe->qhe", attn_probs, value_rows, preferred_element_type=jnp.float32
    ).astype(jnp.bfloat16)
    return (context, top_score + jnp.log(exp_total))


def attend_back(image_entry):
    queries, key_rows, value_rows, grad_context, log_total = image_entry
    scale_factor = queries.shape[-1] ** (-0.5)
    scores = (
        jnp.einsum("qhe,khe->hqk", queries, key_rows, preferred_element_type=jnp.float32)
        * scale_factor
    )
    soft_probs = jnp.exp(scores - log_total)
    probs_low = soft_probs.astype(jnp.bfloat16)
    grad_probs = jnp.einsum(
        "qhe,khe->hqk", grad_context, value_rows, preferred_element_type=jnp.float32
    )
    grad_values = jnp.einsum(
        "hqk,qhe->khe", probs_low, grad_context, preferred_element_type=jnp.float32
    )
    grad_scores = soft_probs * (
        grad_probs - jnp.sum(soft_probs * grad_probs, axis=2, keepdims=True)
    )
    scores_low = (grad_scores * scale_factor).astype(jnp.bfloat16)
    grad_queries = jnp.einsum(
        "hqk,khe->qhe", scores_low, key_rows, preferred_element_type=jnp.float32
    )
    grad_keys = jnp.einsum("hqk,qhe->khe", scores_low, queries, preferred_element_type=jnp.float32)
    return (grad_queries, grad_keys, grad_values)


def on_device(
    tokens_in,
    cotangent,
    slot_mask,
    norm1_gain,
    norm1_bias,
    w_qkv,
    b_qkv,
    w_out,
    b_out,
    norm2_gain,
    norm2_bias,
    w_fc1,
    b_fc1,
    w_fc2,
    b_fc2,
):
    tok_rows = tokens_in.shape[0]
    image_count = tok_rows // SEQ
    gathered = (
        lax.all_gather(norm1_gain.astype(jnp.bfloat16), "dp", axis=1, tiled=True),
        lax.all_gather(norm1_bias.astype(jnp.bfloat16), "dp", axis=1, tiled=True),
        lax.all_gather(w_qkv.astype(jnp.bfloat16), "dp", axis=0, tiled=True),
        lax.all_gather(b_qkv.astype(jnp.bfloat16), "dp", axis=2, tiled=True),
        lax.all_gather(w_out.astype(jnp.bfloat16), "dp", axis=1, tiled=True),
        lax.all_gather(b_out.astype(jnp.bfloat16), "dp", axis=1, tiled=True),
        lax.all_gather(norm2_gain.astype(jnp.bfloat16), "dp", axis=1, tiled=True),
        lax.all_gather(norm2_bias.astype(jnp.bfloat16), "dp", axis=1, tiled=True),
        lax.all_gather(w_fc1.astype(jnp.bfloat16), "dp", axis=0, tiled=True),
        lax.all_gather(b_fc1.astype(jnp.bfloat16), "dp", axis=1, tiled=True),
        lax.all_gather(w_fc2.astype(jnp.bfloat16), "dp", axis=1, tiled=True),
        lax.all_gather(b_fc2.astype(jnp.bfloat16), "dp", axis=1, tiled=True),
    )
    (
        gain_one,
        shift_one,
        weight_mix,
        bias_mix,
        weight_proj,
        bias_proj,
        gain_two,
        shift_two,
        weight_up,
        bias_up,
        weight_down,
        bias_down,
    ) = gathered
    gain_one_f = gain_one.astype(jnp.float32)
    gain_two_f = gain_two.astype(jnp.float32)
    mask_values = slot_mask.astype(jnp.float32)[:, None, None]

    def masked(values):
        return (values.reshape(image_count, SEQ, -1) * mask_values).reshape(tok_rows, -1)

    inputs_f = tokens_in.astype(jnp.float32)
    normed_one, inv_one = layer_norm_slice(inputs_f)
    normed_in = lax.all_gather(
        (normed_one * gain_one_f + shift_one.astype(jnp.float32)).astype(jnp.bfloat16),
        "tensor",
        axis=1,
        tiled=True,
    )
    mixed = jnp.einsum("td,dcf->tcf", normed_in, weight_mix, preferred_element_type=jnp.float32)
    bias_pair = bias_mix.astype(jnp.float32)
    heads_local = mixed.shape[2] // HD
    head_shape = (image_count, SEQ, heads_local, HD)
    query_heads = (mixed[:, 0] + bias_pair[0]).astype(jnp.bfloat16).reshape(head_shape)
    key_heads = mixed[:, 1].astype(jnp.bfloat16).reshape(head_shape)
    value_heads = (mixed[:, 2] + bias_pair[1]).astype(jnp.bfloat16).reshape(head_shape)
    context, log_total = lax.map(attend, (query_heads, key_heads, value_heads))
    context_flat = context.reshape(tok_rows, -1)
    attn_out = lax.psum_scatter(
        jnp.dot(context_flat, weight_proj, preferred_element_type=jnp.float32).astype(jnp.bfloat16),
        "tensor",
        scatter_dimension=1,
        tiled=True,
    ).astype(jnp.float32)
    resid_mid = inputs_f + attn_out + bias_proj.astype(jnp.float32)
    normed_two, inv_two = layer_norm_slice(resid_mid)
    normed_mid = lax.all_gather(
        (normed_two * gain_two_f + shift_two.astype(jnp.float32)).astype(jnp.bfloat16),
        "tensor",
        axis=1,
        tiled=True,
    )
    pre_act = jnp.dot(normed_mid, weight_up, preferred_element_type=jnp.float32) + bias_up.astype(
        jnp.float32
    )
    sig_gate = jax.nn.sigmoid(1.702 * pre_act)
    activation = (pre_act * sig_gate).astype(jnp.bfloat16)
    mlp_out = lax.psum_scatter(
        jnp.dot(activation, weight_down, preferred_element_type=jnp.float32).astype(jnp.bfloat16),
        "tensor",
        scatter_dimension=1,
        tiled=True,
    ).astype(jnp.float32)
    block_out = masked(resid_mid + mlp_out + bias_down.astype(jnp.float32)).astype(jnp.bfloat16)
    grad_res = masked(cotangent.astype(jnp.float32))
    grad_b_fc2 = jnp.sum(grad_res, axis=0, keepdims=True)
    grad_mlp = lax.all_gather(grad_res.astype(jnp.bfloat16), "tensor", axis=1, tiled=True)
    grad_w_fc2 = jnp.einsum("tf,td->fd", activation, grad_mlp, preferred_element_type=jnp.float32)
    grad_act = jnp.einsum("td,fd->tf", grad_mlp, weight_down, preferred_element_type=jnp.float32)
    grad_pre = grad_act * (sig_gate + 1.702 * pre_act * sig_gate * (1.0 - sig_gate))
    grad_b_fc1 = jnp.sum(grad_pre, axis=0, keepdims=True)
    grad_pre_low = grad_pre.astype(jnp.bfloat16)
    grad_w_fc1 = jnp.einsum(
        "td,tf->df", normed_mid, grad_pre_low, preferred_element_type=jnp.float32
    )
    grad_normed_mid = lax.psum_scatter(
        jnp.einsum("tf,df->td", grad_pre_low, weight_up, preferred_element_type=jnp.float32).astype(
            jnp.bfloat16
        ),
        "tensor",
        scatter_dimension=1,
        tiled=True,
    ).astype(jnp.float32)
    grad_mid, grad_norm2_gain, grad_norm2_bias = norm_backward(
        grad_normed_mid, normed_two, inv_two, gain_two_f
    )
    grad_resid = grad_res + grad_mid
    grad_b_out = jnp.sum(grad_resid, axis=0, keepdims=True)
    grad_attn = lax.all_gather(grad_resid.astype(jnp.bfloat16), "tensor", axis=1, tiled=True)
    grad_w_out = jnp.einsum(
        "tf,td->fd", context_flat, grad_attn, preferred_element_type=jnp.float32
    )
    grad_context = jnp.einsum(
        "td,fd->tf", grad_attn, weight_proj, preferred_element_type=jnp.float32
    ).astype(jnp.bfloat16)
    grad_queries, grad_keys, grad_values = lax.map(
        attend_back,
        (query_heads, key_heads, value_heads, grad_context.reshape(head_shape), log_total),
    )
    grad_queries = grad_queries.reshape(tok_rows, -1)
    grad_keys = grad_keys.reshape(tok_rows, -1)
    grad_values = grad_values.reshape(tok_rows, -1)
    grad_b_qkv = jnp.stack((jnp.sum(grad_queries, axis=0), jnp.sum(grad_values, axis=0)))[
        :, None, :
    ]
    grad_mixed = jnp.stack((grad_queries, grad_keys, grad_values), axis=1).astype(jnp.bfloat16)
    grad_w_qkv = jnp.einsum(
        "td,tcf->dcf", normed_in, grad_mixed, preferred_element_type=jnp.float32
    )
    grad_normed_in = lax.psum_scatter(
        jnp.einsum(
            "tcf,dcf->td", grad_mixed, weight_mix, preferred_element_type=jnp.float32
        ).astype(jnp.bfloat16),
        "tensor",
        scatter_dimension=1,
        tiled=True,
    ).astype(jnp.float32)
    grad_first, grad_norm1_gain, grad_norm1_bias = norm_backward(
        grad_normed_in, normed_one, inv_one, gain_one_f
    )
    grad_tokens = (grad_resid + grad_first).astype(jnp.bfloat16)
    summed = tuple(
        (
            lax.psum_scatter(grad_norm1_gain, "dp", scatter_dimension=1, tiled=True),
            lax.psum_scatter(grad_norm1_bias, "dp", scatter_dimension=1, tiled=True),
            lax.psum_scatter(grad_w_qkv, "dp", scatter_dimension=0, tiled=True),
            lax.psum_scatter(grad_b_qkv, "dp", scatter_dimension=2, tiled=True),
            lax.psum_scatter(grad_w_out, "dp", scatter_dimension=1, tiled=True),
            lax.psum_scatter(grad_b_out, "dp", scatter_dimension=1, tiled=True),
            lax.psum_scatter(grad_norm2_gain, "dp", scatter_dimension=1, tiled=True),
            lax.psum_scatter(grad_norm2_bias, "dp", scatter_dimension=1, tiled=True),
            lax.psum_scatter(grad_w_fc1, "dp", scatter_dimension=0, tiled=True),
            lax.psum_scatter(grad_b_fc1, "dp", scatter_dimension=1, tiled=True),
            lax.psum_scatter(grad_w_fc2, "dp", scatter_dimension=1, tiled=True),
            lax.psum_scatter(grad_b_fc2, "dp", scatter_dimension=1, tiled=True),
        )
    )
    return (block_out, grad_tokens) + summed


def solution(mesh):
    placed = (
        P("dp", "tensor"),
        P("dp", "tensor"),
        P("dp"),
        P("tensor", "dp"),
        P("tensor", "dp"),
        P("dp", None, "tensor"),
        P(None, "tensor", "dp"),
        P("tensor", "dp"),
        P("tensor", "dp"),
        P("tensor", "dp"),
        P("tensor", "dp"),
        P("dp", "tensor"),
        P("tensor", "dp"),
        P("tensor", "dp"),
        P("tensor", "dp"),
    )
    return jax.shard_map(
        on_device,
        mesh=mesh,
        in_specs=placed,
        out_specs=(
            P("dp", "tensor"),
            P("dp", "tensor"),
            P("tensor", "dp"),
            P("tensor", "dp"),
            P("dp", None, "tensor"),
            P(None, "tensor", "dp"),
            P("tensor", "dp"),
            P("tensor", "dp"),
            P("tensor", "dp"),
            P("tensor", "dp"),
            P("dp", "tensor"),
            P("tensor", "dp"),
            P("tensor", "dp"),
            P("tensor", "dp"),
        ),
        check_vma=False,
    )
```

profile of v0, /device:TPU:10, one launch (start us, length us, event | category | flops | bytes accessed | tf_op | source)
XLA Modules:
  0.0 1606.1 jit_solution(14664923070070772784)
XLA Ops:
  16.1 11.7 all-reduce.8
  29.5 9.2 psum.56
  39.6 12.1 psum.57
  54.8 10.8 all_gather.52
  67.4 10.1 all_gather.53
  77.5 63.7 %all-gather.8.cloned.1.call-done = bf16[2308,1024]{1,0:T(8,128)(2,1)} async-done(((bf16[2308,256]{1,0:T(8,128)(2,1)}), bf16[2308,1024]{1,0:T(8,128)(2,1)}) %all-gather.8.cloned.1.call-update) | async-done | bytes 4726800 | tf_op jit(solution)/shard_map/all_gather | solution.py:137
  141.2 6.4 fusion.86
  152.6 4.3 squeeze.34
  159.4 4.6 reshape.163
  164.0 4.3 copy.120
  171.4 4.3 squeeze.33
  179.2 27.7 %while.26 = (s32[]{:T(128)}, bf16[4,577,4,64]{1,3,2,0:T(8,128)(2,1)}, f32[4,4,577,1]{2,1,3,0:T(4,128)}, bf16[4,577,4,64]{1,3,2,0:T(8,128)(2,1)}, bf16[4,577,4,64...) while((s32[]{:T(128)}, bf16[4,577,4,64]{1,3,2,0:T(8,128)(2,1)}, ...), condition=%wide.region_7.8_spmd, body=%wide.region_4.7_spmd.sunk | while | flops 353050112 | bytes 17368312 | solution.py:150
  206.9 3.9 copy.121
  210.8 4.0 reshape.90
  214.8 4.9 convolution_convert_fusion.2
  222.7 83.8 %reduce-scatter.33.cloned.1.call-done = bf16[2308,256]{1,0:T(8,128)(2,1)} async-done(((bf16[2308,1024]{1,0:T(8,128)(2,1)}), bf16[2308,256]{1,0:T(8,128)(2,1)}) %reduce-scatter.33.cloned.1.call-update) | async-done | bytes 1181712 | tf_op jit(solution)/shard_map/reduce_scatter | solution.py:152
  308.3 9.7 psum.58
  319.6 10.9 psum.59
  342.2 8.7 all_gather.59
  350.8 75.1 %all-gather.12.cloned.1.call-done = bf16[2308,1024]{1,0:T(8,128)(2,1)} async-done(((bf16[2308,256]{1,0:T(8,128)(2,1)}), bf16[2308,1024]{1,0:T(8,128)(2,1)}) %all-gather.12.cloned.1.call-update) | async-done | bytes 4726800 | tf_op jit(solution)/shard_map/all_gather | solution.py:160
  425.9 12.5 multiply_convert_fusion.1
  438.4 19.0 %all-gather.16.cloned.1.call-done = bf16[1024,1024]{1,0:T(8,128)(2,1)} async-done(((bf16[1024,128]{1,0:T(8,128)(2,1)}), bf16[1024,1024]{1,0:T(8,128)(2,1)}) %all-gather.16.cloned.1.call-update) | async-done | bytes 2097168 | tf_op jit(solution)/shard_map/all_gather | solution.py:111
  457.4 88.8 %all-gather.18.cloned.1.call-done = bf16[2308,1024]{1,0:T(8,128)(2,1)} async-done(((bf16[2308,256]{1,0:T(8,128)(2,1)}), bf16[2308,1024]{1,0:T(8,128)(2,1)}) %all-gather.18.cloned.1.call-update) | async-done | bytes 4726800 | tf_op jit(solution)/shard_map/all_gather | solution.py:180
  546.2 12.5 fusion.124
  560.9 7.0 convolution_convert_fusion
  568.0 9.5 convolution_convert_fusion.1
  578.7 76.0 %reduce-scatter.37.cloned.1.call-done = bf16[2308,256]{1,0:T(8,128)(2,1)} async-done(((bf16[2308,1024]{1,0:T(8,128)(2,1)}), bf16[2308,256]{1,0:T(8,128)(2,1)}) %reduce-scatter.37.cloned.1.call-update) | async-done | bytes 1181712 | tf_op jit(solution)/shard_map/reduce_scatter | solution.py:189
  659.5 19.6 %all-reduce.7 = (f32[2308,1]{0,1:T(1,128)}, f32[2308,1]{0,1:T(1,128)}) all-reduce(f32[2308,1]{0,1:T(1,128)} %broadcast_in_dim.81, f32[2308,1]{0,1:T(1,128)} %broadcast_in_dim.80), channel_id=1, replica_groups=mesh['dp'=8,'tensor'=4] {'tensor'}, use_global_device_ids=true, to_apply=%region_18.19 | all-reduce | flops 4616 | bytes 36928 | tf_op jit(solution)/shard_map/psum | solution.py:16
  681.7 62.4 %reduce-scatter.35.cloned.1.call-done = bf16[2308,256]{1,0:T(8,128)(2,1)} async-done(((bf16[2308,1024]{1,0:T(8,128)(2,1)}), bf16[2308,256]{1,0:T(8,128)(2,1)}) %reduce-scatter.35.cloned.1.call-update) | async-done | bytes 1181712 | tf_op jit(solution)/shard_map/reduce_scatter | solution.py:171
  744.1 6.1 fusion.119
  752.9 87.3 %all-gather.20.cloned.1.call-done = bf16[2308,1024]{1,0:T(8,128)(2,1)} async-done(((bf16[2308,256]{1,0:T(8,128)(2,1)}), bf16[2308,1024]{1,0:T(8,128)(2,1)}) %all-gather.20.cloned.1.call-update) | async-done | bytes 4726800 | tf_op jit(solution)/shard_map/all_gather | solution.py:202
  849.6 135.4 %while.27 = (s32[]{:T(128)}, f32[4,577,4,64]{1,3,2,0:T(8,128)}, bf16[4,577,4,64]{1,3,2,0:T(8,128)(2,1)}, f32[4,577,4,64]{1,3,2,0:T(8,128)}, bf16[4,577,4,64]{1,3...) while((s32[]{:T(128)}, f32[4,577,4,64]{1,3,2,0:T(8,128)}, ...), condition=%wide.region_21.22_spmd, body=%wide.region_19.21_spmd.sunk | while | flops 880270016 | bytes 90117384 | solution.py:209
  855.3 4.7 fusion.180
  860.0 11.7 fusion.183
  871.7 11.8 fusion.182
  889.1 4.7 fusion.180
  893.8 11.6 fusion.183
  905.4 11.8 fusion.182
  922.9 4.7 fusion.180
  927.6 11.7 fusion.183
  939.3 11.8 fusion.182
  956.8 4.7 fusion.180
  961.5 11.7 fusion.183
  973.2 11.8 fusion.182
  985.0 6.7 fusion.122
  1012.5 5.7 bitcast_convert_fusion
  1025.0 80.1 %reduce-scatter.39.cloned.1.call-done = bf16[2308,256]{1,0:T(8,128)(2,1)} async-done(((bf16[2308,1024]{1,0:T(8,128)(2,1)}), bf16[2308,256]{1,0:T(8,128)(2,1)}) %reduce-scatter.39.cloned.1.call-update) | async-done | bytes 1181712 | tf_op jit(solution)/shard_map/reduce_scatter | solution.py:223
  1110.1 10.2 fusion.113
  1120.3 10.2 fusion.126
  1131.8 5.1 fusion.125
  1137.0 8.8 fusion.84
  1147.4 32.5 %reduce-scatter.55.cloned.1.call-done = f32[32,1]{1,0:T(8,128)} async-done(((f32[256,1]{1,0:T(8,128)}), f32[32,1]{1,0:T(8,128)}) %reduce-scatter.55.cloned.1.call-update) | async-done | bytes 144
  1181.2 34.9 %reduce-scatter.57.cloned.1.call-done = f32[32,1]{1,0:T(8,128)} async-done(((f32[256,1]{1,0:T(8,128)}), f32[32,1]{1,0:T(8,128)}) %reduce-scatter.57.cloned.1.call-update) | async-done | bytes 144
  1217.4 35.2 %reduce-scatter.63.cloned.1.call-done = f32[32,1]{1,0:T(8,128)} async-done(((f32[256,1]{1,0:T(8,128)}), f32[32,1]{1,0:T(8,128)}) %reduce-scatter.63.cloned.1.call-update) | async-done | bytes 144
  1254.0 34.9 %reduce-scatter.59.cloned.1.call-done = f32[32,1]{1,0:T(8,128)} async-done(((f32[256,1]{1,0:T(8,128)}), f32[32,1]{1,0:T(8,128)}) %reduce-scatter.59.cloned.1.call-update) | async-done | bytes 144
  1290.2 35.2 %reduce-scatter.53.cloned.1.call-done = f32[32,2]{1,0:T(8,128)} async-done(((f32[256,2]{1,0:T(8,128)}), f32[32,2]{1,0:T(8,128)}) %reduce-scatter.53.cloned.1.call-update) | async-done | bytes 272
  1330.9 16.6 %all-reduce.6 = (f32[2308,1]{0,1:T(1,128)}, f32[2308,1]{0,1:T(1,128)}) all-reduce(f32[2308,1]{0,1:T(1,128)} %broadcast_in_dim.83, f32[2308,1]{0,1:T(1,128)} %broadcast_in_dim.82), channel_id=1, replica_groups=mesh['dp'=8,'tensor'=4] {'tensor'}, use_global_device_ids=true, to_apply=%region_26.27 | all-reduce | flops 4616 | bytes 36928 | tf_op jit(solution)/shard_map/psum | solution.py:16
  1349.0 4.5 fusion.103
  1353.5 8.2 reduce-scatter.49.cloned.1.call-done
  1363.0 35.4 %reduce-scatter.51.cloned.1.call-done = f32[32,1]{1,0:T(8,128)} async-done(((f32[256,1]{1,0:T(8,128)}), f32[32,1]{1,0:T(8,128)}) %reduce-scatter.51.cloned.1.call-update) | async-done | bytes 144
  1399.7 53.8 %reduce-scatter.45.cloned.1.call-done = f32[128,1024]{1,0:T(8,128)} async-done(((f32[1024,1024]{1,0:T(8,128)}), f32[128,1024]{1,0:T(8,128)}) %reduce-scatter.45.cloned.1.call-update) | async-done | bytes 524304 | tf_op jit(solution)/shard_map/reduce_scatter | solution.py:245
  1453.5 55.7 %reduce-scatter.47.cloned.1.call-done = f32[1024,128]{1,0:T(8,128)} async-done(((f32[1024,1024]{1,0:T(8,128)}), f32[1024,128]{1,0:T(8,128)}) %reduce-scatter.47.cloned.1.call-update) | async-done | bytes 524304 | tf_op jit(solution)/shard_map/reduce_scatter | solution.py:247
  1509.1 39.8 %reduce-scatter.43.cloned.1.call-done = f32[256,128]{1,0:T(8,128)} async-done(((f32[256,1024]{1,0:T(8,128)}), f32[256,128]{1,0:T(8,128)}) %reduce-scatter.43.cloned.1.call-update) | async-done | bytes 131088 | tf_op jit(solution)/shard_map/reduce_scatter | solution.py:241
  1548.9 50.2 %reduce-scatter.41.cloned.1.call-done = f32[128,3,256]{2,0,1:T(8,128)} async-done(((f32[1024,3,256]{2,0,1:T(8,128)}), f32[128,3,256]{2,0,1:T(8,128)}) %reduce-scatter.41.cloned.1.call-update) | async-done | bytes 393232 | tf_op jit(solution)/shard_map/reduce_scatter | solution.py:239
  (274 shorter events, 170.8 us)
Async XLA Ops:
  7.2 31.6 %copy-start.1 = (bf16[2308,256]{1,0:T(8,128)(2,1)S(1)}, bf16[2308,256]{1,0:T(8,128)(2,1)}, u32[]{:S(2)}) copy-start(bf16[2308,256]{1,0:T(8,128)(2,1)} %param.19) | copy-start | bytes 3545092
  7.2 70.3 %all-gather.10.cloned.1.call-start = ((), (), s32[]{:S(2)}) async-start(), calls=%async_computation.17 | async-start | bytes 1769472 | tf_op jit(solution)/shard_map/all_gather | solution.py:103
  9.0 132.2 %all-gather.8.cloned.1.call-start = ((), (), s32[]{:S(2)}) async-start(), calls=%async_computation.16 | async-start | bytes 5918720 | tf_op jit(solution)/shard_map/all_gather | solution.py:137
  27.8 26.7 %copy-start.22 = (f32[256]{0:T(256)}, f32[256]{0:T(256)S(1)}, u32[]{:S(2)}) copy-start(f32[256]{0:T(256)S(1)} %mul.201) | copy-start | bytes 3076
  38.8 15.7 copy-start.15
  38.8 15.8 copy-start.33
  38.8 15.9 copy-start.21
  54.5 251.9 %reduce-scatter.33.cloned.1.call-start = ((), (), s32[]{:S(2)}) async-start(), calls=%async_computation.18 | async-start | bytes 5918720 | tf_op jit(solution)/shard_map/reduce_scatter | solution.py:152
  152.6 4.3 copy-start.24
  206.9 7.9 copy-start.5
  206.9 7.9 copy-start.11
  219.6 1.0 copy-start.13
  219.6 1.9 copy-start.37
  219.6 2.4 copy-start.36
  219.6 2.4 copy-start.35
  219.7 131.1 %all-gather.14.cloned.1.call-start = ((), (), s32[]{:S(2)}) async-start(), calls=%async_computation.20 | async-start | bytes 2359296 | tf_op jit(solution)/shard_map/all_gather | solution.py:109
  221.4 204.5 %all-gather.12.cloned.1.call-start = ((), (), s32[]{:S(2)}) async-start(), calls=%async_computation.19 | async-start | bytes 5918720 | tf_op jit(solution)/shard_map/all_gather | solution.py:160
  306.5 12.2 copy-start.2
  318.1 0.6 copy-start.17
  330.6 0.6 copy-start.20
  331.2 8.1 copy-start.10
  334.7 122.7 %all-gather.16.cloned.1.call-start = ((), (), s32[]{:S(2)}) async-start(), calls=%async_computation.21 | async-start | bytes 2359296 | tf_op jit(solution)/shard_map/all_gather | solution.py:111
  336.6 209.6 %all-gather.18.cloned.1.call-start = ((), (), s32[]{:S(2)}) async-start(), calls=%async_computation.23 | async-start | bytes 5918720 | tf_op jit(solution)/shard_map/all_gather | solution.py:180
  341.4 313.3 %reduce-scatter.37.cloned.1.call-start = ((), (), s32[]{:S(2)}) async-start(), calls=%async_computation.24 | async-start | bytes 5918720 | tf_op jit(solution)/shard_map/reduce_scatter | solution.py:189
  546.2 14.7 copy-start.31
  558.7 2.1 copy-start.38
  567.9 176.2 %reduce-scatter.35.cloned.1.call-start = ((), (), s32[]{:S(2)}) async-start(), calls=%async_computation.22 | async-start | bytes 5918720 | tf_op jit(solution)/shard_map/reduce_scatter | solution.py:171
  577.5 0.7 copy-start.34
  577.5 262.7 %all-gather.20.cloned.1.call-start = ((), (), s32[]{:S(2)}) async-start(), calls=%async_computation.25 | async-start | bytes 5918720 | tf_op jit(solution)/shard_map/all_gather | solution.py:202
  654.7 89.4 %copy-start.9 = (bf16[2308,256]{1,0:T(8,128)(2,1)S(1)}, bf16[2308,256]{1,0:T(8,128)(2,1)}, u32[]{:S(2)}) copy-start(bf16[2308,256]{1,0:T(8,128)(2,1)} %reduce-scatter.37.cloned.1.call-done) | copy-start | bytes 3545092
  750.2 1.5 copy-start.3
  751.7 88.6 %copy-start.12 = (bf16[256,1024]{1,0:T(8,128)(2,1)S(1)}, bf16[256,1024]{1,0:T(8,128)(2,1)}, u32[]{:S(2)}) copy-start(bf16[256,1024]{1,0:T(8,128)(2,1)} %all_gather.53) | copy-start | bytes 1572868
  752.8 352.2 %reduce-scatter.39.cloned.1.call-start = ((), (), s32[]{:S(2)}) async-start(), calls=%async_computation.26 | async-start | bytes 5918720 | tf_op jit(solution)/shard_map/reduce_scatter | solution.py:223
  852.6 2.7 copy-start
  886.4 2.7 copy-start
  920.2 2.7 copy-start
  954.0 2.8 copy-start
  1008.7 1.6 copy-start.8
  1008.7 2.0 copy-start.7
  1010.3 2.2 copy-start.32
  1010.8 1.8 copy-start.14
  1018.2 0.7 copy-start.26
  1018.2 1.8 copy-start.30
  1018.2 2.6 copy-start.28
  1018.2 3.5 copy-start.29
  1018.2 4.4 copy-start.27
  1018.2 5.3 copy-start.25
  1018.3 86.8 %copy-start.16 = (f32[2308]{0:T(1024)S(1)}, f32[2308]{0:T(1024)}, u32[]{:S(2)}) copy-start(f32[2308]{0:T(1024)} %copy-done.15) | copy-start | bytes 27700
  1018.3 86.8 %copy-start.19 = (f32[2308]{0:T(1024)S(1)}, f32[2308]{0:T(1024)}, u32[]{:S(2)}) copy-start(f32[2308]{0:T(1024)} %copy-done.18) | copy-start | bytes 27700
  1018.3 86.8 %copy-start.23 = (f32[256]{0:T(256)S(1)}, f32[256]{0:T(256)}, u32[]{:S(2)}) copy-start(f32[256]{0:T(256)} %copy-done.22) | copy-start | bytes 3076
  1018.3 127.5 %reduce-scatter.61.cloned.1.call-start = ((), (), s32[]{:S(2)}) async-start(), calls=%async_computation.37 | async-start | bytes 589824
  1019.9 160.0 %reduce-scatter.55.cloned.1.call-start = ((), (), s32[]{:S(2)}) async-start(), calls=%async_computation.34 | async-start | bytes 147456
  1020.8 195.3 %reduce-scatter.57.cloned.1.call-start = ((), (), s32[]{:S(2)}) async-start(), calls=%async_computation.35 | async-start | bytes 147456
  1021.7 231.0 %reduce-scatter.63.cloned.1.call-start = ((), (), s32[]{:S(2)}) async-start(), calls=%async_computation.38 | async-start | bytes 147456
  1022.6 266.3 %reduce-scatter.59.cloned.1.call-start = ((), (), s32[]{:S(2)}) async-start(), calls=%async_computation.36 | async-start | bytes 147456
  1023.4 302.0 %reduce-scatter.53.cloned.1.call-start = ((), (), s32[]{:S(2)}) async-start(), calls=%async_computation.33 | async-start | bytes 147456
  1024.9 336.7 %reduce-scatter.49.cloned.1.call-start = ((), (), s32[]{:S(2)}) async-start(), calls=%async_computation.31 | async-start | bytes 147456
  1109.2 289.2 %reduce-scatter.51.cloned.1.call-start = ((), (), s32[]{:S(2)}) async-start(), calls=%async_computation.32 | async-start | bytes 147456
  1110.0 343.4 %reduce-scatter.45.cloned.1.call-start = ((), (), s32[]{:S(2)}) async-start(), calls=%async_computation.29 | async-start | bytes 4718592 | tf_op jit(solution)/shard_map/reduce_scatter | solution.py:245
  1120.3 388.8 %reduce-scatter.47.cloned.1.call-start = ((), (), s32[]{:S(2)}) async-start(), calls=%async_computation.30 | async-start | bytes 4718592 | tf_op jit(solution)/shard_map/reduce_scatter | solution.py:247
  1130.6 1.3 copy-start.6
  1130.6 418.4 %reduce-scatter.43.cloned.1.call-start = ((), (), s32[]{:S(2)}) async-start(), calls=%async_computation.28 | async-start | bytes 1179648 | tf_op jit(solution)/shard_map/reduce_scatter | solution.py:241
  1136.9 462.2 %reduce-scatter.41.cloned.1.call-start = ((), (), s32[]{:S(2)}) async-start(), calls=%async_computation.27 | async-start | bytes 3538944 | tf_op jit(solution)/shard_map/reduce_scatter | solution.py:239
  1145.7 203.2 %copy-start.4 = (f32[2308,256]{1,0:T(8,128)S(1)}, f32[2308,256]{1,0:T(8,128)}, u32[]{:S(2)}) copy-start(f32[2308,256]{1,0:T(8,128)} %copy-done.3) | copy-start | bytes 7090180
  (1 other events, 0.6 us)
Sparse Core Ops, SparseCore 0:
  10.5 26.9 all-gather.9
  54.6 86.5 all-gather.7
  219.8 86.6 reduce-scatter.32
  308.8 28.3 all-gather.13
  339.2 86.6 all-gather.11
  428.2 29.1 all-gather.15
  459.5 86.6 all-gather.17
  568.1 86.6 reduce-scatter.36
  657.0 87.0 reduce-scatter.34
  753.0 87.2 all-gather.19
  1018.4 86.6 reduce-scatter.38
  1108.5 34.5 reduce-scatter.60
  1146.5 33.3 reduce-scatter.54
  1182.7 33.3 reduce-scatter.56
  1219.3 33.3 reduce-scatter.62
  1255.5 33.3 reduce-scatter.58
  1292.0 33.3 reduce-scatter.52
  1328.3 33.3 reduce-scatter.48
  1365.0 33.3 reduce-scatter.50
  1402.1 51.2 reduce-scatter.44
  1457.8 51.3 reduce-scatter.46
  1512.9 36.0 reduce-scatter.42
  1552.9 46.1 reduce-scatter.40
where the time goes:
time: 1620 us; the launch traced here: 1610 us
  waiting for transfers between devices  1050 us (65%)
  matrix products  249 us (15%)
  blocking collectives  119 us (7%)
  local copies, waits for them, and re-layouts  103 us (6%)
  other arithmetic  65.1 us (4%)
    unnamed x31, waiting for transfers between devices  217 us
    all_gather x1, waiting for transfers between devices, on_device(): lax.all_gather(grad_res.astype(jnp.bfloat16), 'tensor', axis=1, tiled=True)  88.8 us
    all_gather x1, waiting for transfers between devices, on_device(): lax.all_gather(grad_resid.astype(jnp.bfloat16), 'tensor', axis=1, tiled=T...  87.3 us
    reduce_scatter x1, waiting for transfers between devices, on_device(): lax.psum_scatter(jnp.dot(context_flat, weight_proj, preferred_element_typ...  83.8 us
    reduce_scatter x1, waiting for transfers between devices, on_device(): lax.psum_scatter(jnp.einsum('tcf,dcf->td', grad_mixed, weight_mix, prefer...  80.1 us
    reduce_scatter x1, waiting for transfers between devices, on_device(): lax.psum_scatter(jnp.einsum('tf,df->td', grad_pre_low, weight_up, preferr...  76 us
    all_gather x1, waiting for transfers between devices, on_device(): lax.all_gather((normed_two * gain_two_f + shift_two.astype(jnp.float32))....  75.1 us
    all_gather x1, waiting for transfers between devices, on_device(): lax.all_gather((normed_one * gain_one_f + shift_one.astype(jnp.float32))....  63.7 us
  transfers between devices with their start and end apart: 23, of which 20 were waited for; matrix products, arithmetic and copies ran while one was open for 8% of the time, Pallas kernels for 0%

commit v1 on v0

v1 whole, which is shorter than its diff:
```python
import functools
import jax
import jax.numpy as jnp
from jax import lax
from jax.experimental import pallas as pl
from jax.experimental.pallas import tpu as pltpu
from jax.sharding import PartitionSpec as P

D = 1024
HD = 64
SEQ = 577
ROWS = 592
STEP = 16
F32 = jnp.float32
BF16 = jnp.bfloat16
LAST = (((1,), (1,)), ((), ()))
VMEM_BYTES = 66_000_000


def mm(a, b):
    return jnp.dot(a, b, preferred_element_type=F32)


def mm_t(a, b):
    return lax.dot_general(a, b, LAST, preferred_element_type=F32)


def cols(i, n):
    return pl.ds(pl.multiple_of(i * n, n), n)


def row_stats(values):
    mean = jnp.sum(values, axis=1, keepdims=True) * (1.0 / D)
    centered = values - mean
    var = jnp.sum(centered * centered, axis=1, keepdims=True) * (1.0 / D)
    inv = lax.rsqrt(var + 1e-05)
    return centered * inv, inv


def wide(ref, rows):
    return jnp.concatenate([ref[t, rows, :].astype(F32) for t in range(4)], axis=1)


def vec(vectors, row):
    return jnp.concatenate([vectors[t, row : row + 1, :] for t in range(4)], axis=1)


def norm_in(x, vectors, nin):
    gain, shift = vec(vectors, 0), vec(vectors, 1)

    @pl.loop(0, ROWS // STEP)
    def _(i):
        rows = pl.ds(pl.multiple_of(i * STEP, STEP), STEP)
        xhat, _ = row_stats(wide(x, rows))
        nin[rows, :] = (xhat * gain + shift).astype(BF16)


def flip(src, dst, n):
    @pl.loop(0, n // 256)
    def _(i):
        dst[cols(i, 256), :] = src[:, cols(i, 256)].T


def project(nin, wqkv, vectors, t, q, k, v):
    here = pl.ds(t * 256, 256)
    q[:, here] = (mm(nin[...], wqkv[t, :, 0:256]) + vectors[t, 2:3, :]).astype(BF16)
    k[:, here] = mm(nin[...], wqkv[t, :, 256:512]).astype(BF16)
    v[:, here] = (mm(nin[...], wqkv[t, :, 512:768]) + vectors[t, 3:4, :]).astype(BF16)


def attend_pair(pair, q, k, v, ctx, probs, slot):
    here = cols(pair, 128)
    lane = lax.broadcasted_iota(jnp.int32, (ROWS, 128), 1)
    row = lax.broadcasted_iota(jnp.int32, (ROWS, 128), 0)
    queries = q[:, here].astype(F32) * (HD**-0.5)
    keys = k[:, here].astype(F32)
    values = v[:, here]
    blocked = jnp.where(row >= SEQ, -1e30, 0.0)
    parts = []
    for h in range(2):
        own = (lane < 64) if h == 0 else (lane >= 64)
        spare = 64 if h == 0 else 0
        qa = jnp.where(own, queries, jnp.where(lane == spare, 1.0, 0.0)).astype(BF16)
        ka = jnp.where(lane == spare, blocked, keys).astype(BF16)
        scores = mm_t(ka, qa)
        top = jnp.max(scores, axis=0, keepdims=True)
        e = jnp.exp(scores - top)
        total = jnp.sum(e, axis=0, keepdims=True)
        p = (e * (1.0 / total)).astype(BF16)
        probs[slot, h] = p
        parts.append(
            lax.dot_general(p, values, (((0,), (0,)), ((), ())), preferred_element_type=F32)
        )
    ctx[:, here] = jnp.where(lane < 64, parts[0], parts[1]).astype(BF16)


def out_block(i, ctx, wout, x, vectors, resid):
    w = jnp.concatenate([wout[2 * i], wout[2 * i + 1]], axis=1)
    resid[:, cols(i, 256)] = x[i].astype(F32) + mm(ctx[...], w) + vectors[i, 4:5, :]


def norm_mid(resid, vectors, nmid):
    gain, shift = vec(vectors, 5), vec(vectors, 6)

    @pl.loop(0, ROWS // STEP)
    def _(i):
        rows = pl.ds(pl.multiple_of(i * STEP, STEP), STEP)
        xhat, _ = row_stats(resid[rows, :])
        nmid[rows, :] = (xhat * gain + shift).astype(BF16)


def hidden_tile(t, j, nmid, w1, b1, act, act_t, slope):
    here = pl.ds(pl.multiple_of(t * 1024 + j * 256, 256), 256)
    bias = b1[t, :, cols(j, 256)]
    pre = mm(nmid[...], w1[t, :, cols(j, 256)]) + bias
    sig = 1.0 / (1.0 + jnp.exp(-1.702 * pre))
    a = pre * sig
    slope[:, here] = (sig + 1.702 * a * (1.0 - sig)).astype(BF16)
    low = a.astype(BF16)
    act[:, here] = low
    act_t[here, :] = low.T


def down_block(i, act, w2, resid, vectors, mask, out):
    w = jnp.concatenate([w2[2 * i], w2[2 * i + 1]], axis=1)
    total = resid[:, cols(i, 256)] + mm(act[...], w) + vectors[i, 7:8, :]
    out[i] = (total * mask[...]).astype(BF16)


def grad_norm_rows(values, gain, n):
    xhat, inv = row_stats(values)
    e = n * gain
    first = jnp.sum(e, axis=1, keepdims=True) * (1.0 / D)
    second = jnp.sum(e * xhat, axis=1, keepdims=True) * (1.0 / D)
    return inv * (e - first - xhat * second), n * xhat


def fold(a):
    return a[0:8] + a[8:16]


def attend_back_pair(pair, q, k, v, ctx, gctx, probs, slot, gmix, sums):
    here = cols(pair, 128)
    lane = lax.broadcasted_iota(jnp.int32, (ROWS, 128), 1)
    queries, keys, values = q[:, here], k[:, here], v[:, here].astype(F32)
    go = gctx[:, here]
    go_f = go.astype(F32)
    dots = go_f * ctx[:, here].astype(F32)
    dq, dk, dv = [], [], []
    for h in range(2):
        own = (lane < 64) if h == 0 else (lane >= 64)
        spare = 64 if h == 0 else 0
        delta = -jnp.sum(jnp.where(own, dots, 0.0), axis=1, keepdims=True)
        high = delta.astype(BF16).astype(F32)
        rest = delta - high
        ga = jnp.where(
            own, go_f, jnp.where(lane == spare, high, jnp.where(lane == spare + 1, rest, 0.0))
        ).astype(BF16)
        marks = jnp.where((lane == spare) | (lane == spare + 1), 1.0, 0.0)
        va = jnp.where(own, values, marks).astype(BF16)
        p = probs[slot, h]
        gs = (p.astype(F32) * mm_t(va, ga)).astype(BF16)
        dv.append(mm(p, go))
        dk.append(mm(gs, queries))
        dq.append(
            lax.dot_general(gs, keys, (((0,), (0,)), ((), ())), preferred_element_type=F32)
        )
    scale = HD**-0.5
    low = lane < 64
    gq = jnp.where(low, dq[0], dq[1]) * scale
    gk = jnp.where(low, dk[0], dk[1]) * scale
    gv = jnp.where(low, dv[0], dv[1])
    t, half = pair // 2, pair % 2
    at = [pl.ds(pl.multiple_of(c * 256 + half * 128, 128), 128) for c in range(3)]
    gmix[t, :, at[0]] = gq.astype(BF16)
    gmix[t, :, at[1]] = gk.astype(BF16)
    gmix[t, :, at[2]] = gv.astype(BF16)
    sums[2:3, here] = jnp.sum(gq, axis=0, keepdims=True)
    sums[3:4, here] = jnp.sum(gv, axis=0, keepdims=True)


ACT = jax.ShapeDtypeStruct((ROWS, D), BF16)
TURNED = jax.ShapeDtypeStruct((D, ROWS), BF16)
SAVED = dict(
    nin_t=TURNED,
    q=ACT,
    k=ACT,
    v=ACT,
    ctx=ACT,
    ctx_t=TURNED,
    nmid_t=TURNED,
    resid=jax.ShapeDtypeStruct((ROWS, D), F32),
    act_t=jax.ShapeDtypeStruct((4 * D, ROWS), BF16),
    slope=jax.ShapeDtypeStruct((ROWS, 4 * D), BF16),
)
PROBS = jax.ShapeDtypeStruct((8, 2, ROWS, ROWS), BF16)
IMAGE = jax.ShapeDtypeStruct((4, ROWS, 256), BF16)
ANY = pl.BlockSpec(memory_space=pl.ANY)
VM = pl.BlockSpec(memory_space=pltpu.VMEM)


def scratch(like):
    return pltpu.VMEM(like.shape, like.dtype)


def forward_kernel(x_h, wqkv_h, wout_h, w1_h, w2_h, vectors, b1, mask, *rest):
    n = len(SAVED)
    out_h, probs_h = rest[0], rest[1]
    saved_h = dict(zip(SAVED, rest[2 : 2 + n]))
    rest = rest[2 + n :]
    saved = dict(zip(SAVED, rest[:n]))
    x, wqkv, wout, w1, w2, nin, nmid, act, probs, out, in_sem, probs_sem, out_sem = rest[n:]
    loads = [
        pltpu.make_async_copy(a, b, in_sem.at[i])
        for i, (a, b) in enumerate(((x_h, x), (wqkv_h, wqkv), (wout_h, wout), (w1_h, w1), (w2_h, w2)))
    ]
    for c in loads:
        c.start()
    loads[0].wait()
    norm_in(x, vectors, nin)
    loads[1].wait()
    for t in range(4):
        project(nin, wqkv, vectors, t, saved["q"], saved["k"], saved["v"])
    flip(nin, saved["nin_t"], D)

    def put(pair, slot):
        return pltpu.make_async_copy(probs.at[slot], probs_h.at[pair], probs_sem.at[slot])

    @pl.loop(0, 8)
    def _(pair):
        slot = pair % 2

        @pl.when(pair >= 2)
        def _():
            put(pair - 2, slot).wait()

        attend_pair(pair, saved["q"], saved["k"], saved["v"], saved["ctx"], probs, slot)
        put(pair, slot).start()

    put(6, 0).wait()
    put(7, 1).wait()
    loads[2].wait()

    @pl.loop(0, 4)
    def _(i):
        out_block(i, saved["ctx"], wout, x, vectors, saved["resid"])

    norm_mid(saved["resid"], vectors, nmid)
    loads[3].wait()

    @pl.loop(0, 16)
    def _(i):
        hidden_tile(i // 4, i % 4, nmid, w1, b1, act, saved["act_t"], saved["slope"])

    flip(saved["ctx"], saved["ctx_t"], D)
    flip(nmid, saved["nmid_t"], D)
    loads[4].wait()

    @pl.loop(0, 4)
    def _(i):
        down_block(i, act, w2, saved["resid"], vectors, mask, out)

    stores = [pltpu.make_async_copy(out, out_h, out_sem.at[n])]
    stores += [pltpu.make_async_copy(saved[a], saved_h[a], out_sem.at[i]) for i, a in enumerate(SAVED)]
    for c in stores:
        c.start()
    for c in stores:
        c.wait()


def forward(x, wqkv, wout, w1, w2, vectors, b1, mask):
    n = len(SAVED)
    outs = pl.pallas_call(
        forward_kernel,
        out_shape=[IMAGE, PROBS, *SAVED.values()],
        in_specs=[ANY] * 5 + [VM, VM, VM],
        out_specs=[ANY] * (2 + n),
        scratch_shapes=[scratch(a) for a in SAVED.values()]
        + [scratch(a) for a in (x, wqkv, wout, w1, w2)]
        + [
            scratch(ACT),
            scratch(ACT),
            pltpu.VMEM((ROWS, 4 * D), BF16),
            pltpu.VMEM((2, 2, ROWS, ROWS), BF16),
            scratch(IMAGE),
            pltpu.SemaphoreType.DMA((5,)),
            pltpu.SemaphoreType.DMA((2,)),
            pltpu.SemaphoreType.DMA((n + 1,)),
        ],
        compiler_params=pltpu.CompilerParams(vmem_limit_bytes=VMEM_BYTES),
        name="forward",
    )(x, wqkv, wout, w1, w2, vectors, b1, mask)
    return outs[0], outs[1], dict(zip(SAVED, outs[2:]))


GRADS = dict(
    wqkv=jax.ShapeDtypeStruct((4, 1024, 768), BF16),
    wout=jax.ShapeDtypeStruct((8, 1024, 128), BF16),
    w1=jax.ShapeDtypeStruct((4, 1024, 1024), BF16),
    w2=jax.ShapeDtypeStruct((8, 4096, 128), BF16),
)


def send_tile(stage, sem, i, value, targets):
    slot = lax.rem(i, 2)

    def copies(s):
        return [
            pltpu.make_async_copy(
                stage.at[s] if w == 256 else stage.at[s, :, pl.ds(c, w)], ref, sem.at[s]
            )
            for ref, c, w in targets
        ]

    @pl.when(i >= 2)
    def _():
        pltpu.make_async_copy(stage.at[slot], stage.at[slot], sem.at[slot]).wait()

    stage[slot] = value
    for c in copies(slot):
        c.start()


def drain(stage, sem):
    for slot in range(2):
        pltpu.make_async_copy(stage.at[slot], stage.at[slot], sem.at[slot]).wait()


def backward_kernel(x_h, ct_h, wqkv_h, wout_h, w1_h, w2_h, vectors, mask, probs_h, *rest):
    n = len(SAVED)
    saved_h = dict(zip(SAVED, rest[:n]))
    gtok_h, sums_o = rest[n], rest[n + 1]
    g_h = dict(zip(GRADS, rest[n + 2 : n + 6]))
    rest = rest[n + 6 :]
    saved = dict(zip(SAVED, rest[:n]))
    (x, wqkv, wout, w1, w2, b1, gmlp, gattn, gctx, gn, gmix, probs, sums, part, stage,
     in_sem, probs_sem, tile_sem, saved_sem) = rest[n:]
    gtok = x
    names = dict(ct=(ct_h, gtok), x=(x_h, x), w2=(w2_h, w2), w1=(w1_h, w1), wout=(wout_h, wout), wqkv=(wqkv_h, wqkv))
    load = {a: pltpu.make_async_copy(*names[a], in_sem.at[i]) for i, a in enumerate(names)}
    load_saved = {a: pltpu.make_async_copy(saved_h[a], saved[a], saved_sem.at[i]) for i, a in enumerate(SAVED)}
    load["ct"].start()
    for a in ("act_t", "slope"):
        load_saved[a].start()
    for a in ("w2", "w1", "wout", "wqkv"):
        load[a].start()
    for a in SAVED:
        if a not in ("act_t", "slope"):
            load_saved[a].start()
    part[...] = jnp.zeros_like(part)
    sums[...] = jnp.zeros_like(sums)
    load["ct"].wait()

    @pl.loop(0, ROWS // STEP)
    def _(i):
        rows = pl.ds(pl.multiple_of(i * STEP, STEP), STEP)
        g = jnp.concatenate([x[t, rows, :].astype(F32) * mask[...] for t in range(4)], axis=1)
        gmlp[rows, :] = g.astype(BF16)
        part[0] += fold(g)

    load["x"].start()
    load_saved["act_t"].wait()

    @pl.loop(0, 16)
    def _(i):
        t, c = i // 4, i % 4
        r = mm(saved["act_t"][cols(t, 1024), :], gmlp[:, cols(c, 256)]).astype(BF16)
        send_tile(stage, tile_sem, i, r, [
            (g_h["w2"].at[2 * c + e, cols(t, 1024), :], e * 128, 128) for e in range(2)])

    load_saved["slope"].wait()
    load["w2"].wait()
    slope = saved["slope"]

    @pl.loop(0, 16)
    def _(i):
        w = jnp.concatenate([w2[d, cols(i, 256), :] for d in range(8)], axis=1)
        gpre = mm_t(gmlp[...], w) * slope[:, cols(i, 256)].astype(F32)
        slope[:, cols(i, 256)] = gpre.astype(BF16)
        b1[i // 4, :, cols(i % 4, 256)] = jnp.sum(gpre, axis=0, keepdims=True)

    load_saved["nmid_t"].wait()

    @pl.loop(0, 16)
    def _(i):
        r = mm(saved["nmid_t"][...], slope[:, cols(i, 256)]).astype(BF16)
        send_tile(stage, tile_sem, i + 16, r, [(g_h["w1"].at[i // 4, :, cols(i % 4, 256)], 0, 256)])

    load["w1"].wait()

    @pl.loop(0, 4)
    def _(i):
        total = mm_t(slope[:, 0:1024], w1[0, cols(i, 256), :])
        for t in range(1, 4):
            total += mm_t(slope[:, t * 1024 : t * 1024 + 1024], w1[t, cols(i, 256), :])
        gn[:, cols(i, 256)] = total

    load_saved["resid"].wait()
    gain2 = vec(vectors, 5)

    @pl.loop(0, ROWS // STEP)
    def _(i):
        rows = pl.ds(pl.multiple_of(i * STEP, STEP), STEP)
        normed = gn[rows, :]
        g, scaled = grad_norm_rows(saved["resid"][rows, :], gain2, normed)
        g = g + gmlp[rows, :].astype(F32)
        part[1] += fold(normed)
        part[2] += fold(scaled)
        part[3] += fold(g)
        gn[rows, :] = g
        gattn[rows, :] = g.astype(BF16)

    load["wout"].wait()
    load_saved["ctx_t"].wait()

    @pl.loop(0, 4)
    def _(i):
        w = jnp.concatenate([wout[d, cols(i, 256), :] for d in range(8)], axis=1)
        gctx[:, cols(i, 256)] = mm_t(gattn[...], w).astype(BF16)
        r = mm(saved["ctx_t"][...], gattn[:, cols(i, 256)]).astype(BF16)
        send_tile(stage, tile_sem, i + 32, r, [(g_h["wout"].at[2 * i + e], e * 128, 128) for e in range(2)])

    for a in ("q", "k", "v", "ctx"):
        load_saved[a].wait()

    def get(pair, slot):
        return pltpu.make_async_copy(probs_h.at[pair], probs.at[slot], probs_sem.at[slot])

    get(0, 0).start()

    @pl.loop(0, 8)
    def _(pair):
        slot = pair % 2

        @pl.when(pair < 7)
        def _():
            get(pair + 1, 1 - slot).start()

        get(pair, slot).wait()
        attend_back_pair(pair, saved["q"], saved["k"], saved["v"], saved["ctx"], gctx, probs, slot, gmix, sums)

    load_saved["nin_t"].wait()

    @pl.loop(0, 12)
    def _(i):
        t, c = i // 3, i % 3
        r = mm(saved["nin_t"][...], gmix[t, :, cols(c, 256)]).astype(BF16)
        send_tile(stage, tile_sem, i + 36, r, [(g_h["wqkv"].at[t, :, cols(c, 256)], 0, 256)])

    load["wqkv"].wait()
    resid = saved["resid"]

    @pl.loop(0, 4)
    def _(i):
        total = mm_t(gmix[0], wqkv[0, cols(i, 256), :])
        for t in range(1, 4):
            total += mm_t(gmix[t], wqkv[t, cols(i, 256), :])
        resid[:, cols(i, 256)] = total

    load["x"].wait()
    gain1 = vec(vectors, 0)

    @pl.loop(0, ROWS // STEP)
    def _(i):
        rows = pl.ds(pl.multiple_of(i * STEP, STEP), STEP)
        normed = resid[rows, :]
        g, scaled = grad_norm_rows(wide(x, rows), gain1, normed)
        g = g + gn[rows, :]
        part[4] += fold(normed)
        part[5] += fold(scaled)
        for t in range(4):
            gtok[t, rows, :] = g[:, t * 256 : t * 256 + 256].astype(BF16)

    for row, i in ((7, 0), (6, 1), (5, 2), (4, 3), (1, 4), (0, 5)):
        sums[row : row + 1, :] = jnp.sum(part[i], axis=0, keepdims=True)
    sums_o[0:8, :] = sums[...]
    for t in range(4):
        sums_o[8 + t : 9 + t, :] = b1[t]
    done = pltpu.make_async_copy(gtok, gtok_h, in_sem.at[0])
    done.start()
    done.wait()
    drain(stage, tile_sem)


def backward(x, ct, wqkv, wout, w1, w2, vectors, mask, probs, saved):
    n = len(SAVED)
    outs = pl.pallas_call(
        backward_kernel,
        out_shape=[IMAGE, jax.ShapeDtypeStruct((12, D), F32), *GRADS.values()],
        in_specs=[ANY] * 6 + [VM, VM, ANY] + [ANY] * n,
        out_specs=[ANY, VM] + [ANY] * 4,
        scratch_shapes=[scratch(a) for a in SAVED.values()]
        + [scratch(a) for a in (x, wqkv, wout, w1, w2)]
        + [
            pltpu.VMEM((4, 1, 1024), F32),
            scratch(ACT),
            scratch(ACT),
            scratch(ACT),
            pltpu.VMEM((ROWS, D), F32),
            pltpu.VMEM((4, ROWS, 768), BF16),
            pltpu.VMEM((2, 2, ROWS, ROWS), BF16),
            pltpu.VMEM((8, D), F32),
            pltpu.VMEM((6, 8, D), F32),
            pltpu.VMEM((2, 1024, 256), BF16),
            pltpu.SemaphoreType.DMA((6,)),
            pltpu.SemaphoreType.DMA((2,)),
            pltpu.SemaphoreType.DMA((2,)),
            pltpu.SemaphoreType.DMA((n,)),
        ],
        compiler_params=pltpu.CompilerParams(vmem_limit_bytes=VMEM_BYTES),
        name="backward",
    )(x, ct, wqkv, wout, w1, w2, vectors, mask, probs, *[saved[a] for a in SAVED])
    return outs[0], outs[1], dict(zip(GRADS, outs[2:]))


def gather_plain(w_qkv, w_out, w_fc1, w_fc2):
    def all_of(shard, axis):
        return lax.all_gather(
            lax.all_gather(shard.astype(BF16), "dp", axis=axis, tiled=True), "tensor", axis=0
        )

    wqkv = all_of(w_qkv.reshape(-1, 768), 0)
    wout = all_of(w_out, 1).reshape(D, 8, 128).transpose(1, 0, 2)
    w1 = all_of(w_fc1, 0)
    w2 = all_of(w_fc2, 1).reshape(4 * D, 8, 128).transpose(1, 0, 2)
    return wqkv, wout, w1, w2


def scatter_plain(grads):
    def mine(grad, axis):
        part = lax.psum_scatter(grad, "tensor", scatter_dimension=0, tiled=True)
        return lax.psum_scatter(part, "dp", scatter_dimension=axis, tiled=True).astype(F32)

    g_qkv = mine(grads["wqkv"], 1)[0]
    g_out = mine(grads["wout"].transpose(1, 0, 2).reshape(D, D), 1)
    g_fc1 = mine(grads["w1"], 1)[0]
    g_fc2 = mine(grads["w2"].transpose(1, 0, 2).reshape(4 * D, D), 1)
    return g_qkv, g_out, g_fc1, g_fc2


def on_device(
    tokens_in,
    cotangent,
    slot_mask,
    norm1_gain,
    norm1_bias,
    w_qkv,
    b_qkv,
    w_out,
    b_out,
    norm2_gain,
    norm2_bias,
    w_fc1,
    b_fc1,
    w_fc2,
    b_fc2,
):
    def images(rows):
        return jnp.pad(rows.reshape(4, SEQ, 256), ((0, 0), (0, ROWS - SEQ), (0, 0)))

    def exchange(pieces):
        return lax.all_to_all(pieces, "tensor", split_axis=0, concat_axis=0, tiled=True)

    mask = jnp.broadcast_to(
        lax.dynamic_index_in_dim(slot_mask, lax.axis_index("tensor"), 0).astype(F32), (1, 256)
    )
    small = jnp.concatenate(
        (norm1_gain, norm1_bias, b_qkv[0], b_qkv[1], b_out, norm2_gain, norm2_bias, b_fc2)
    ).astype(BF16)
    vectors = lax.all_gather(
        lax.all_gather(small, "dp", axis=1, tiled=True), "tensor", axis=0
    ).astype(F32)
    hidden_bias = lax.all_gather(
        lax.all_gather(b_fc1.astype(BF16), "dp", axis=1, tiled=True), "tensor", axis=0
    ).astype(F32)
    x = exchange(images(tokens_in))
    ct = exchange(images(cotangent))
    weights = gather_plain(w_qkv, w_out, w_fc1, w_fc2)
    out, probs, saved = forward(x, *weights, vectors, hidden_bias, mask)
    gtok, sums, grads = backward(x, ct, *weights, vectors, mask, probs, saved)
    g_qkv, g_out, g_fc1, g_fc2 = scatter_plain(grads)

    def total(part, axis):
        part = lax.psum_scatter(part, "tensor", scatter_dimension=0, tiled=True)
        return lax.psum_scatter(part, "dp", scatter_dimension=axis, tiled=True)

    g_small = total(sums[0:8].reshape(8, 4, 256).transpose(1, 0, 2), 2)[0]
    g_hidden = total(sums[8:12], 1)

    def rows(pieces):
        return pieces[:, :SEQ].reshape(4 * SEQ, 256)

    return (
        rows(exchange(out)),
        rows(exchange(gtok)),
        g_small[0:1],
        g_small[1:2],
        g_qkv.reshape(w_qkv.shape),
        g_small[2:4][:, None],
        g_out,
        g_small[4:5],
        g_small[5:6],
        g_small[6:7],
        g_fc1,
        g_hidden,
        g_fc2,
        g_small[7:8],
    )


def solution(mesh):
    both, turned = P("dp", "tensor"), P("tensor", "dp")
    mixed, pair = P("dp", None, "tensor"), P(None, "tensor", "dp")
    params = (turned, turned, mixed, pair, turned, turned, turned, turned, both, turned, turned, turned)
    return jax.shard_map(
        on_device,
        mesh=mesh,
        in_specs=(both, both, P("dp"), *params),
        out_specs=(both, both, *params),
        check_vma=False,
    )
```

time: 1620 us -> 1500 us (0.926)
  matrix products: 249 us -> 0 us
  Pallas kernels: 0 us -> 162 us
  waiting for transfers between devices: 1050 us -> 1120 us
  other arithmetic: 65.1 us -> 3.8 us
  local copies, waits for them, and re-layouts: 103 us -> 74.1 us
  starting transfers between devices: 1.38 us -> 23.5 us
  blocking collectives: 119 us -> 98.6 us
    dot_general x40 -> x0, matrix products: 249 us -> none  [the longest x4 47.3 us: attend_back(): jnp.einsum('hqk,khe->qhe', scores_low, key_rows, preferred_element_type=j...]
    pallas_call x0 -> x2, Pallas kernels: none -> 162 us  [the longest x1 98.6 us: backward(): pl.pallas_call(backward_kernel, out_shape=[IMAGE, jax.ShapeDtypeStruct((1...]
    unnamed x31 -> x20, waiting for transfers between devices: 217 us -> 70.4 us
    reduce_scatter x8 -> x9, waiting for transfers between devices: 502 us -> 599 us  [the longest x4 447 us: mine(): part = lax.psum_scatter(grad, 'tensor', scatter_dimension=0, tiled=True)]
    psum x6 -> x0, blocking collectives: 78.1 us -> none  [the longest x4 42 us: row_total(): return lax.psum(partial_sum, 'tensor')]
    all_gather x7, waiting for transfers between devices: 334 us -> 403 us  [the longest x4 329 us: all_of(): lax.all_gather(lax.all_gather(shard.astype(BF16), 'dp', axis=axis, tiled=...]
    all_to_all x0 -> x4, waiting for transfers between devices: none -> 51.1 us  [exchange(): lax.all_to_all(pieces, 'tensor', split_axis=0, concat_axis=0, tiled=True)]
    all_gather x3 -> x5, blocking collectives: 29.5 us -> 80.4 us  [the longest x1 35.9 us: on_device(): lax.all_gather(lax.all_gather(b_fc1.astype(BF16), 'dp', axis=1, tiled=Tru...]
  transfers between devices with their start and end apart: 23 -> 22, of which waited for: 20 -> 17; matrix products, arithmetic and copies ran while one was open for 8% -> 5% of each run, Pallas kernels for 0% -> 4%
where the time goes in v1:
time: 1500 us
  waiting for transfers between devices  1120 us (75%)
  Pallas kernels  162 us (11%)
  blocking collectives  98.6 us (7%)
  local copies, waits for them, and re-layouts  74.1 us (5%)
  starting transfers between devices  23.5 us (2%)
  between operations  15.3 us (1%)
    reduce_scatter x4, waiting for transfers between devices, mine(): part = lax.psum_scatter(grad, 'tensor', scatter_dimension=0, tiled=True)  447 us
    all_gather x4, waiting for transfers between devices, all_of(): lax.all_gather(lax.all_gather(shard.astype(BF16), 'dp', axis=axis, tiled=...  329 us
    reduce_scatter x4, waiting for transfers between devices, mine(): lax.psum_scatter(part, 'dp', scatter_dimension=axis, tiled=True).astype(F32)  152 us
    pallas_call x1, Pallas kernels, backward(): pl.pallas_call(backward_kernel, out_shape=[IMAGE, jax.ShapeDtypeStruct((1...  98.6 us
    all_gather x3, waiting for transfers between devices, all_of(): lax.all_gather(shard.astype(BF16), 'dp', axis=axis, tiled=True)  74 us
    unnamed x20, waiting for transfers between devices  70.4 us
    pallas_call x1, Pallas kernels, forward(): pl.pallas_call(forward_kernel, out_shape=[IMAGE, PROBS, *SAVED.values()],...  63.8 us
    all_to_all x4, waiting for transfers between devices, exchange(): lax.all_to_all(pieces, 'tensor', split_axis=0, concat_axis=0, tiled=True)  51.1 us
  transfers between devices with their start and end apart: 22, of which 17 were waited for; matrix products, arithmetic and copies ran while one was open for 5% of the time, Pallas kernels for 4%

profile of v1, /device:TPU:10, one launch (start us, length us, event | category | flops | bytes accessed | tf_op | source)
XLA Modules:
  0.0 1500.8 jit_solution(11019710077170264003)
XLA Ops:
  7.2 1.9 copy.45
  9.2 1.9 copy.49
  11.2 0.7 convert_element_type.44
  12.1 12.1 all_gather.57
  24.3 13.3 all-gather.16.cloned.1.call-done
  37.7 30.3 %all-gather.20.cloned.1.call-done = bf16[1024,1024]{0,1:T(8,128)(2,1)} async-done(((bf16[1024,128]{0,1:T(8,128)(2,1)}), bf16[1024,1024]{0,1:T(8,128)(2,1)}) %all-gather.20.cloned.1.call-update) | async-done | bytes 2097168 | tf_op jit(solution)/shard_map/all_gather | solution.py:519
  68.1 30.3 %all-gather.18.cloned.1.call-done = bf16[1024,1024]{1,0:T(8,128)(2,1)} async-done(((bf16[128,1024]{1,0:T(8,128)(2,1)}), bf16[1024,1024]{1,0:T(8,128)(2,1)}) %all-gather.18.cloned.1.call-update) | async-done | bytes 2097168 | tf_op jit(solution)/shard_map/all_gather | solution.py:519
  98.7 1.1 pad.7
  99.8 5.1 all-to-all-start
  105.0 1.6 reshape.72
  106.6 1.1 pad.8
  107.8 51.1 %all-to-all-done.x_h = bf16[4,592,256]{2,1,0:T(8,128)(2,1)S(1)} async-done(((bf16[4,592,256]{2,1,0:T(8,128)(2,1)}), bf16[4,592,256]{2,1,0:T(8,128)(2,1)S(1)}, u32[]{:S(2)}, u32[]{:S(2)}) %all-to-all-start) | async-done | bytes 1212448 | tf_op jit(solution)/shard_map/all_to_all | solution.py:562
  158.9 8.9 all-to-all-start.2
  168.0 7.9 all-gather.6
  176.0 8.7 all_gather.69
  184.8 35.9 %all-gather.7 = bf16[4,1,1024]{2,1,0:T(2,128)(2,1)S(1)} all-gather(bf16[1,1,1024]{2,1,0:T(2,128)(2,1)S(1)} %bitcast.74), channel_id=7, replica_groups=mesh['dp'=8,'tensor'=4] {'tensor'}, dimensions={0}, use_global_device_ids=true | all-gather | bytes 10240 | tf_op jit(solution)/shard_map/all_gather | solution.py:573
  220.6 0.6 convert_element_type.55.b1
  222.5 15.8 %all-gather.4 = bf16[32,256]{1,0:T(8,128)(2,1)S(1)} all-gather(bf16[8,256]{1,0:T(8,128)(2,1)S(1)} %bitcast.73), channel_id=6, replica_groups=mesh['dp'=8,'tensor'=4] {'tensor'}, dimensions={0}, use_global_device_ids=true | all-gather | bytes 20480 | tf_op jit(solution)/shard_map/all_gather | solution.py:570
  238.3 0.6 bitcast_convert_fusion.1.vectors
  238.9 3.9 copy.48
  242.8 50.2 %all-gather.22.cloned.1.call-done = bf16[4096,768]{0,1:T(8,128)(2,1)} async-done(((bf16[1024,768]{0,1:T(8,128)(2,1)}), bf16[4096,768]{0,1:T(8,128)(2,1)}) %all-gather.22.cloned.1.call-update) | async-done | bytes 6291472 | tf_op jit(solution)/shard_map/all_gather | solution.py:518
  293.1 8.6 copy.46
  301.7 140.9 %all-gather.28.cloned.1.call-done = bf16[4096,1024]{0,1:T(8,128)(2,1)} async-done(((bf16[1024,1024]{0,1:T(8,128)(2,1)}), bf16[4096,1024]{0,1:T(8,128)(2,1)}) %all-gather.28.cloned.1.call-update) | async-done | bytes 8388624 | tf_op jit(solution)/shard_map/all_gather | solution.py:518
  442.7 12.0 copy.50
  454.7 137.4 %all-gather.26.cloned.1.call-done = bf16[4096,1024]{1,0:T(8,128)(2,1)} async-done(((bf16[1024,1024]{1,0:T(8,128)(2,1)}), bf16[4096,1024]{1,0:T(8,128)(2,1)}) %all-gather.26.cloned.1.call-update) | async-done | bytes 8388624 | tf_op jit(solution)/shard_map/all_gather | solution.py:518
  592.7 63.8 %forward.1 = (bf16[4,592,256]{2,1,0:T(8,128)(2,1)}, bf16[8,2,592,592]{3,2,1,0:T(8,128)(2,1)}, bf16[1024,592]{1,0:T(8,128)(2,1)}, bf16[592,1024]{1,0:T(8,128)(2,1...) custom-call(bf16[4,592,256]{2,1,0:T(8,128)(2,1)} %copy-done, ...), custom_call_target="tpu_custom_call" | custom-call | tf_op jit(solution)/shard_map/forward/pallas_call | solution.py:273
  656.5 98.6 %backward.1 = (bf16[4,592,256]{2,1,0:T(8,128)(2,1)}, f32[12,1024]{1,0:T(8,128)}, bf16[4,1024,768]{2,1,0:T(8,128)(2,1)}, bf16[8,1024,128]{2,1,0:T(8,128)(2,1)}, b...) custom-call(bf16[4,592,256]{2,1,0:T(8,128)(2,1)} %copy-done, bf16[4,592,256]{2,1,0:T(8,128)(2,1)} %all-to-all-done.2.ct_h, ...), custom_call_target="tpu_custom_call" | custom-call | tf_op jit(solution)/shard_map/backward/pallas_call | solution.py:487
  755.1 1.4 slice.64
  756.6 3.9 copy.53
  761.2 0.7 reduce-scatter.26.cloned.1.call-update
  761.9 11.7 copy.54
  774.9 0.8 slice.76
  775.7 18.1 %all-reduce.2 = f32[4,1024]{1,0:T(4,128)S(1)} all-reduce(f32[4,1024]{1,0:T(4,128)S(1)} %slice.76), channel_id=16, replica_groups=mesh['dp'=8,'tensor'=4] {'tensor'}, use_global_device_ids=true, to_apply=%region_8.9.clone | all-reduce | flops 4096 | bytes 32768
  793.8 0.7 constant_dynamic-slice_fusion
  794.4 1.0 copy.61
  795.6 1.5 copy.59
  797.1 21.9 %reduce-scatter.22.cloned.1.call-done = bf16[256,1024]{0,1:T(8,128)(2,1)} async-done(((bf16[1024,1024]{0,1:T(8,128)(2,1)}), bf16[256,1024]{0,1:T(8,128)(2,1)}) %reduce-scatter.22.cloned.1.call-update) | async-done | bytes 524304 | tf_op jit(solution)/shard_map/reduce_scatter | solution.py:531
  819.1 114.5 %reduce-scatter.18.cloned.1.call-done = bf16[1,1024,768]{2,1,0:T(8,128)(2,1)} async-done(((bf16[4,1024,768]{2,1,0:T(8,128)(2,1)}), bf16[1,1024,768]{2,1,0:T(8,128)(2,1)}) %reduce-scatter.18.cloned.1.call-update) | async-done | bytes 1572880 | tf_op jit(solution)/shard_map/reduce_scatter | solution.py:531
  933.6 147.0 %reduce-scatter.26.cloned.1.call-done = bf16[1,1024,1024]{2,1,0:T(8,128)(2,1)} async-done(((bf16[4,1024,1024]{2,1,0:T(8,128)(2,1)}), bf16[1,1024,1024]{2,1,0:T(8,128)(2,1)}) %reduce-scatter.26.cloned.1.call-update) | async-done | bytes 2097168 | tf_op jit(solution)/shard_map/reduce_scatter | solution.py:531
  1080.7 5.3 all-to-all-start.1
  1085.9 164.0 %reduce-scatter.30.cloned.1.call-done = bf16[1024,1024]{0,1:T(8,128)(2,1)} async-done(((bf16[4096,1024]{0,1:T(8,128)(2,1)}), bf16[1024,1024]{0,1:T(8,128)(2,1)}) %reduce-scatter.30.cloned.1.call-update) | async-done | bytes 2097168 | tf_op jit(solution)/shard_map/reduce_scatter | solution.py:531
  1250.0 3.5 all-to-all-start.3
  1253.5 33.2 %reduce-scatter.36.cloned.1.call-done = f32[128,1]{1,0:T(8,128)} async-done(((f32[1024,1]{1,0:T(8,128)}), f32[128,1]{1,0:T(8,128)}) %reduce-scatter.36.cloned.1.call-update) | async-done | bytes 528
  1286.8 1.4 copy.62
  1288.2 35.7 %reduce-scatter.34.cloned.1.call-done = f32[32,8]{1,0:T(8,128)} async-done(((f32[256,8]{1,0:T(8,128)}), f32[32,8]{1,0:T(8,128)}) %reduce-scatter.34.cloned.1.call-update) | async-done | bytes 1040
  1323.9 0.8 slice.85
  1324.7 1.2 fusion
  1325.9 0.6 copy.63
  1326.5 0.6 copy.64
  1327.1 0.6 copy.65
  1327.7 0.6 copy.66
  1328.3 0.6 copy.67
  1330.1 1.1 slice.81
  1331.2 2.6 reshape.71
  1333.9 1.3 reshape.73
  1335.2 25.8 %reduce-scatter.24.cloned.1.call-done = bf16[256,128]{0,1:T(8,128)(2,1)} async-done(((bf16[256,1024]{0,1:T(8,128)(2,1)}), bf16[256,128]{0,1:T(8,128)(2,1)}) %reduce-scatter.24.cloned.1.call-update) | async-done | bytes 65552 | tf_op jit(solution)/shard_map/reduce_scatter | solution.py:532
  1361.0 1.6 copy.57
  1362.6 40.4 %reduce-scatter.20.cloned.1.call-done = bf16[1,128,768]{2,1,0:T(8,128)(2,1)} async-done(((bf16[1,1024,768]{2,1,0:T(8,128)(2,1)}), bf16[1,128,768]{2,1,0:T(8,128)(2,1)}) %reduce-scatter.20.cloned.1.call-update) | async-done | bytes 196624 | tf_op jit(solution)/shard_map/reduce_scatter | solution.py:532
  1403.0 1.1 copy.52
  1404.0 0.9 copy.55
  1405.0 42.7 %reduce-scatter.28.cloned.1.call-done = bf16[1,128,1024]{2,1,0:T(8,128)(2,1)} async-done(((bf16[1,1024,1024]{2,1,0:T(8,128)(2,1)}), bf16[1,128,1024]{2,1,0:T(8,128)(2,1)}) %reduce-scatter.28.cloned.1.call-update) | async-done | bytes 262160 | tf_op jit(solution)/shard_map/reduce_scatter | solution.py:532
  1447.7 1.8 bitcast_convert_fusion
  1449.5 42.6 %reduce-scatter.32.cloned.1.call-done = bf16[1024,128]{0,1:T(8,128)(2,1)} async-done(((bf16[1024,1024]{0,1:T(8,128)(2,1)}), bf16[1024,128]{0,1:T(8,128)(2,1)}) %reduce-scatter.32.cloned.1.call-update) | async-done | bytes 262160 | tf_op jit(solution)/shard_map/reduce_scatter | solution.py:532
  1492.1 1.9 copy.58
  (88 shorter events, 5.7 us)
Async XLA Ops:
  7.2 4.0 copy-start.2
  7.2 4.8 copy-start.3
  7.2 30.4 %all-gather.16.cloned.1.call-start = ((), (), s32[]{:S(2)}) async-start(), calls=%async_computation.15 | async-start | bytes 1769472 | tf_op jit(solution)/shard_map/all_gather | solution.py:519
  9.1 58.8 %all-gather.20.cloned.1.call-start = ((), (), s32[]{:S(2)}) async-start(), calls=%async_computation.17 | async-start | bytes 2359296 | tf_op jit(solution)/shard_map/all_gather | solution.py:519
  11.1 87.3 %all-gather.18.cloned.1.call-start = ((), (), s32[]{:S(2)}) async-start(), calls=%async_computation.16 | async-start | bytes 2359296 | tf_op jit(solution)/shard_map/all_gather | solution.py:519
  11.9 227.0 %all-gather.24.cloned.1.call-start = ((), (), s32[]{:S(2)}) async-start(), calls=%async_computation.28 | async-start | bytes 2621440 | tf_op jit(solution)/shard_map/all_gather | solution.py:518
  24.2 268.9 %all-gather.22.cloned.1.call-start = ((), (), s32[]{:S(2)}) async-start(), calls=%async_computation.27 | async-start | bytes 7864320 | tf_op jit(solution)/shard_map/all_gather | solution.py:518
  37.6 405.1 %all-gather.28.cloned.1.call-start = ((), (), s32[]{:S(2)}) async-start(), calls=%async_computation.30 | async-start | bytes 10485760 | tf_op jit(solution)/shard_map/all_gather | solution.py:518
  68.0 30.4 %copy-start.1 = (bf16[2308,256]{1,0:T(8,128)(2,1)S(1)}, bf16[2308,256]{1,0:T(8,128)(2,1)}, u32[]{:S(2)}) copy-start(bf16[2308,256]{1,0:T(8,128)(2,1)} %param.15) | copy-start | bytes 3545092
  68.0 524.1 %all-gather.26.cloned.1.call-start = ((), (), s32[]{:S(2)}) async-start(), calls=%async_computation.29 | async-start | bytes 10485760 | tf_op jit(solution)/shard_map/all_gather | solution.py:518
  99.8 59.0 %all-to-all-start = ((bf16[4,592,256]{2,1,0:T(8,128)(2,1)}), bf16[4,592,256]{2,1,0:T(8,128)(2,1)S(1)}, u32[]{:S(2)}, u32[]{:S(2)}) async-start(bf16[4,592,256]{2,1,0:T(8,128)(2,1)} %pad.7), calls=%async_computation | async-start | bytes 2424832 | tf_op jit(solution)/shard_map/all_to_all | solution.py:562
  107.7 60.1 %copy-start.5 = (f32[1,32]{1,0:T(1,128)S(1)}, f32[1,32]{1,0:T(1,128)}, u32[]{:S(2)}) copy-start(f32[1,32]{1,0:T(1,128)} %param.18) | copy-start | bytes 388
  107.7 60.1 %copy-start.6 = (f32[1,32]{1,0:T(1,128)S(1)}, f32[1,32]{1,0:T(1,128)}, u32[]{:S(2)}) copy-start(f32[1,32]{1,0:T(1,128)} %param.19) | copy-start | bytes 388
  107.7 60.2 %copy-start.4 = (f32[2,1,32]{2,1,0:T(1,128)S(1)}, f32[2,1,32]{2,1,0:T(1,128)}, u32[]{:S(2)}) copy-start(f32[2,1,32]{2,1,0:T(1,128)} %param.21) | copy-start | bytes 772
  107.7 60.2 %copy-start.7 = (f32[1,32]{1,0:T(1,128)S(1)}, f32[1,32]{1,0:T(1,128)}, u32[]{:S(2)}) copy-start(f32[1,32]{1,0:T(1,128)} %param.23) | copy-start | bytes 388
  107.7 60.2 %copy-start.8 = (f32[1,32]{1,0:T(1,128)S(1)}, f32[1,32]{1,0:T(1,128)}, u32[]{:S(2)}) copy-start(f32[1,32]{1,0:T(1,128)} %param.24) | copy-start | bytes 388
  107.7 60.2 %copy-start.9 = (f32[1,32]{1,0:T(1,128)S(1)}, f32[1,32]{1,0:T(1,128)}, u32[]{:S(2)}) copy-start(f32[1,32]{1,0:T(1,128)} %param.25) | copy-start | bytes 388
  107.7 60.2 %copy-start.10 = (f32[1,32]{1,0:T(1,128)S(1)}, f32[1,32]{1,0:T(1,128)}, u32[]{:S(2)}) copy-start(f32[1,32]{1,0:T(1,128)} %param.29) | copy-start | bytes 388
  107.7 68.3 %copy-start.11 = (f32[1,128]{1,0:T(1,128)S(1)}, f32[1,128]{1,0:T(1,128)}, u32[]{:S(2)}) copy-start(f32[1,128]{1,0:T(1,128)} %param.27) | copy-start | bytes 1540
  107.7 113.5 %copy-start.12 = (s32[4]{0:T(128)S(1)}, s32[4]{0:T(128)}, u32[]{:S(2)}) copy-start(s32[4]{0:T(128)} %param.17) | copy-start | bytes 52
  158.9 84.0 %copy-start = (bf16[4,592,256]{2,1,0:T(8,128)(2,1)}, bf16[4,592,256]{2,1,0:T(8,128)(2,1)S(1)}, u32[]{:S(2)}) copy-start(bf16[4,592,256]{2,1,0:T(8,128)(2,1)S(1)} %all-to-all-done.x_h) | copy-start | bytes 3637252
  158.9 497.6 %all-to-all-start.2 = ((bf16[4,592,256]{2,1,0:T(8,128)(2,1)}), bf16[4,592,256]{2,1,0:T(8,128)(2,1)}, u32[]{:S(2)}, u32[]{:S(2)}) async-start(bf16[4,592,256]{2,1,0:T(8,128)(2,1)} %pad.8), calls=%async_computation.2 | async-start | bytes 2424832 | tf_op jit(solution)/shard_map/all_to_all | solution.py:562
  167.8 627.7 %reduce-scatter.16.cloned.1.call-start = ((), (), s32[]{:S(2)}) async-start(), calls=%async_computation.18 | async-start | bytes 40960 | tf_op jit(solution)/shard_map/reduce_scatter | solution.py:584
  756.5 62.5 %reduce-scatter.22.cloned.1.call-start = ((), (), s32[]{:S(2)}) async-start(), calls=%async_computation.21 | async-start | bytes 2621440 | tf_op jit(solution)/shard_map/reduce_scatter | solution.py:531
  760.5 173.0 %reduce-scatter.18.cloned.1.call-start = ((), (), s32[]{:S(2)}) async-start(), calls=%async_computation.19 | async-start | bytes 7864320 | tf_op jit(solution)/shard_map/reduce_scatter | solution.py:531
  761.1 319.5 %reduce-scatter.26.cloned.1.call-start = ((), (), s32[]{:S(2)}) async-start(), calls=%async_computation.23 | async-start | bytes 10485760 | tf_op jit(solution)/shard_map/reduce_scatter | solution.py:531
  761.9 488.1 %reduce-scatter.30.cloned.1.call-start = ((), (), s32[]{:S(2)}) async-start(), calls=%async_computation.25 | async-start | bytes 10485760 | tf_op jit(solution)/shard_map/reduce_scatter | solution.py:531
  773.7 0.7 copy-start.13
  773.7 513.1 %reduce-scatter.36.cloned.1.call-start = ((), (), s32[]{:S(2)}) async-start(), calls=%async_computation.32 | async-start | bytes 589824
  795.5 528.4 %reduce-scatter.34.cloned.1.call-start = ((), (), s32[]{:S(2)}) async-start(), calls=%async_computation.31 | async-start | bytes 147456
  797.1 563.9 %reduce-scatter.24.cloned.1.call-start = ((), (), s32[]{:S(2)}) async-start(), calls=%async_computation.22 | async-start | bytes 589824 | tf_op jit(solution)/shard_map/reduce_scatter | solution.py:532
  819.0 584.0 %reduce-scatter.20.cloned.1.call-start = ((), (), s32[]{:S(2)}) async-start(), calls=%async_computation.20 | async-start | bytes 1769472 | tf_op jit(solution)/shard_map/reduce_scatter | solution.py:532
  933.6 514.1 %reduce-scatter.28.cloned.1.call-start = ((), (), s32[]{:S(2)}) async-start(), calls=%async_computation.24 | async-start | bytes 2359296 | tf_op jit(solution)/shard_map/reduce_scatter | solution.py:532
  1080.7 169.3 %all-to-all-start.1 = ((bf16[4,592,256]{2,1,0:T(8,128)(2,1)}), bf16[4,592,256]{2,1,0:T(8,128)(2,1)S(1)}, u32[]{:S(2)}, u32[]{:S(2)}) async-start(bf16[4,592,256]{2,1,0:T(8,128)(2,1)} %get-tuple-element.32), calls=%async_computation.1 | async-start | bytes 2424832 | tf_op jit(solution)/shard_map/all_to_all | solution.py:562
  1085.9 406.1 %reduce-scatter.32.cloned.1.call-start = ((), (), s32[]{:S(2)}) async-start(), calls=%async_computation.26 | async-start | bytes 2359296 | tf_op jit(solution)/shard_map/reduce_scatter | solution.py:532
  1250.0 83.8 %all-to-all-start.3 = ((bf16[4,592,256]{2,1,0:T(8,128)(2,1)}), bf16[4,592,256]{2,1,0:T(8,128)(2,1)S(1)}, u32[]{:S(2)}, u32[]{:S(2)}) async-start(bf16[4,592,256]{2,1,0:T(8,128)(2,1)} %get-tuple-element.44), calls=%async_computation.3 | async-start | bytes 2424832 | tf_op jit(solution)/shard_map/all_to_all | solution.py:562
Sparse Core Ops, SparseCore 0:
  10.5 27.0 all-gather.15
  40.0 27.8 all-gather.19
  70.4 27.8 all-gather.17
  99.8 73.5 all-gather.23
  174.8 118.2 all-gather.21
  294.5 148.1 all-gather.27
  444.2 147.8 all-gather.25
  756.6 17.1 reduce-scatter.15
  776.2 42.7 reduce-scatter.21
  821.1 112.3 reduce-scatter.17
  935.9 144.6 reduce-scatter.25
  1082.9 167.0 reduce-scatter.29
  1253.6 33.1 reduce-scatter.35
  1290.5 33.3 reduce-scatter.33
  1326.8 34.1 reduce-scatter.23
  1364.5 38.4 reduce-scatter.19
  1406.5 41.1 reduce-scatter.27
  1450.8 41.1 reduce-scatter.31

commit v2 on v1

--- a/solution.py
+++ b/solution.py
@@ -513,6 +513,517 @@
     return outs[0], outs[1], dict(zip(GRADS, outs[2:]))
 
 
+MESH = pl.DeviceIdType.MESH
+PARTS = dict(
+    sv=((4, 4, 2, 16, 256), F32),
+    wqkv=((4, 4, 2, 128, 768), BF16),
+    wout=((4, 2, 4, 256, 128), BF16),
+    w1=((4, 4, 2, 128, 1024), BF16),
+    w2=((4, 2, 4, 1024, 128), BF16),
+)
+BY_COLUMN = ("wout", "w2")
+
+
+def block_of(name, ref, t, yx, c):
+    return ref.at[yx, c, t] if name in BY_COLUMN else ref.at[t, yx, c]
+
+
+def half_of(ref, h):
+    n = ref.shape[0] // 2
+    return ref.at[pl.ds(h * n, n)]
+
+
+class Place:
+    def __init__(self):
+        d, self.t = lax.axis_index("dp"), lax.axis_index("tensor")
+        self.y, self.x, self.c = d // 4, d // 2 % 2, d % 2
+        self.yx = d // 2
+        self.x_yx = self.y * 2 + 1 - self.x
+        self.y_yx = (1 - self.y) * 2 + self.x
+        self.xy_yx = (1 - self.y) * 2 + 1 - self.x
+        self.d = d
+        self.x_id = (self.x_yx * 2 + self.c, self.t)
+        self.y_id = (self.y_yx * 2 + self.c, self.t)
+        self.c_id = (self.yx * 2 + 1 - self.c, self.t)
+
+    def z_id(self, t):
+        return (self.d, t)
+
+    def greet(self):
+        barrier = pltpu.get_barrier_semaphore()
+        others = [self.x_id, self.y_id, self.c_id]
+        others += [self.z_id(lax.rem(self.t + k, 4)) for k in (1, 2, 3)]
+        for other in others:
+            pl.semaphore_signal(barrier, inc=1, device_id=other, device_id_type=MESH)
+        pl.semaphore_wait(barrier, 6)
+
+
+def remote(src, dst, send, recv, where):
+    return pltpu.make_async_remote_copy(
+        src_ref=src, dst_ref=dst, send_sem=send, recv_sem=recv, device_id=where, device_id_type=MESH
+    )
+
+
+class Gather:
+    SENDS = 2 * 3 + 4 * 6 + 4
+
+    def __init__(self, place, name, own, whole, sems):
+        self.p, self.name, self.own, self.whole = place, name, own, whole
+        self.z_send, self.z_recv, self.xy_send, self.xy_recv, self.c_send, self.c_recv = sems
+
+    def at(self, t, yx):
+        return block_of(self.name, self.whole, t, yx, self.p.c)
+
+    def z_copy(self, up, step):
+        p = self.p
+        s = p.t - (step - 1) if up else p.t + (step - 1)
+        src = self.own if step == 1 else self.at(s, p.yx)
+        dst = self.at(s, p.yx)
+        to = p.t + 1 if up else p.t - 1
+        return remote(src, dst, self.z_send.at[1 - up, step - 1], self.z_recv.at[s], p.z_id(to))
+
+    def z_sends(self, step, act):
+        p = self.p
+        for up in (1, 0):
+            going = (p.t < 3) & (p.t - (step - 1) >= 0) if up else (p.t > 0) & (p.t + (step - 1) <= 3)
+
+            @pl.when(going)
+            def _():
+                c = self.z_copy(up, step)
+                c.start() if act == "start" else c.wait_send()
+
+    def xy_copy(self, k, s, mine=False):
+        p = self.p
+        yx = (p.yx, p.yx, p.yx, p.x_yx, p.yx, p.y_yx)[k]
+        h = (0, 1, 0, 0, 1, 1)[k]
+        to = (p.x_id, p.y_id, p.y_id, p.y_id, p.x_id, p.x_id)[k]
+        dst = half_of(self.at(s, yx), h)
+        src = half_of(self.own, h) if mine else dst
+        return remote(src, dst, self.xy_send.at[s, k], self.xy_recv.at[s, k], to)
+
+    def first(self, s, mine=False):
+        for k in (0, 1):
+            self.xy_copy(k, s, mine).start()
+
+    def second(self, s, mine=False):
+        for got, own, other in ((0, 2, 3), (1, 4, 5)):
+            self.xy_copy(own, s, mine).start()
+            self.xy_copy(got, s).wait_recv()
+            self.xy_copy(other, s).start()
+
+    def core_copy(self, s):
+        c = self.p.c
+        ref = self.whole.at[:, c, s] if self.name in BY_COLUMN else self.whole.at[s, :, c]
+        return remote(ref, ref, self.c_send.at[s], self.c_recv.at[s], self.p.c_id)
+
+    def last(self, s):
+        for k in (2, 3, 4, 5):
+            self.xy_copy(k, s).wait_recv()
+        self.core_copy(s).start()
+
+    def each(self, step, do):
+        p = self.p
+        if step == 0:
+            do(p.t)
+            return
+
+        @pl.when(p.t - step >= 0)
+        def _():
+            do(p.t - step)
+
+        @pl.when(p.t + step <= 3)
+        def _():
+            do(p.t + step)
+
+    def stage(self, i):
+        if i == 0:
+            self.z_sends(1, "start")
+            self.first(self.p.t, True)
+        if 1 <= i <= 3:
+
+            def arrived(s):
+                remote(
+                    self.at(s, self.p.yx), self.at(s, self.p.yx), self.z_send.at[0, 0], self.z_recv.at[s], self.p.c_id
+                ).wait_recv()
+
+            self.each(i, arrived)
+            if i < 3:
+                self.z_sends(i + 1, "start")
+            self.each(i, self.first)
+        if 1 <= i <= 4:
+            self.each(i - 1, functools.partial(self.second, mine=i == 1))
+        if 2 <= i <= 5:
+            self.each(i - 2, self.last)
+
+    def done(self):
+        for s in range(4):
+            self.core_copy(s).wait_recv()
+
+    def finish(self):
+        for step in (1, 2, 3):
+            self.z_sends(step, "wait")
+        for s in range(4):
+            for k in range(6):
+                self.xy_copy(k, s).wait_send()
+            self.core_copy(s).wait_send()
+
+
+GATHER_SEMS = [
+    pltpu.SemaphoreType.DMA((2, 3)),
+    pltpu.SemaphoreType.DMA((4,)),
+    pltpu.SemaphoreType.DMA((4, 6)),
+    pltpu.SemaphoreType.DMA((4, 6)),
+    pltpu.SemaphoreType.DMA((4,)),
+    pltpu.SemaphoreType.DMA((4,)),
+]
+
+
+class Swap:
+    SEMS = [pltpu.SemaphoreType.DMA((4,)), pltpu.SemaphoreType.DMA((4,))]
+
+    def __init__(self, place, pieces, whole, sems):
+        self.p, self.pieces, self.whole = place, pieces, whole
+        self.send, self.recv = sems
+
+    def copy(self, k):
+        p = self.p
+        to = lax.rem(p.t + k, 4)
+        return remote(self.pieces.at[to], self.whole.at[p.t], self.send.at[k], self.recv.at[k], p.z_id(to))
+
+    def start(self):
+        for k in (1, 3, 2):
+            self.copy(k).start()
+
+    def done(self):
+        for k in (1, 2, 3):
+            self.copy(k).wait_recv()
+
+    def finish(self):
+        for k in (1, 2, 3):
+            self.copy(k).wait_send()
+
+
+class Bounce:
+    def __init__(self, src, buf, dst, sems):
+        self.load = pltpu.make_async_copy(src, buf, sems.at[0])
+        self.store = pltpu.make_async_copy(buf, dst, sems.at[1])
+
+
+def gather_kernel(x_in, ct_in, *rest):
+    names = list(PARTS)
+    n = len(names)
+    own = dict(zip(names, rest[:n]))
+    x, ct = rest[n : n + 2]
+    whole = dict(zip(names, rest[n + 2 : 2 * n + 2]))
+    rest = rest[2 * n + 2 :]
+    bufs, (x_buf, ct_buf) = dict(zip(names, rest[:n])), rest[n : n + 2]
+    rest = rest[n + 2 :]
+    local_sem, swap_sems, sems = rest[0], rest[1:5], rest[5:]
+    place = Place()
+    gathers = [
+        Gather(place, a, own[a], whole[a], sems[6 * i : 6 * i + 6]) for i, a in enumerate(names)
+    ]
+    swaps = [Swap(place, x_in, x, swap_sems[0:2]), Swap(place, ct_in, ct, swap_sems[2:4])]
+    local = [
+        Bounce(own[a], bufs[a], block_of(a, whole[a], place.t, place.yx, place.c), local_sem.at[i])
+        for i, a in enumerate(names)
+    ]
+    local += [
+        Bounce(x_in.at[place.t], x_buf, x.at[place.t], local_sem.at[n]),
+        Bounce(ct_in.at[place.t], ct_buf, ct.at[place.t], local_sem.at[n + 1]),
+    ]
+    for b in local:
+        b.load.start()
+    place.greet()
+    for b in local:
+        b.load.wait()
+        b.store.start()
+    swaps[0].start()
+    stored = False
+    for tick in range(n + 5):
+        for i, g in enumerate(gathers):
+            if tick - i == 2 and not stored:
+                for b in local:
+                    b.store.wait()
+                stored = True
+            if 0 <= tick - i <= 5:
+                g.stage(tick - i)
+        if tick == 3:
+            swaps[1].start()
+    for g in gathers:
+        g.done()
+    for s in swaps:
+        s.done()
+        s.finish()
+    for g in gathers:
+        g.finish()
+
+
+def gather(x_in, ct_in, own):
+    names = list(PARTS)
+    n = len(names)
+    outs = pl.pallas_call(
+        gather_kernel,
+        out_shape=[IMAGE, IMAGE] + [jax.ShapeDtypeStruct(*PARTS[a]) for a in names],
+        in_specs=[ANY] * (n + 2),
+        out_specs=[ANY] * (n + 2),
+        scratch_shapes=[pltpu.VMEM(PARTS[a][0][3:], PARTS[a][1]) for a in names]
+        + [pltpu.VMEM((ROWS, 256), BF16)] * 2
+        + [pltpu.SemaphoreType.DMA((n + 2, 2))]
+        + Swap.SEMS * 2
+        + GATHER_SEMS * n,
+        compiler_params=pltpu.CompilerParams(
+            collective_id=0, has_side_effects=True, vmem_limit_bytes=VMEM_BYTES
+        ),
+        name="gather",
+    )(x_in, ct_in, *[own[a] for a in names])
+    return outs[0], outs[1], dict(zip(names, outs[2:]))
+
+
+REDUCED = ("w2", "w1", "wout", "wqkv")
+
+
+class Reduce:
+    def __init__(self, place, name, grad, own, got, got1, got2, got3, result, sems):
+        self.p, self.name, self.grad, self.own, self.got = place, name, grad, own, got
+        self.got1, self.got2, self.got3, self.result = got1, got2, got3, result
+        self.send, self.recv, self.local = sems
+
+    def plane(self, c):
+        return self.grad.at[:, c] if self.name in BY_COLUMN else self.grad.at[:, :, c]
+
+    def block(self, ref, t, yx):
+        return ref.at[yx, t] if self.name in BY_COLUMN else ref.at[t, yx]
+
+    def core_copy(self):
+        return remote(self.plane(1 - self.p.c), self.got, self.send.at[0], self.recv.at[0], self.p.c_id)
+
+    def own_copy(self):
+        return pltpu.make_async_copy(self.plane(self.p.c), self.own, self.local)
+
+    def add(self, dst, *more):
+        rows = dst.shape[0]
+        n = min(64, rows)
+
+        @pl.loop(0, rows // n)
+        def _(i):
+            r = pl.ds(pl.multiple_of(i * n, n), n)
+            total = dst[r, :].astype(F32)
+            for ref in more:
+                total += ref[r, :].astype(F32)
+            dst[r, :] = total.astype(BF16)
+
+    def first_copy(self, by_y, j, t):
+        p = self.p
+        yx = (1 - p.y) * 2 + j if by_y else j * 2 + 1 - p.x
+        src = half_of(self.block(self.own, t, yx), 0 if by_y else 1)
+        k = (0 if by_y else 2) + j
+        n = 1 + k * 4 + t
+        return remote(src, self.got1.at[k, t], self.send.at[n], self.recv.at[n], p.y_id if by_y else p.x_id)
+
+    def second_copy(self, j, t):
+        p = self.p
+        by_x = j == 0
+        src = half_of(self.block(self.own, t, p.x_yx if by_x else p.y_yx), j)
+        return remote(src, self.got2.at[j, t], self.send.at[17 + j * 4 + t], self.recv.at[17 + j * 4 + t],
+                      p.x_id if by_x else p.y_id)
+
+    def z_copy(self, k):
+        p = self.p
+        to = lax.rem(p.t + k, 4)
+        src = self.block(self.own, to, p.yx)
+        return remote(src, self.got3.at[k - 1], self.send.at[24 + k], self.recv.at[24 + k], p.z_id(to))
+
+    def stage(self, i):
+        p = self.p
+        if i == 0:
+            self.core_copy().start()
+            self.own_copy().start()
+        if i == 1:
+            self.own_copy().wait()
+            self.core_copy().wait_recv()
+            self.sum_core()
+        if i == 2:
+            self.sum_first()
+        if i == 3:
+            self.sum_second()
+        if i == 4:
+            self.sum_last()
+
+    def sum_core(self):
+        p = self.p
+        for yx, by_y, by_x in ((p.xy_yx, 1 - p.x, 1 - p.y), (p.y_yx, p.x, None), (p.x_yx, None, p.y), (p.yx, None, None)):
+            for t in range(4):
+                self.add(self.block(self.own, t, yx), self.block(self.got, t, yx))
+                if by_y is not None:
+                    self.first_copy(True, by_y, t).start()
+                if by_x is not None:
+                    self.first_copy(False, by_x, t).start()
+
+    def sum_first(self):
+        p = self.p
+        for t in range(4):
+            for j in range(2):
+                self.first_copy(True, j, t).wait_recv()
+                self.first_copy(False, j, t).wait_recv()
+        for t in range(4):
+            self.add(half_of(self.block(self.own, t, p.x_yx), 0), self.got1.at[1 - p.x, t])
+            self.second_copy(0, t).start()
+            self.add(half_of(self.block(self.own, t, p.y_yx), 1), self.got1.at[2 + 1 - p.y, t])
+            self.second_copy(1, t).start()
+        for t in range(4):
+            self.add(half_of(self.block(self.own, t, p.yx), 0), self.got1.at[p.x, t])
+            self.add(half_of(self.block(self.own, t, p.yx), 1), self.got1.at[2 + p.y, t])
+
+    def sum_second(self):
+        p = self.p
+        for k in (1, 2, 3, 0):
+            t = lax.rem(p.t + k, 4)
+            for j in (0, 1):
+                self.second_copy(j, t).wait_recv()
+                self.add(half_of(self.block(self.own, t, p.yx), j), self.got2.at[j, t])
+            if k:
+                self.z_copy(k).start()
+
+    def sum_last(self):
+        p = self.p
+        for k in (1, 2, 3):
+            self.z_copy(k).wait_recv()
+        mine = self.block(self.own, p.t, p.yx)
+        rows = mine.shape[0]
+
+        @pl.loop(0, rows // 64)
+        def _(i):
+            r = pl.ds(pl.multiple_of(i * 64, 64), 64)
+            total = mine[r, :].astype(F32)
+            for k in range(3):
+                total += self.got3[k, r, :].astype(F32)
+            self.result[r, :] = total
+
+    def finish(self):
+        self.core_copy().wait_send()
+        for t in range(4):
+            for j in range(2):
+                self.first_copy(True, j, t).wait_send()
+                self.first_copy(False, j, t).wait_send()
+                self.second_copy(j, t).wait_send()
+        for k in (1, 2, 3):
+            self.z_copy(k).wait_send()
+
+
+def reduce_shapes(name):
+    shape = PARTS[name][0]
+    rows, width = shape[3:]
+    plane = (4, 4, rows, width)
+    return plane, (4, 4, rows // 2, width), (2, 4, rows // 2, width), (3, rows, width), (rows, width)
+
+
+class Total:
+    def __init__(self, place, acc, sent, got, sems):
+        self.p, self.acc, self.sent, self.got = place, acc, sent, got
+        self.send, self.recv = sems
+
+    def copies(self, i):
+        p = self.p
+        if i < 3:
+            return [remote(self.sent.at[i], self.got.at[i], self.send.at[i], self.recv.at[i], (p.c_id, p.x_id, p.y_id)[i])]
+        return [
+            remote(self.sent.at[3], self.got.at[2 + k], self.send.at[2 + k], self.recv.at[2 + k], p.z_id(lax.rem(p.t + k, 4)))
+            for k in (1, 2, 3)
+        ]
+
+    def start(self, i):
+        self.sent[i] = self.acc[...]
+        for c in self.copies(i):
+            c.start()
+
+    def end(self, i):
+        for c in self.copies(i):
+            c.wait()
+        for k in (i,) if i < 3 else (3, 4, 5):
+            self.acc[...] += self.got[k]
+
+
+def reduce_kernel(out_in, gtok_in, sums_in, *rest):
+    n = len(REDUCED)
+    grads = dict(zip(REDUCED, rest[:n]))
+    out, gtok, sums = rest[n : n + 3]
+    results = dict(zip(REDUCED, rest[n + 3 : 2 * n + 3]))
+    rest = rest[2 * n + 3 :]
+    out_buf, gtok_buf, sent, got = rest[:4]
+    local_sem, total_send, total_recv = rest[4:7]
+    swap_sems = rest[7:11]
+    rest = rest[11:]
+    place = Place()
+    parts = []
+    for i, a in enumerate(REDUCED):
+        own, got0, got1, got2, got3, send, recv, local = rest[8 * i : 8 * i + 8]
+        parts.append(Reduce(place, a, grads[a], own, got0, got1, got2, got3, results[a], (send, recv, local)))
+    swaps = [Swap(place, out_in, out, swap_sems[0:2]), Swap(place, gtok_in, gtok, swap_sems[2:4])]
+    local = [
+        Bounce(out_in.at[place.t], out_buf, out.at[place.t], local_sem.at[0]),
+        Bounce(gtok_in.at[place.t], gtok_buf, gtok.at[place.t], local_sem.at[1]),
+    ]
+    for b in local:
+        b.load.start()
+    place.greet()
+    for r in parts:
+        r.stage(0)
+    total = Total(place, sums, sent, got, (total_send, total_recv))
+    sums[...] = sums_in[...]
+    total.start(0)
+    for b in local:
+        b.load.wait()
+        b.store.start()
+    for s in swaps:
+        s.start()
+    small = 0
+    for tick in range(1, n + 4):
+        for i, r in enumerate(parts):
+            if 1 <= tick - i <= 4:
+                r.stage(tick - i)
+        if small < 4:
+            total.end(small)
+            small += 1
+            if small < 4:
+                total.start(small)
+    for b in local:
+        b.store.wait()
+    for s in swaps:
+        s.done()
+        s.finish()
+    for r in parts:
+        r.finish()
+
+
+def reduce(out, gtok, sums, grads):
+    n = len(REDUCED)
+    shapes = [reduce_shapes(a) for a in REDUCED]
+    outs = pl.pallas_call(
+        reduce_kernel,
+        out_shape=[IMAGE, IMAGE, jax.ShapeDtypeStruct((16, D), F32)]
+        + [jax.ShapeDtypeStruct(s[4], F32) for s in shapes],
+        in_specs=[ANY, ANY, VM] + [ANY] * n,
+        out_specs=[ANY, ANY, VM] + [VM] * n,
+        scratch_shapes=[pltpu.VMEM((ROWS, 256), BF16)] * 2
+        + [pltpu.VMEM((4, 16, D), F32), pltpu.VMEM((6, 16, D), F32)]
+        + [pltpu.SemaphoreType.DMA((2, 2)), pltpu.SemaphoreType.DMA((6,)), pltpu.SemaphoreType.DMA((6,))]
+        + Swap.SEMS * 2
+        + sum(
+            (
+                [pltpu.VMEM(s[0], BF16)] * 2
+                + [pltpu.VMEM(s[k], BF16) for k in (1, 2, 3)]
+                + [pltpu.SemaphoreType.DMA((28,)), pltpu.SemaphoreType.DMA((28,)), pltpu.SemaphoreType.DMA]
+                for s in shapes
+            ),
+            [],
+        ),
+        compiler_params=pltpu.CompilerParams(
+            collective_id=1, has_side_effects=True, vmem_limit_bytes=VMEM_BYTES
+        ),
+        name="reduce",
+    )(out, gtok, sums, *[grads[a].reshape(PARTS[a][0]) for a in REDUCED])
+    return outs[0], outs[1], outs[2], dict(zip(REDUCED, outs[3:]))
 def gather_plain(w_qkv, w_out, w_fc1, w_fc2):
     def all_of(shard, axis):
         return lax.all_gather(
@@ -539,6 +1050,7 @@
 
 
 def on_device(
+    dp,
     tokens_in,
     cotangent,
     slot_mask,
@@ -567,32 +1079,55 @@
     small = jnp.concatenate(
         (norm1_gain, norm1_bias, b_qkv[0], b_qkv[1], b_out, norm2_gain, norm2_bias, b_fc2)
     ).astype(BF16)
-    vectors = lax.all_gather(
-        lax.all_gather(small, "dp", axis=1, tiled=True), "tensor", axis=0
-    ).astype(F32)
-    hidden_bias = lax.all_gather(
-        lax.all_gather(b_fc1.astype(BF16), "dp", axis=1, tiled=True), "tensor", axis=0
-    ).astype(F32)
-    x = exchange(images(tokens_in))
-    ct = exchange(images(cotangent))
-    weights = gather_plain(w_qkv, w_out, w_fc1, w_fc2)
+    d, t = lax.axis_index("dp"), lax.axis_index("tensor")
+    if dp == 8:
+        sv = lax.dynamic_update_slice(jnp.zeros((16, 256), F32), small.astype(F32), (0, d * 32))
+        sv = sv.at[8, 0:128].set(b_fc1[0].astype(BF16).astype(F32))
+        own = dict(
+            sv=sv,
+            wqkv=w_qkv.reshape(128, 768).astype(BF16),
+            wout=w_out.astype(BF16),
+            w1=w_fc1.astype(BF16),
+            w2=w_fc2.astype(BF16),
+        )
+        x, ct, whole = gather(images(tokens_in), images(cotangent), own)
+        vectors = jnp.sum(whole["sv"][:, :, :, 0:8], axis=(1, 2))
+        hidden_bias = whole["sv"][:, :, :, 8, 0:128].reshape(4, 1, 1024)
+        weights = [whole[a].reshape(GRADS[a].shape) for a in GRADS]
+    else:
+        vectors = lax.all_gather(
+            lax.all_gather(small, "dp", axis=1, tiled=True), "tensor", axis=0
+        ).astype(F32)
+        hidden_bias = lax.all_gather(
+            lax.all_gather(b_fc1.astype(BF16), "dp", axis=1, tiled=True), "tensor", axis=0
+        ).astype(F32)
+        x = exchange(images(tokens_in))
+        ct = exchange(images(cotangent))
+        weights = gather_plain(w_qkv, w_out, w_fc1, w_fc2)
     out, probs, saved = forward(x, *weights, vectors, hidden_bias, mask)
     gtok, sums, grads = backward(x, ct, *weights, vectors, mask, probs, saved)
-    g_qkv, g_out, g_fc1, g_fc2 = scatter_plain(grads)
-
-    def total(part, axis):
-        part = lax.psum_scatter(part, "tensor", scatter_dimension=0, tiled=True)
-        return lax.psum_scatter(part, "dp", scatter_dimension=axis, tiled=True)
-
-    g_small = total(sums[0:8].reshape(8, 4, 256).transpose(1, 0, 2), 2)[0]
-    g_hidden = total(sums[8:12], 1)
+    if dp == 8:
+        out, gtok, sums, got = reduce(out, gtok, jnp.pad(sums, ((0, 4), (0, 0))), grads)
+        g_qkv, g_out, g_fc1, g_fc2 = (got[a] for a in GRADS)
+        g_small = lax.dynamic_slice(sums, (0, t * 256 + d * 32), (8, 32))
+        g_hidden = lax.dynamic_slice(sums, (8 + t, d * 128), (1, 128))
+    else:
+        g_qkv, g_out, g_fc1, g_fc2 = scatter_plain(grads)
+        out, gtok = exchange(out), exchange(gtok)
+
+        def total(part, axis):
+            part = lax.psum_scatter(part, "tensor", scatter_dimension=0, tiled=True)
+            return lax.psum_scatter(part, "dp", scatter_dimension=axis, tiled=True)
+
+        g_small = total(sums[0:8].reshape(8, 4, 256).transpose(1, 0, 2), 2)[0]
+        g_hidden = total(sums[8:12], 1)
 
     def rows(pieces):
         return pieces[:, :SEQ].reshape(4 * SEQ, 256)
 
     return (
-        rows(exchange(out)),
-        rows(exchange(gtok)),
+        rows(out),
+        rows(gtok),
         g_small[0:1],
         g_small[1:2],
         g_qkv.reshape(w_qkv.shape),
@@ -613,7 +1148,7 @@
     mixed, pair = P("dp", None, "tensor"), P(None, "tensor", "dp")
     params = (turned, turned, mixed, pair, turned, turned, turned, turned, both, turned, turned, turned)
     return jax.shard_map(
-        on_device,
+        functools.partial(on_device, mesh.shape["dp"]),
         mesh=mesh,
         in_specs=(both, both, P("dp"), *params),
         out_specs=(both, both, *params),

time: 1500 us -> 470 us (0.31)
  waiting for transfers between devices: 1120 us -> 0 us
  Pallas kernels: 162 us -> 443 us
  blocking collectives: 98.6 us -> 0 us
  local copies, waits for them, and re-layouts: 74.1 us -> 21.5 us
  starting transfers between devices: 23.5 us -> 0 us
    reduce_scatter x9 -> x0, waiting for transfers between devices: 599 us -> none  [the longest x4 447 us: mine(): part = lax.psum_scatter(grad, 'tensor', scatter_dimension=0, tiled=True)]
    all_gather x7 -> x0, waiting for transfers between devices: 403 us -> none  [the longest x4 329 us: all_of(): lax.all_gather(lax.all_gather(shard.astype(BF16), 'dp', axis=axis, tiled=...]
    pallas_call x0 -> x2, Pallas kernels: none -> 280 us  [the longest x1 142 us: gather(): pl.pallas_call(gather_kernel, out_shape=[IMAGE, IMAGE] + [jax.ShapeDtypeS...]
    all_gather x5 -> x0, blocking collectives: 80.4 us -> none  [the longest x1 35.9 us: on_device(): lax.all_gather(lax.all_gather(b_fc1.astype(BF16), 'dp', axis=1, tiled=Tru...]
    unnamed x20 -> x0, waiting for transfers between devices: 70.4 us -> none
    all_to_all x4 -> x0, waiting for transfers between devices: 51.1 us -> none  [exchange(): lax.all_to_all(pieces, 'tensor', split_axis=0, concat_axis=0, tiled=True)]
    all_to_all x4 -> x0, starting transfers between devices: 22.9 us -> none  [exchange(): lax.all_to_all(pieces, 'tensor', split_axis=0, concat_axis=0, tiled=True)]
    unnamed x1 -> x0, blocking collectives: 18.1 us -> none
  transfers between devices with their start and end apart: 22 -> 0, of which waited for: 17 -> 0; matrix products, arithmetic and copies ran while one was open for 5% -> 0% of each run, Pallas kernels for 4% -> 0%
where the time goes in v2:
time: 470 us
  Pallas kernels  443 us (94%)
  local copies, waits for them, and re-layouts  21.5 us (5%)
    pallas_call x1, Pallas kernels, gather(): pl.pallas_call(gather_kernel, out_shape=[IMAGE, IMAGE] + [jax.ShapeDtypeS...  142 us
    pallas_call x1, Pallas kernels, reduce(): pl.pallas_call(reduce_kernel, out_shape=[IMAGE, IMAGE, jax.ShapeDtypeStru...  138 us
    pallas_call x1, Pallas kernels, backward(): pl.pallas_call(backward_kernel, out_shape=[IMAGE, jax.ShapeDtypeStruct((1...  98.7 us
    pallas_call x1, Pallas kernels, forward(): pl.pallas_call(forward_kernel, out_shape=[IMAGE, PROBS, *SAVED.values()],...  63.8 us

profile of v2, /device:TPU:10, one launch (start us, length us, event | category | flops | bytes accessed | tf_op | source)
XLA Modules:
  0.0 469.7 jit_solution(14514324060948555959)
XLA Ops:
  0.6 1.6 reshape.101
  2.2 0.0 copy-start
  2.2 1.1 pad.14.x_in
  3.4 0.6 copy-done
  3.9 0.3 reshape.102
  4.3 0.0 copy-start.12
  4.3 0.0 copy-start.13
  4.3 0.0 copy-start.11
  4.3 0.0 copy-start.14
  4.3 0.0 copy-start.15
  4.3 0.0 copy-start.16
  4.3 0.0 copy-start.17
  4.3 0.0 copy-start.18
  4.4 0.0 copy-start.6
  4.4 0.0 copy-start.8
  4.4 1.2 pad.15.ct_in
  5.5 0.0 copy-done.12
  5.6 0.0 copy-done.13
  5.6 0.0 copy-done.11
  5.6 0.0 copy-done.14
  5.6 0.0 copy-done.15
  5.7 0.0 copy-done.16
  5.7 0.0 copy-done.17
  5.8 0.7 dynamic_update_slice.3
  6.4 0.0 copy-done.18
  6.5 0.2 scatter.4.rest_0_
  6.7 0.0 copy-done.6
  6.7 0.0 copy-start.10
  6.7 0.2 copy.32
  6.9 0.8 copy.33.rest_1_
  7.7 0.0 copy-done.8
  7.7 0.6 convert_element_type.41.rest_2_
  8.4 0.0 copy-done.2
  8.4 0.7 convert_element_type.42.rest_3_
  9.1 0.0 copy-done.3
  9.1 0.7 convert_element_type.43.rest_4_
  9.8 0.0 copy-done.10
  9.8 142.4 %gather.1 = (bf16[4,592,256]{2,1,0:T(8,128)(2,1)}, bf16[4,592,256]{2,1,0:T(8,128)(2,1)}, f32[4,4,2,16,256]{4,3,2,1,0:T(8,128)}, bf16[4,4,2,128,768]{4,3,2,1,0:T(...) custom-call(bf16[4,592,256]{2,1,0:T(8,128)(2,1)} %pad.14.x_in, ...), custom_call_target="tpu_custom_call" | custom-call | tf_op jit(solution)/shard_map/gather/pallas_call | solution.py:765
  152.3 1.6 slice_reduce_fusion.vectors
  153.8 1.5 slice.63
  155.4 0.0 copy-done.19
  155.4 0.6 dynamic_slice.10
  156.6 0.6 broadcast_in_dim.12.mask
  157.2 63.8 %forward.1 = (bf16[4,592,256]{2,1,0:T(8,128)(2,1)}, bf16[8,2,592,592]{3,2,1,0:T(8,128)(2,1)}, bf16[1024,592]{1,0:T(8,128)(2,1)}, bf16[592,1024]{1,0:T(8,128)(2,1...) custom-call(bf16[4,592,256]{2,1,0:T(8,128)(2,1)} %get-tuple-element., ...), custom_call_target="tpu_custom_call" | custom-call | tf_op jit(solution)/shard_map/forward/pallas_call | solution.py:273
  221.0 98.7 %backward.1 = (bf16[4,592,256]{2,1,0:T(8,128)(2,1)}, f32[12,1024]{1,0:T(8,128)}, bf16[4,1024,768]{2,1,0:T(8,128)(2,1)}, bf16[8,1024,128]{2,1,0:T(8,128)(2,1)}, b...) custom-call(bf16[4,592,256]{2,1,0:T(8,128)(2,1)} %get-tuple-element.58.x_h, ...), custom_call_target="tpu_custom_call" | custom-call | tf_op jit(solution)/shard_map/backward/pallas_call | solution.py:487
  319.7 1.5 pad.16.sums_in
  321.2 137.8 %reduce.3 = (bf16[4,592,256]{2,1,0:T(8,128)(2,1)}, bf16[4,592,256]{2,1,0:T(8,128)(2,1)}, f32[16,1024]{1,0:T(8,128)}, f32[1024,128]{1,0:T(8,128)}, f32[128,1024]{...) custom-call(bf16[4,592,256]{2,1,0:T(8,128)(2,1)} %get-tuple-element.64.out_in, ...), custom_call_target="tpu_custom_call" | custom-call | tf_op jit(solution)/shard_map/reduce/pallas_call | solution.py:1002
  459.1 1.4 slice.64
  460.4 0.0 copy-start.1
  460.4 1.3 reshape.111
  461.8 0.0 copy-done.1
  461.8 0.1 slice.65
  461.9 1.3 reshape.112
  463.2 0.8 constant_dynamic-slice_fusion
  464.0 0.5 fusion
  464.6 0.2 copy.34
  464.7 0.0 copy-start.4
  464.7 0.9 copy.35
  465.6 0.6 slice.68
  466.2 1.3 dynamic_slice.12
  467.5 0.7 copy.42
  468.1 0.8 copy.43
  468.9 0.0 copy-done.4
  468.9 0.8 copy.44
  (21 shorter events, 0.1 us)
Async XLA Ops:
  2.2 1.7 copy-start
  4.3 1.3 copy-start.12
  4.3 1.3 copy-start.13
  4.3 1.3 copy-start.11
  4.3 1.3 copy-start.14
  4.3 1.3 copy-start.15
  4.3 1.3 copy-start.16
  4.3 1.3 copy-start.17
  4.3 2.1 copy-start.18
  4.4 2.3 copy-start.6
  4.4 3.3 copy-start.8
  5.5 2.8 copy-start.2
  5.6 3.6 copy-start.3
  6.7 3.1 copy-start.10
  9.8 145.5 %copy-start.19 = (s32[4]{0:T(128)S(1)}, s32[4]{0:T(128)}, u32[]{:S(2)}) copy-start(s32[4]{0:T(128)} %param.19) | copy-start | bytes 52
  460.4 1.4 copy-start.1
  461.9 2.7 copy-start.7
  463.2 4.3 copy-start.9
  463.2 4.9 %copy-start.5 = (f32[128,1024]{1,0:T(8,128)S(1)}, f32[128,1024]{1,0:T(8,128)}, u32[]{:S(2)}) copy-start(f32[128,1024]{1,0:T(8,128)} %get-tuple-element.150) | copy-start | bytes 1572868
  464.7 4.2 copy-start.4

commit v3 on v2

--- a/solution.py
+++ b/solution.py
@@ -10,7 +10,7 @@
 HD = 64
 SEQ = 577
 ROWS = 592
-STEP = 16
+CHUNK = 32
 F32 = jnp.float32
 BF16 = jnp.bfloat16
 LAST = (((1,), (1,)), ((), ()))
@@ -41,6 +41,14 @@
     return jnp.concatenate([ref[t, rows, :].astype(F32) for t in range(4)], axis=1)
 
 
+def over_rows(do):
+    @pl.loop(0, 576 // CHUNK)
+    def _(i):
+        do(pl.ds(pl.multiple_of(i * CHUNK, CHUNK), CHUNK))
+
+    do(pl.ds(576, ROWS - 576))
+
+
 def vec(vectors, row):
     return jnp.concatenate([vectors[t, row : row + 1, :] for t in range(4)], axis=1)
 
@@ -48,9 +56,8 @@
 def norm_in(x, vectors, nin):
     gain, shift = vec(vectors, 0), vec(vectors, 1)
 
-    @pl.loop(0, ROWS // STEP)
-    def _(i):
-        rows = pl.ds(pl.multiple_of(i * STEP, STEP), STEP)
+    @over_rows
+    def _(rows):
         xhat, _ = row_stats(wide(x, rows))
         nin[rows, :] = (xhat * gain + shift).astype(BF16)
 
@@ -62,10 +69,14 @@
 
 
 def project(nin, wqkv, vectors, t, q, k, v):
-    here = pl.ds(t * 256, 256)
-    q[:, here] = (mm(nin[...], wqkv[t, :, 0:256]) + vectors[t, 2:3, :]).astype(BF16)
-    k[:, here] = mm(nin[...], wqkv[t, :, 256:512]).astype(BF16)
-    v[:, here] = (mm(nin[...], wqkv[t, :, 512:768]) + vectors[t, 3:4, :]).astype(BF16)
+    here = cols(t, 256)
+
+    def part(c):
+        return mm(nin[...], wqkv[t, :, :, :, c * 256 : c * 256 + 256].reshape(D, 256))
+
+    q[:, here] = (part(0) + vectors[t, 2:3, :]).astype(BF16)
+    k[:, here] = part(1).astype(BF16)
+    v[:, here] = (part(2) + vectors[t, 3:4, :]).astype(BF16)
 
 
 def attend_pair(pair, q, k, v, ctx, probs, slot):
@@ -95,16 +106,15 @@
 
 
 def out_block(i, ctx, wout, x, vectors, resid):
-    w = jnp.concatenate([wout[2 * i], wout[2 * i + 1]], axis=1)
+    w = jnp.concatenate([wout[i, c].reshape(D, 128) for c in range(2)], axis=1)
     resid[:, cols(i, 256)] = x[i].astype(F32) + mm(ctx[...], w) + vectors[i, 4:5, :]
 
 
 def norm_mid(resid, vectors, nmid):
     gain, shift = vec(vectors, 5), vec(vectors, 6)
 
-    @pl.loop(0, ROWS // STEP)
-    def _(i):
-        rows = pl.ds(pl.multiple_of(i * STEP, STEP), STEP)
+    @over_rows
+    def _(rows):
         xhat, _ = row_stats(resid[rows, :])
         nmid[rows, :] = (xhat * gain + shift).astype(BF16)
 
@@ -112,7 +122,7 @@
 def hidden_tile(t, j, nmid, w1, b1, act, act_t, slope):
     here = pl.ds(pl.multiple_of(t * 1024 + j * 256, 256), 256)
     bias = b1[t, :, cols(j, 256)]
-    pre = mm(nmid[...], w1[t, :, cols(j, 256)]) + bias
+    pre = mm(nmid[...], w1[t, :, :, :, cols(j, 256)].reshape(D, 256)) + bias
     sig = 1.0 / (1.0 + jnp.exp(-1.702 * pre))
     a = pre * sig
     slope[:, here] = (sig + 1.702 * a * (1.0 - sig)).astype(BF16)
@@ -121,10 +131,13 @@
     act_t[here, :] = low.T
 
 
-def down_block(i, act, w2, resid, vectors, mask, out):
-    w = jnp.concatenate([w2[2 * i], w2[2 * i + 1]], axis=1)
-    total = resid[:, cols(i, 256)] + mm(act[...], w) + vectors[i, 7:8, :]
-    out[i] = (total * mask[...]).astype(BF16)
+def down_block(i, t, act, w2, total):
+    w = jnp.concatenate([w2[i, c, t] for c in range(2)], axis=1)
+    total[:, cols(i, 256)] += mm(act[:, cols(t, 1024)], w)
+
+
+def finish_block(i, total, vectors, mask, out):
+    out[i] = ((total[:, cols(i, 256)] + vectors[i, 7:8, :]) * mask[...]).astype(BF16)
 
 
 def grad_norm_rows(values, gain, n):
@@ -136,7 +149,7 @@
 
 
 def fold(a):
-    return a[0:8] + a[8:16]
+    return jnp.sum(a.reshape(-1, 8, D), axis=0)
 
 
 def attend_back_pair(pair, q, k, v, ctx, gctx, probs, slot, gmix, sums):
@@ -203,93 +216,148 @@
     return pltpu.VMEM(like.shape, like.dtype)
 
 
+PARTS = dict(
+    sv=((4, 4, 2, 16, 256), F32),
+    wqkv=((4, 4, 2, 128, 768), BF16),
+    wout=((4, 2, 4, 256, 128), BF16),
+    w1=((4, 4, 2, 128, 1024), BF16),
+    w2=((4, 2, 4, 1024, 128), BF16),
+)
+WEIGHTS = ("wqkv", "wout", "w1", "w2")
+
+
+def part(name):
+    return jax.ShapeDtypeStruct(*PARTS[name])
+
+
+class Forward:
+    SCRATCH = [scratch(a) for a in SAVED.values()] + [
+        scratch(ACT),
+        pltpu.VMEM((ROWS, 4 * D), BF16),
+        pltpu.VMEM((ROWS, D), F32),
+        pltpu.VMEM((2, 2, ROWS, ROWS), BF16),
+        scratch(IMAGE),
+        pltpu.SemaphoreType.DMA((2,)),
+        pltpu.SemaphoreType.DMA((len(SAVED) + 1,)),
+    ]
+
+    def __init__(self, x, weights, vectors, b1, mask, out_h, probs_h, saved_h, refs):
+        n = len(SAVED)
+        self.x, self.w, self.vectors, self.b1, self.mask = x, weights, vectors, b1, mask
+        self.out_h, self.probs_h, self.saved_h = out_h, probs_h, saved_h
+        self.saved = dict(zip(SAVED, refs[:n]))
+        self.normed, self.act, self.total, self.probs, self.out, self.probs_sem, self.out_sem = refs[n:]
+
+    def start_norm(self):
+        norm_in(self.x, self.vectors, self.normed)
+        flip(self.normed, self.saved["nin_t"], D)
+
+    def put(self, pair, slot):
+        return pltpu.make_async_copy(self.probs.at[slot], self.probs_h.at[pair], self.probs_sem.at[slot])
+
+    def heads(self, s, i):
+        a = self.saved
+        project(self.normed, self.w["wqkv"], self.vectors, s, a["q"], a["k"], a["v"])
+
+        @pl.loop(0, 2)
+        def _(slot):
+            pair = s * 2 + slot
+            if i:
+                self.put(pair, slot).wait()
+            attend_pair(pair, a["q"], a["k"], a["v"], a["ctx"], self.probs, slot)
+            self.put(pair, slot).start()
+
+    def middle(self):
+        a = self.saved
+
+        @pl.loop(0, 4)
+        def _(i):
+            out_block(i, a["ctx"], self.w["wout"], self.x, self.vectors, a["resid"])
+            self.total[:, cols(i, 256)] = a["resid"][:, cols(i, 256)]
+
+        norm_mid(a["resid"], self.vectors, self.normed)
+
+    def hidden(self, s):
+        @pl.loop(0, 4)
+        def _(j):
+            hidden_tile(s, j, self.normed, self.w["w1"], self.b1, self.act, self.saved["act_t"], self.saved["slope"])
+
+    def down(self, s):
+        @pl.loop(0, 4)
+        def _(i):
+            down_block(i, s, self.act, self.w["w2"], self.total)
+
+    def turn(self):
+        flip(self.saved["ctx"], self.saved["ctx_t"], D)
+        flip(self.normed, self.saved["nmid_t"], D)
+
+    def finish(self):
+        @pl.loop(0, 4)
+        def _(i):
+            finish_block(i, self.total, self.vectors, self.mask, self.out)
+
+    def stores(self, names):
+        at = list(SAVED)
+        return [
+            pltpu.make_async_copy(self.saved[a], self.saved_h[a], self.out_sem.at[at.index(a)]) for a in names
+        ]
+
+    def store_out(self):
+        return pltpu.make_async_copy(self.out, self.out_h, self.out_sem.at[len(SAVED)])
+
+    def drain_last(self, s):
+        for slot in range(2):
+            self.put(s * 2 + slot, slot).wait()
+
+    def drain(self):
+        for slot in range(2):
+            self.put(6 + slot, slot).wait()
+
+
 def forward_kernel(x_h, wqkv_h, wout_h, w1_h, w2_h, vectors, b1, mask, *rest):
     n = len(SAVED)
-    out_h, probs_h = rest[0], rest[1]
     saved_h = dict(zip(SAVED, rest[2 : 2 + n]))
-    rest = rest[2 + n :]
-    saved = dict(zip(SAVED, rest[:n]))
-    x, wqkv, wout, w1, w2, nin, nmid, act, probs, out, in_sem, probs_sem, out_sem = rest[n:]
+    x, *weights, in_sem = rest[2 + n : 8 + n]
     loads = [
         pltpu.make_async_copy(a, b, in_sem.at[i])
-        for i, (a, b) in enumerate(((x_h, x), (wqkv_h, wqkv), (wout_h, wout), (w1_h, w1), (w2_h, w2)))
+        for i, (a, b) in enumerate(zip((x_h, wqkv_h, wout_h, w1_h, w2_h), (x, *weights)))
     ]
     for c in loads:
         c.start()
-    loads[0].wait()
-    norm_in(x, vectors, nin)
-    loads[1].wait()
-    for t in range(4):
-        project(nin, wqkv, vectors, t, saved["q"], saved["k"], saved["v"])
-    flip(nin, saved["nin_t"], D)
-
-    def put(pair, slot):
-        return pltpu.make_async_copy(probs.at[slot], probs_h.at[pair], probs_sem.at[slot])
-
-    @pl.loop(0, 8)
-    def _(pair):
-        slot = pair % 2
-
-        @pl.when(pair >= 2)
-        def _():
-            put(pair - 2, slot).wait()
-
-        attend_pair(pair, saved["q"], saved["k"], saved["v"], saved["ctx"], probs, slot)
-        put(pair, slot).start()
-
-    put(6, 0).wait()
-    put(7, 1).wait()
-    loads[2].wait()
-
-    @pl.loop(0, 4)
-    def _(i):
-        out_block(i, saved["ctx"], wout, x, vectors, saved["resid"])
-
-    norm_mid(saved["resid"], vectors, nmid)
-    loads[3].wait()
-
-    @pl.loop(0, 16)
-    def _(i):
-        hidden_tile(i // 4, i % 4, nmid, w1, b1, act, saved["act_t"], saved["slope"])
-
-    flip(saved["ctx"], saved["ctx_t"], D)
-    flip(nmid, saved["nmid_t"], D)
-    loads[4].wait()
-
-    @pl.loop(0, 4)
-    def _(i):
-        down_block(i, act, w2, saved["resid"], vectors, mask, out)
-
-    stores = [pltpu.make_async_copy(out, out_h, out_sem.at[n])]
-    stores += [pltpu.make_async_copy(saved[a], saved_h[a], out_sem.at[i]) for i, a in enumerate(SAVED)]
+    for c in loads:
+        c.wait()
+    f = Forward(x, dict(zip(WEIGHTS, weights)), vectors, b1, mask, rest[0], rest[1], saved_h, rest[8 + n :])
+    f.start_norm()
+    for s in range(4):
+        f.heads(s, s)
+    f.middle()
+    for s in range(4):
+        f.hidden(s)
+        f.down(s)
+    f.turn()
+    f.finish()
+    f.drain()
+    stores = [*f.stores(SAVED), f.store_out()]
     for c in stores:
         c.start()
     for c in stores:
         c.wait()
 
 
-def forward(x, wqkv, wout, w1, w2, vectors, b1, mask):
+def forward(x, weights, vectors, b1, mask):
     n = len(SAVED)
     outs = pl.pallas_call(
         forward_kernel,
         out_shape=[IMAGE, PROBS, *SAVED.values()],
         in_specs=[ANY] * 5 + [VM, VM, VM],
         out_specs=[ANY] * (2 + n),
-        scratch_shapes=[scratch(a) for a in SAVED.values()]
-        + [scratch(a) for a in (x, wqkv, wout, w1, w2)]
-        + [
-            scratch(ACT),
-            scratch(ACT),
-            pltpu.VMEM((ROWS, 4 * D), BF16),
-            pltpu.VMEM((2, 2, ROWS, ROWS), BF16),
-            scratch(IMAGE),
-            pltpu.SemaphoreType.DMA((5,)),
-            pltpu.SemaphoreType.DMA((2,)),
-            pltpu.SemaphoreType.DMA((n + 1,)),
-        ],
+        scratch_shapes=[scratch(IMAGE)]
+        + [scratch(part(a)) for a in WEIGHTS]
+        + [pltpu.SemaphoreType.DMA((5,))]
+        + Forward.SCRATCH,
         compiler_params=pltpu.CompilerParams(vmem_limit_bytes=VMEM_BYTES),
         name="forward",
-    )(x, wqkv, wout, w1, w2, vectors, b1, mask)
+    )(x, *[weights[a] for a in WEIGHTS], vectors, b1, mask)
     return outs[0], outs[1], dict(zip(SAVED, outs[2:]))
 
 
@@ -351,9 +419,8 @@
     sums[...] = jnp.zeros_like(sums)
     load["ct"].wait()
 
-    @pl.loop(0, ROWS // STEP)
-    def _(i):
-        rows = pl.ds(pl.multiple_of(i * STEP, STEP), STEP)
+    @over_rows
+    def _(rows):
         g = jnp.concatenate([x[t, rows, :].astype(F32) * mask[...] for t in range(4)], axis=1)
         gmlp[rows, :] = g.astype(BF16)
         part[0] += fold(g)
@@ -398,9 +465,8 @@
     load_saved["resid"].wait()
     gain2 = vec(vectors, 5)
 
-    @pl.loop(0, ROWS // STEP)
-    def _(i):
-        rows = pl.ds(pl.multiple_of(i * STEP, STEP), STEP)
+    @over_rows
+    def _(rows):
         normed = gn[rows, :]
         g, scaled = grad_norm_rows(saved["resid"][rows, :], gain2, normed)
         g = g + gmlp[rows, :].astype(F32)
@@ -460,9 +526,8 @@
     load["x"].wait()
     gain1 = vec(vectors, 0)
 
-    @pl.loop(0, ROWS // STEP)
-    def _(i):
-        rows = pl.ds(pl.multiple_of(i * STEP, STEP), STEP)
+    @over_rows
+    def _(rows):
         normed = resid[rows, :]
         g, scaled = grad_norm_rows(wide(x, rows), gain1, normed)
         g = g + gn[rows, :]
@@ -514,13 +579,6 @@
 
 
 MESH = pl.DeviceIdType.MESH
-PARTS = dict(
-    sv=((4, 4, 2, 16, 256), F32),
-    wqkv=((4, 4, 2, 128, 768), BF16),
-    wout=((4, 2, 4, 256, 128), BF16),
-    w1=((4, 4, 2, 128, 1024), BF16),
-    w2=((4, 2, 4, 1024, 128), BF16),
-)
 BY_COLUMN = ("wout", "w2")
 
 
@@ -549,6 +607,10 @@
     def z_id(self, t):
         return (self.d, t)
 
+    def order(self, i):
+        t = self.t
+        return (t, t + 1 - 2 * (t % 2), 2 - t // 2, 3 - 3 * (t // 2))[i]
+
     def greet(self):
         barrier = pltpu.get_barrier_semaphore()
         others = [self.x_id, self.y_id, self.c_id]
@@ -565,31 +627,30 @@
 
 
 class Gather:
-    SENDS = 2 * 3 + 4 * 6 + 4
+    SEMS = [
+        pltpu.SemaphoreType.DMA((2, 4)),
+        pltpu.SemaphoreType.DMA((4,)),
+        pltpu.SemaphoreType.DMA((4, 6)),
+        pltpu.SemaphoreType.DMA((4, 6)),
+        pltpu.SemaphoreType.DMA((4,)),
+        pltpu.SemaphoreType.DMA((4,)),
+    ]
 
     def __init__(self, place, name, own, whole, sems):
         self.p, self.name, self.own, self.whole = place, name, own, whole
         self.z_send, self.z_recv, self.xy_send, self.xy_recv, self.c_send, self.c_recv = sems
 
-    def at(self, t, yx):
-        return block_of(self.name, self.whole, t, yx, self.p.c)
-
-    def z_copy(self, up, step):
+    def at(self, s, yx):
+        return block_of(self.name, self.whole, s, yx, self.p.c)
+
+    def z_copies(self, s, act, src=None):
         p = self.p
-        s = p.t - (step - 1) if up else p.t + (step - 1)
-        src = self.own if step == 1 else self.at(s, p.yx)
         dst = self.at(s, p.yx)
-        to = p.t + 1 if up else p.t - 1
-        return remote(src, dst, self.z_send.at[1 - up, step - 1], self.z_recv.at[s], p.z_id(to))
-
-    def z_sends(self, step, act):
-        p = self.p
-        for up in (1, 0):
-            going = (p.t < 3) & (p.t - (step - 1) >= 0) if up else (p.t > 0) & (p.t + (step - 1) <= 3)
+        for way, going, to in ((0, (s <= p.t) & (p.t < 3), p.t + 1), (1, (s >= p.t) & (p.t > 0), p.t - 1)):
 
             @pl.when(going)
             def _():
-                c = self.z_copy(up, step)
+                c = remote(dst if src is None else src, dst, self.z_send.at[way, s], self.z_recv.at[s], p.z_id(to))
                 c.start() if act == "start" else c.wait_send()
 
     def xy_copy(self, k, s, mine=False):
@@ -601,13 +662,24 @@
         src = half_of(self.own, h) if mine else dst
         return remote(src, dst, self.xy_send.at[s, k], self.xy_recv.at[s, k], to)
 
-    def first(self, s, mine=False):
+    def open(self):
+        s = self.p.t
+        self.z_copies(s, "start", self.own)
         for k in (0, 1):
-            self.xy_copy(k, s, mine).start()
-
-    def second(self, s, mine=False):
+            self.xy_copy(k, s, True).start()
+
+    def arrive(self, i):
+        s = self.p.order(i)
+        here = self.at(s, self.p.yx)
+        remote(here, here, self.z_send.at[0, s], self.z_recv.at[s], self.p.c_id).wait_recv()
+        self.z_copies(s, "start")
+        for k in (0, 1):
+            self.xy_copy(k, s).start()
+
+    def second(self, i):
+        s = self.p.order(i)
         for got, own, other in ((0, 2, 3), (1, 4, 5)):
-            self.xy_copy(own, s, mine).start()
+            self.xy_copy(own, s, i == 0).start()
             self.xy_copy(got, s).wait_recv()
             self.xy_copy(other, s).start()
 
@@ -616,66 +688,21 @@
         ref = self.whole.at[:, c, s] if self.name in BY_COLUMN else self.whole.at[s, :, c]
         return remote(ref, ref, self.c_send.at[s], self.c_recv.at[s], self.p.c_id)
 
-    def last(self, s):
+    def last(self, i):
+        s = self.p.order(i)
         for k in (2, 3, 4, 5):
             self.xy_copy(k, s).wait_recv()
         self.core_copy(s).start()
 
-    def each(self, step, do):
-        p = self.p
-        if step == 0:
-            do(p.t)
-            return
-
-        @pl.when(p.t - step >= 0)
-        def _():
-            do(p.t - step)
-
-        @pl.when(p.t + step <= 3)
-        def _():
-            do(p.t + step)
-
-    def stage(self, i):
-        if i == 0:
-            self.z_sends(1, "start")
-            self.first(self.p.t, True)
-        if 1 <= i <= 3:
-
-            def arrived(s):
-                remote(
-                    self.at(s, self.p.yx), self.at(s, self.p.yx), self.z_send.at[0, 0], self.z_recv.at[s], self.p.c_id
-                ).wait_recv()
-
-            self.each(i, arrived)
-            if i < 3:
-                self.z_sends(i + 1, "start")
-            self.each(i, self.first)
-        if 1 <= i <= 4:
-            self.each(i - 1, functools.partial(self.second, mine=i == 1))
-        if 2 <= i <= 5:
-            self.each(i - 2, self.last)
-
-    def done(self):
+    def have(self, i):
+        self.core_copy(self.p.order(i)).wait_recv()
+
+    def finish(self):
         for s in range(4):
-            self.core_copy(s).wait_recv()
-
-    def finish(self):
-        for step in (1, 2, 3):
-            self.z_sends(step, "wait")
-        for s in range(4):
+            self.z_copies(s, "wait")
             for k in range(6):
                 self.xy_copy(k, s).wait_send()
             self.core_copy(s).wait_send()
-
-
-GATHER_SEMS = [
-    pltpu.SemaphoreType.DMA((2, 3)),
-    pltpu.SemaphoreType.DMA((4,)),
-    pltpu.SemaphoreType.DMA((4, 6)),
-    pltpu.SemaphoreType.DMA((4, 6)),
-    pltpu.SemaphoreType.DMA((4,)),
-    pltpu.SemaphoreType.DMA((4,)),
-]
 
 
 class Swap:
@@ -709,75 +736,147 @@
         self.store = pltpu.make_async_copy(buf, dst, sems.at[1])
 
 
-def gather_kernel(x_in, ct_in, *rest):
-    names = list(PARTS)
-    n = len(names)
+SEQUENCE = (
+    ("sv", "O"), ("wout", "O"), ("wqkv", "O"), ("sv", "S", 0), ("wout", "A", 1), ("sv", "A", 1), ("w1", "O"),
+    ("wout", "S", 0), ("wqkv", "A", 1), ("sv", "S", 1), ("wqkv", "S", 0), ("wout", "A", 2), ("w1", "S", 0),
+    ("wout", "A", 3), ("sv", "L", 0), ("sv", "A", 2), ("sv", "A", 3), ("wqkv", "S", 1), ("w1", "A", 1),
+    ("wqkv", "A", 2), ("wqkv", "A", 3), ("XS",), ("sv", "L", 1), ("sv", "S", 2), ("w1", "S", 1),
+    ("wout", "S", 1), ("sv", "S", 3), ("wout", "S", 2), ("sv", "L", 2), ("w2", "O"), ("wout", "S", 3),
+    ("sv", "L", 3), ("wqkv", "S", 2), ("wqkv", "S", 3), ("w1", "A", 2), ("wqkv", "L", 0), ("w2", "S", 0),
+    ("LN1",), ("w1", "A", 3), ("wqkv", "L", 1), ("wqkv", "L", 2), ("wout", "L", 0), ("w1", "L", 0), ("Q", 0),
+    ("w2", "A", 1), ("wout", "L", 1), ("wout", "L", 2), ("w1", "S", 2), ("wqkv", "L", 3), ("w2", "A", 2),
+    ("Q", 1), ("Q", 2), ("w2", "A", 3), ("w1", "S", 3), ("wout", "L", 3), ("w2", "S", 1), ("w1", "L", 1),
+    ("Q", 3), ("CS",), ("OUT",), ("w1", "L", 2), ("F", 0), ("w2", "S", 2), ("w2", "S", 3), ("w2", "L", 0),
+    ("F", 1), ("w1", "L", 3), ("w2", "L", 1), ("F", 2), ("F", 3), ("D", 0), ("w2", "L", 2), ("D", 1),
+    ("w2", "L", 3), ("D", 2), ("D", 3), ("END",),
+)
+
+
+def spread_kernel(x_in, ct_in, mask, *rest):
+    names, n, m = list(PARTS), len(PARTS), len(SAVED)
     own = dict(zip(names, rest[:n]))
-    x, ct = rest[n : n + 2]
-    whole = dict(zip(names, rest[n + 2 : 2 * n + 2]))
-    rest = rest[2 * n + 2 :]
-    bufs, (x_buf, ct_buf) = dict(zip(names, rest[:n])), rest[n : n + 2]
-    rest = rest[n + 2 :]
-    local_sem, swap_sems, sems = rest[0], rest[1:5], rest[5:]
-    place = Place()
-    gathers = [
-        Gather(place, a, own[a], whole[a], sems[6 * i : 6 * i + 6]) for i, a in enumerate(names)
-    ]
-    swaps = [Swap(place, x_in, x, swap_sems[0:2]), Swap(place, ct_in, ct, swap_sems[2:4])]
+    x_h, ct_h, out_h, probs_h, vectors = rest[n : n + 5]
+    rest = rest[n + 5 :]
+    whole_h, saved_h = dict(zip(WEIGHTS, rest[:4])), dict(zip(SAVED, rest[4 : 4 + m]))
+    rest = rest[4 + m :]
+    x, ct, b1 = rest[:3]
+    whole = dict(zip(names, rest[3 : 3 + n]))
+    rest = rest[3 + n :]
+    local_sem, keep_sem = rest[0], rest[1]
+    swap_sems, rest = rest[2:6], rest[6:]
+    sems, refs = rest[: 6 * n], rest[6 * n :]
+    p = Place()
+    f = Forward(x, whole, vectors, b1, mask, out_h, probs_h, saved_h, refs)
+    gathers = {a: Gather(p, a, own[a], whole[a], sems[6 * i : 6 * i + 6]) for i, a in enumerate(names)}
+    swaps = dict(XS=Swap(p, x_in, x, swap_sems[0:2]), CS=Swap(p, ct_in, ct, swap_sems[2:4]))
     local = [
-        Bounce(own[a], bufs[a], block_of(a, whole[a], place.t, place.yx, place.c), local_sem.at[i])
+        pltpu.make_async_copy(own[a], block_of(a, whole[a], p.t, p.yx, p.c), local_sem.at[i])
         for i, a in enumerate(names)
     ]
     local += [
-        Bounce(x_in.at[place.t], x_buf, x.at[place.t], local_sem.at[n]),
-        Bounce(ct_in.at[place.t], ct_buf, ct.at[place.t], local_sem.at[n + 1]),
+        pltpu.make_async_copy(x_in.at[p.t], x.at[p.t], local_sem.at[n]),
+        pltpu.make_async_copy(ct_in.at[p.t], ct.at[p.t], local_sem.at[n + 1]),
     ]
-    for b in local:
-        b.load.start()
-    place.greet()
-    for b in local:
-        b.load.wait()
-        b.store.start()
-    swaps[0].start()
-    stored = False
-    for tick in range(n + 5):
-        for i, g in enumerate(gathers):
-            if tick - i == 2 and not stored:
-                for b in local:
-                    b.store.wait()
-                stored = True
-            if 0 <= tick - i <= 5:
-                g.stage(tick - i)
-        if tick == 3:
-            swaps[1].start()
-    for g in gathers:
-        g.done()
-    for s in swaps:
-        s.done()
+    for c in local:
+        c.start()
+    p.greet()
+    pending = []
+    settled = False
+
+    def keep(src, dst):
+        c = pltpu.make_async_copy(src, dst, keep_sem.at[len(pending)])
+        c.start()
+        pending.append(c)
+
+    for name, *step in SEQUENCE:
+        if name in gathers:
+            g, kind = gathers[name], step[0]
+            if kind == "O":
+                g.open()
+            elif kind == "A":
+                g.arrive(step[1])
+            elif kind == "S":
+                g.second(step[1])
+            else:
+                if not settled:
+                    for c in local:
+                        c.wait()
+                    settled = True
+                g.last(step[1])
+        elif name in swaps:
+            swaps[name].start()
+        elif name == "LN1":
+            for i in range(4):
+                gathers["sv"].have(i)
+            sv = whole["sv"]
+            for t in range(4):
+                vectors[t] = jnp.sum(sv[t, :, :, 0:8].reshape(8, 8, 256), axis=0)
+                for d in range(8):
+                    b1[t, :, d * 128 : d * 128 + 128] = sv[t, d // 2, d % 2, 8:9, 0:128]
+            swaps["XS"].done()
+            keep(x, x_h)
+            f.start_norm()
+        elif name == "Q":
+            gathers["wqkv"].have(step[0])
+            f.heads(p.order(step[0]), step[0])
+        elif name == "OUT":
+            for i in range(4):
+                gathers["wout"].have(i)
+            keep(whole["wqkv"], whole_h["wqkv"])
+            keep(whole["wout"], whole_h["wout"])
+            f.middle()
+            for c in f.stores(("q", "k", "v", "ctx", "nin_t", "resid")):
+                c.start()
+        elif name == "F":
+            gathers["w1"].have(step[0])
+            f.hidden(p.order(step[0]))
+        elif name == "D":
+            if step[0] == 0:
+                keep(whole["w1"], whole_h["w1"])
+                for c in f.stores(("act_t", "slope")):
+                    c.start()
+            gathers["w2"].have(step[0])
+            f.down(p.order(step[0]))
+        elif name == "END":
+            keep(whole["w2"], whole_h["w2"])
+            f.finish()
+            f.store_out().start()
+            swaps["CS"].done()
+            keep(ct, ct_h)
+            f.turn()
+            for c in f.stores(("ctx_t", "nmid_t")):
+                c.start()
+    f.drain_last(p.order(3))
+    for c in [*pending, *f.stores(SAVED), f.store_out()]:
+        c.wait()
+    for s in swaps.values():
         s.finish()
-    for g in gathers:
+    for g in gathers.values():
         g.finish()
 
 
-def gather(x_in, ct_in, own):
-    names = list(PARTS)
-    n = len(names)
+def spread(x_in, ct_in, mask, own):
+    names, n, m = list(PARTS), len(PARTS), len(SAVED)
     outs = pl.pallas_call(
-        gather_kernel,
-        out_shape=[IMAGE, IMAGE] + [jax.ShapeDtypeStruct(*PARTS[a]) for a in names],
-        in_specs=[ANY] * (n + 2),
-        out_specs=[ANY] * (n + 2),
-        scratch_shapes=[pltpu.VMEM(PARTS[a][0][3:], PARTS[a][1]) for a in names]
-        + [pltpu.VMEM((ROWS, 256), BF16)] * 2
-        + [pltpu.SemaphoreType.DMA((n + 2, 2))]
+        spread_kernel,
+        out_shape=[IMAGE, IMAGE, IMAGE, PROBS, jax.ShapeDtypeStruct((4, 8, 256), F32)]
+        + [part(a) for a in WEIGHTS]
+        + list(SAVED.values()),
+        in_specs=[ANY, ANY, VM] + [ANY] * n,
+        out_specs=[ANY] * 4 + [VM] + [ANY] * (4 + m),
+        scratch_shapes=[scratch(IMAGE), scratch(IMAGE), pltpu.VMEM((4, 1, 1024), F32)]
+        + [scratch(part(a)) for a in names]
+        + [pltpu.SemaphoreType.DMA((n + 2,)), pltpu.SemaphoreType.DMA((6,))]
         + Swap.SEMS * 2
-        + GATHER_SEMS * n,
+        + Gather.SEMS * n
+        + Forward.SCRATCH,
         compiler_params=pltpu.CompilerParams(
             collective_id=0, has_side_effects=True, vmem_limit_bytes=VMEM_BYTES
         ),
-        name="gather",
-    )(x_in, ct_in, *[own[a] for a in names])
-    return outs[0], outs[1], dict(zip(names, outs[2:]))
+        name="spread",
+    )(x_in, ct_in, mask, *[own[a] for a in names])
+    x, ct, out, probs, vectors = outs[:5]
+    return x, ct, out, probs, vectors, dict(zip(WEIGHTS, outs[5:9])), dict(zip(SAVED, outs[9:]))
 
 
 REDUCED = ("w2", "w1", "wout", "wqkv")
@@ -1090,10 +1189,7 @@
             w1=w_fc1.astype(BF16),
             w2=w_fc2.astype(BF16),
         )
-        x, ct, whole = gather(images(tokens_in), images(cotangent), own)
-        vectors = jnp.sum(whole["sv"][:, :, :, 0:8], axis=(1, 2))
-        hidden_bias = whole["sv"][:, :, :, 8, 0:128].reshape(4, 1, 1024)
-        weights = [whole[a].reshape(GRADS[a].shape) for a in GRADS]
+        x, ct, out, probs, vectors, weights, saved = spread(images(tokens_in), images(cotangent), mask, own)
     else:
         vectors = lax.all_gather(
             lax.all_gather(small, "dp", axis=1, tiled=True), "tensor", axis=0
@@ -1103,9 +1199,11 @@
         ).astype(F32)
         x = exchange(images(tokens_in))
         ct = exchange(images(cotangent))
-        weights = gather_plain(w_qkv, w_out, w_fc1, w_fc2)
-    out, probs, saved = forward(x, *weights, vectors, hidden_bias, mask)
-    gtok, sums, grads = backward(x, ct, *weights, vectors, mask, probs, saved)
+        plain = gather_plain(w_qkv, w_out, w_fc1, w_fc2)
+        weights = {a: b.reshape(PARTS[a][0]) for a, b in zip(WEIGHTS, plain)}
+        out, probs, saved = forward(x, weights, vectors, hidden_bias, mask)
+    flat = [weights[a].reshape(GRADS[a].shape) for a in GRADS]
+    gtok, sums, grads = backward(x, ct, *flat, vectors, mask, probs, saved)
     if dp == 8:
         out, gtok, sums, got = reduce(out, gtok, jnp.pad(sums, ((0, 4), (0, 0))), grads)
         g_qkv, g_out, g_fc1, g_fc2 = (got[a] for a in GRADS)

time: 470 us -> 379 us (0.81)
  Pallas kernels: 443 us -> 348 us
    pallas_call x2 -> x1, Pallas kernels: 206 us -> 121 us  [spread(): pl.pallas_call(spread_kernel, out_shape=[IMAGE, IMAGE, IMAGE, PROBS, jax....]
    pallas_call x1, Pallas kernels: 98.7 us -> 89 us  [backward(): pl.pallas_call(backward_kernel, out_shape=[IMAGE, jax.ShapeDtypeStruct((1...]
where the time goes in v3:
time: 379 us; the launch traced here: 378 us
  Pallas kernels  348 us (92%)
  local copies, waits for them, and re-layouts  20.5 us (5%)
  other arithmetic  8.3 us (2%)
    pallas_call x1, Pallas kernels, reduce(): pl.pallas_call(reduce_kernel, out_shape=[IMAGE, IMAGE, jax.ShapeDtypeStru...  138 us
    pallas_call x1, Pallas kernels, spread(): pl.pallas_call(spread_kernel, out_shape=[IMAGE, IMAGE, IMAGE, PROBS, jax....  121 us
    pallas_call x1, Pallas kernels, backward(): pl.pallas_call(backward_kernel, out_shape=[IMAGE, jax.ShapeDtypeStruct((1...  89 us

profile of v3, /device:TPU:10, one launch (start us, length us, event | category | flops | bytes accessed | tf_op | source)
XLA Modules:
  0.0 378.5 jit_solution(12752777379868462208)
XLA Ops:
  0.6 0.0 copy-start.4
  0.7 0.0 copy-start.3
  0.7 1.3 dynamic_slice.10
  2.7 0.6 broadcast_in_dim.11.mask
  3.2 0.7 convert.26
  3.9 0.7 convert.27
  4.5 0.7 convert.29
  5.2 0.7 convert.30
  5.8 0.7 convert.31
  6.5 0.7 convert_convert_fusion
  7.2 0.7 convert.32
  7.8 0.7 convert.28
  8.6 0.7 dynamic_update_slice.3
  9.2 0.2 scatter.4.rest_0_
  9.5 0.0 copy-start.9
  9.5 1.5 convert_element_type.43.rest_2_
  11.0 0.0 copy-start
  11.0 1.2 copy.32
  12.3 0.8 copy.33.rest_1_
  13.1 0.0 copy-done.3
  13.1 0.7 convert_element_type.44.rest_3_
  13.9 0.0 copy-done.4
  13.9 0.7 convert_element_type.45.rest_4_
  14.6 0.0 copy-done.9
  14.6 0.0 copy-done
  14.6 0.3 reshape.101
  14.9 0.0 copy-start.1
  14.9 1.1 pad.14.x_in
  16.1 0.6 copy-done.1
  16.6 0.3 reshape.102
  16.9 1.1 pad.15.ct_in
  18.1 121.0 %spread.1 = (bf16[4,592,256]{2,1,0:T(8,128)(2,1)}, bf16[4,592,256]{2,1,0:T(8,128)(2,1)}, bf16[4,592,256]{2,1,0:T(8,128)(2,1)}, bf16[8,2,592,592]{3,2,1,0:T(8,128...) custom-call(bf16[4,592,256]{2,1,0:T(8,128)(2,1)} %pad.14.x_in, ...), custom_call_target="tpu_custom_call" | custom-call | tf_op jit(solution)/shard_map/spread/pallas_call | solution.py:860
  139.1 89.0 %backward.1 = (bf16[4,592,256]{2,1,0:T(8,128)(2,1)}, f32[12,1024]{1,0:T(8,128)}, bf16[4,1024,768]{2,1,0:T(8,128)(2,1)}, bf16[8,1024,128]{2,1,0:T(8,128)(2,1)}, b...) custom-call(bf16[4,592,256]{2,1,0:T(8,128)(2,1)} %get-tuple-element.59.x_h, ...), custom_call_target="tpu_custom_call" | custom-call | tf_op jit(solution)/shard_map/backward/pallas_call | solution.py:552
  228.1 1.5 pad.16.sums_in
  229.6 138.2 %reduce.3 = (bf16[4,592,256]{2,1,0:T(8,128)(2,1)}, bf16[4,592,256]{2,1,0:T(8,128)(2,1)}, f32[16,1024]{1,0:T(8,128)}, f32[1024,128]{1,0:T(8,128)}, f32[128,1024]{...) custom-call(bf16[4,592,256]{2,1,0:T(8,128)(2,1)} %get-tuple-element.58.out_in, ...), custom_call_target="tpu_custom_call" | custom-call | tf_op jit(solution)/shard_map/reduce/pallas_call | solution.py:1101
  367.8 1.3 dynamic_slice.12
  369.0 1.4 slice.56
  370.4 0.0 copy-start.7
  370.4 1.3 reshape.111
  371.7 0.0 copy-start.2
  371.7 0.8 constant_dynamic-slice_fusion
  372.6 0.6 slice.60
  373.1 0.5 fusion
  373.7 0.0 copy-done.7
  373.7 0.2 copy.34
  373.9 0.9 copy.35
  374.8 0.0 copy-done.2
  374.8 0.1 slice.57
  374.9 0.0 copy-start.8
  374.9 0.0 copy-start.6
  374.9 1.3 reshape.112
  376.2 0.0 copy-done.8
  376.2 0.0 copy-start.5
  376.2 0.7 copy.42
  376.9 0.0 copy-done.6
  376.9 0.8 copy.43
  377.7 0.0 copy-done.5
  377.7 0.8 copy.44
  (4 shorter events, 0.0 us)
Async XLA Ops:
  0.6 13.2 %copy-start.4 = (f32[1024,128]{1,0:T(8,128)S(1)}, f32[1024,128]{1,0:T(8,128)}, u32[]{:S(2)}) copy-start(f32[1024,128]{1,0:T(8,128)} %param.30) | copy-start | bytes 1572868
  0.7 12.5 %copy-start.3 = (f32[128,1024]{1,0:T(8,128)S(1)}, f32[128,1024]{1,0:T(8,128)}, u32[]{:S(2)}) copy-start(f32[128,1024]{1,0:T(8,128)} %param.28) | copy-start | bytes 1572868
  9.5 5.1 %copy-start.9 = (f32[16,256]{1,0:T(8,128)}, f32[16,256]{1,0:T(8,128)S(1)}, u32[]{:S(2)}) copy-start(f32[16,256]{1,0:T(8,128)S(1)} %scatter.4.rest_0_) | copy-start | bytes 49156
  11.0 3.6 copy-start
  14.9 1.7 copy-start.1
  370.4 3.3 copy-start.7
  371.7 3.0 copy-start.2
  374.9 1.3 copy-start.8
  374.9 2.0 copy-start.6
  376.2 1.5 copy-start.5

commit v4 on v3

--- a/solution.py
+++ b/solution.py
@@ -14,11 +14,15 @@
 F32 = jnp.float32
 BF16 = jnp.bfloat16
 LAST = (((1,), (1,)), ((), ()))
-VMEM_BYTES = 66_000_000
+VMEM_BYTES = 67_043_328
 
 
 def mm(a, b):
     return jnp.dot(a, b, preferred_element_type=F32)
+
+
+def t_mm(a, b):
+    return lax.dot_general(a, b, (((0,), (0,)), ((), ())), preferred_element_type=F32)
 
 
 def mm_t(a, b):
@@ -65,18 +69,22 @@
 def flip(src, dst, n):
     @pl.loop(0, n // 256)
     def _(i):
-        dst[cols(i, 256), :] = src[:, cols(i, 256)].T
+        dst[i] = src[:, cols(i, 256)].T.reshape(2, 128, ROWS)
 
 
 def project(nin, wqkv, vectors, t, q, k, v):
     here = cols(t, 256)
 
-    def part(c):
-        return mm(nin[...], wqkv[t, :, :, :, c * 256 : c * 256 + 256].reshape(D, 256))
-
-    q[:, here] = (part(0) + vectors[t, 2:3, :]).astype(BF16)
-    k[:, here] = part(1).astype(BF16)
-    v[:, here] = (part(2) + vectors[t, 3:4, :]).astype(BF16)
+    g = mm(nin[...], wqkv[t].reshape(D, 768))
+    q[:, here] = (g[:, 0:256] + vectors[t, 2:3, :]).astype(BF16)
+    k[:, here] = g[:, 256:512].astype(BF16)
+    v[:, here] = (g[:, 512:768] + vectors[t, 3:4, :]).astype(BF16)
+
+
+def head_lanes(h):
+    lane = lax.broadcasted_iota(jnp.int32, (ROWS, 128), 1)
+    own = (lane >= h * 64) & (lane < h * 64 + 64)
+    return lane, own, 64 - h * 64
 
 
 def attend_pair(pair, q, k, v, ctx, probs, slot):
@@ -119,16 +127,14 @@
         nmid[rows, :] = (xhat * gain + shift).astype(BF16)
 
 
-def hidden_tile(t, j, nmid, w1, b1, act, act_t, slope):
+def hidden_tile(t, j, nmid, w1, b1, act, slope):
     here = pl.ds(pl.multiple_of(t * 1024 + j * 256, 256), 256)
     bias = b1[t, :, cols(j, 256)]
     pre = mm(nmid[...], w1[t, :, :, :, cols(j, 256)].reshape(D, 256)) + bias
     sig = 1.0 / (1.0 + jnp.exp(-1.702 * pre))
     a = pre * sig
     slope[:, here] = (sig + 1.702 * a * (1.0 - sig)).astype(BF16)
-    low = a.astype(BF16)
-    act[:, here] = low
-    act_t[here, :] = low.T
+    act[:, here] = a.astype(BF16)
 
 
 def down_block(i, t, act, w2, total):
@@ -152,48 +158,37 @@
     return jnp.sum(a.reshape(-1, 8, D), axis=0)
 
 
-def attend_back_pair(pair, q, k, v, ctx, gctx, probs, slot, gmix, sums):
-    here = cols(pair, 128)
-    lane = lax.broadcasted_iota(jnp.int32, (ROWS, 128), 1)
-    queries, keys, values = q[:, here], k[:, here], v[:, here].astype(F32)
-    go = gctx[:, here]
-    go_f = go.astype(F32)
-    dots = go_f * ctx[:, here].astype(F32)
+def attend_back_pair(queries, keys, values, out, go, probs):
+    values_f, go_f = values.astype(F32), go.astype(F32)
+    dots = go_f * out.astype(F32)
     dq, dk, dv = [], [], []
     for h in range(2):
-        own = (lane < 64) if h == 0 else (lane >= 64)
-        spare = 64 if h == 0 else 0
+        lane, own, spare = head_lanes(h)
         delta = -jnp.sum(jnp.where(own, dots, 0.0), axis=1, keepdims=True)
         high = delta.astype(BF16).astype(F32)
-        rest = delta - high
         ga = jnp.where(
-            own, go_f, jnp.where(lane == spare, high, jnp.where(lane == spare + 1, rest, 0.0))
+            own, go_f, jnp.where(lane == spare, high, jnp.where(lane == spare + 1, delta - high, 0.0))
         ).astype(BF16)
         marks = jnp.where((lane == spare) | (lane == spare + 1), 1.0, 0.0)
-        va = jnp.where(own, values, marks).astype(BF16)
-        p = probs[slot, h]
+        va = jnp.where(own, values_f, marks).astype(BF16)
+        p = probs[h]
         gs = (p.astype(F32) * mm_t(va, ga)).astype(BF16)
         dv.append(mm(p, go))
         dk.append(mm(gs, queries))
         dq.append(
             lax.dot_general(gs, keys, (((0,), (0,)), ((), ())), preferred_element_type=F32)
         )
+    low = head_lanes(0)[1]
     scale = HD**-0.5
-    low = lane < 64
-    gq = jnp.where(low, dq[0], dq[1]) * scale
-    gk = jnp.where(low, dk[0], dk[1]) * scale
-    gv = jnp.where(low, dv[0], dv[1])
-    t, half = pair // 2, pair % 2
-    at = [pl.ds(pl.multiple_of(c * 256 + half * 128, 128), 128) for c in range(3)]
-    gmix[t, :, at[0]] = gq.astype(BF16)
-    gmix[t, :, at[1]] = gk.astype(BF16)
-    gmix[t, :, at[2]] = gv.astype(BF16)
-    sums[2:3, here] = jnp.sum(gq, axis=0, keepdims=True)
-    sums[3:4, here] = jnp.sum(gv, axis=0, keepdims=True)
+    return (
+        jnp.where(low, dq[0], dq[1]) * scale,
+        jnp.where(low, dk[0], dk[1]) * scale,
+        jnp.where(low, dv[0], dv[1]),
+    )
 
 
 ACT = jax.ShapeDtypeStruct((ROWS, D), BF16)
-TURNED = jax.ShapeDtypeStruct((D, ROWS), BF16)
+TURNED = jax.ShapeDtypeStruct((4, 2, 128, ROWS), BF16)
 SAVED = dict(
     nin_t=TURNED,
     q=ACT,
@@ -203,7 +198,7 @@
     ctx_t=TURNED,
     nmid_t=TURNED,
     resid=jax.ShapeDtypeStruct((ROWS, D), F32),
-    act_t=jax.ShapeDtypeStruct((4 * D, ROWS), BF16),
+    act=jax.ShapeDtypeStruct((ROWS, 4 * D), BF16),
     slope=jax.ShapeDtypeStruct((ROWS, 4 * D), BF16),
 )
 PROBS = jax.ShapeDtypeStruct((8, 2, ROWS, ROWS), BF16)
@@ -233,20 +228,19 @@
 class Forward:
     SCRATCH = [scratch(a) for a in SAVED.values()] + [
         scratch(ACT),
-        pltpu.VMEM((ROWS, 4 * D), BF16),
-        pltpu.VMEM((ROWS, D), F32),
         pltpu.VMEM((2, 2, ROWS, ROWS), BF16),
-        scratch(IMAGE),
         pltpu.SemaphoreType.DMA((2,)),
         pltpu.SemaphoreType.DMA((len(SAVED) + 1,)),
     ]
 
-    def __init__(self, x, weights, vectors, b1, mask, out_h, probs_h, saved_h, refs):
+    def __init__(self, x, weights, vectors, b1, mask, out, out_h, probs_h, saved_h, refs):
         n = len(SAVED)
         self.x, self.w, self.vectors, self.b1, self.mask = x, weights, vectors, b1, mask
-        self.out_h, self.probs_h, self.saved_h = out_h, probs_h, saved_h
+        self.out, self.out_h, self.probs_h, self.saved_h = out, out_h, probs_h, saved_h
         self.saved = dict(zip(SAVED, refs[:n]))
-        self.normed, self.act, self.total, self.probs, self.out, self.probs_sem, self.out_sem = refs[n:]
+        self.total = self.saved["resid"]
+        self.normed, self.probs, self.probs_sem, self.out_sem = refs[n:]
+        self.act = self.saved["act"]
 
     def start_norm(self):
         norm_in(self.x, self.vectors, self.normed)
@@ -273,14 +267,13 @@
         @pl.loop(0, 4)
         def _(i):
             out_block(i, a["ctx"], self.w["wout"], self.x, self.vectors, a["resid"])
-            self.total[:, cols(i, 256)] = a["resid"][:, cols(i, 256)]
 
         norm_mid(a["resid"], self.vectors, self.normed)
 
     def hidden(self, s):
         @pl.loop(0, 4)
         def _(j):
-            hidden_tile(s, j, self.normed, self.w["w1"], self.b1, self.act, self.saved["act_t"], self.saved["slope"])
+            hidden_tile(s, j, self.normed, self.w["w1"], self.b1, self.act, self.saved["slope"])
 
     def down(self, s):
         @pl.loop(0, 4)
@@ -317,7 +310,7 @@
 def forward_kernel(x_h, wqkv_h, wout_h, w1_h, w2_h, vectors, b1, mask, *rest):
     n = len(SAVED)
     saved_h = dict(zip(SAVED, rest[2 : 2 + n]))
-    x, *weights, in_sem = rest[2 + n : 8 + n]
+    x, out, *weights, in_sem = rest[2 + n : 9 + n]
     loads = [
         pltpu.make_async_copy(a, b, in_sem.at[i])
         for i, (a, b) in enumerate(zip((x_h, wqkv_h, wout_h, w1_h, w2_h), (x, *weights)))
@@ -326,18 +319,21 @@
         c.start()
     for c in loads:
         c.wait()
-    f = Forward(x, dict(zip(WEIGHTS, weights)), vectors, b1, mask, rest[0], rest[1], saved_h, rest[8 + n :])
+    f = Forward(x, dict(zip(WEIGHTS, weights)), vectors, b1, mask, out, rest[0], rest[1], saved_h, rest[9 + n :])
     f.start_norm()
     for s in range(4):
         f.heads(s, s)
     f.middle()
+    for c in f.stores(("resid",)):
+        c.start()
+        c.wait()
     for s in range(4):
         f.hidden(s)
         f.down(s)
     f.turn()
     f.finish()
     f.drain()
-    stores = [*f.stores(SAVED), f.store_out()]
+    stores = [*f.stores([a for a in SAVED if a != "resid"]), f.store_out()]
     for c in stores:
         c.start()
     for c in stores:
@@ -351,7 +347,7 @@
         out_shape=[IMAGE, PROBS, *SAVED.values()],
         in_specs=[ANY] * 5 + [VM, VM, VM],
         out_specs=[ANY] * (2 + n),
-        scratch_shapes=[scratch(IMAGE)]
+        scratch_shapes=[scratch(IMAGE), scratch(IMAGE)]
         + [scratch(part(a)) for a in WEIGHTS]
         + [pltpu.SemaphoreType.DMA((5,))]
         + Forward.SCRATCH,
@@ -408,12 +404,12 @@
     load = {a: pltpu.make_async_copy(*names[a], in_sem.at[i]) for i, a in enumerate(names)}
     load_saved = {a: pltpu.make_async_copy(saved_h[a], saved[a], saved_sem.at[i]) for i, a in enumerate(SAVED)}
     load["ct"].start()
-    for a in ("act_t", "slope"):
-        load_saved[a].start()
+    load_saved["act"].start()
+    load_saved["slope"].start()
     for a in ("w2", "w1", "wout", "wqkv"):
         load[a].start()
     for a in SAVED:
-        if a not in ("act_t", "slope"):
+        if a not in ("act", "slope"):
             load_saved[a].start()
     part[...] = jnp.zeros_like(part)
     sums[...] = jnp.zeros_like(sums)
@@ -426,12 +422,12 @@
         part[0] += fold(g)
 
     load["x"].start()
-    load_saved["act_t"].wait()
+    load_saved["act"].wait()
 
     @pl.loop(0, 16)
     def _(i):
         t, c = i // 4, i % 4
-        r = mm(saved["act_t"][cols(t, 1024), :], gmlp[:, cols(c, 256)]).astype(BF16)
+        r = t_mm(saved["act"][:, cols(t, 1024)], gmlp[:, cols(c, 256)]).astype(BF16)
         send_tile(stage, tile_sem, i, r, [
             (g_h["w2"].at[2 * c + e, cols(t, 1024), :], e * 128, 128) for e in range(2)])
 
@@ -450,7 +446,7 @@
 
     @pl.loop(0, 16)
     def _(i):
-        r = mm(saved["nmid_t"][...], slope[:, cols(i, 256)]).astype(BF16)
+        r = mm(saved["nmid_t"][...].reshape(D, ROWS), slope[:, cols(i, 256)]).astype(BF16)
         send_tile(stage, tile_sem, i + 16, r, [(g_h["w1"].at[i // 4, :, cols(i % 4, 256)], 0, 256)])
 
     load["w1"].wait()
@@ -483,7 +479,7 @@
     def _(i):
         w = jnp.concatenate([wout[d, cols(i, 256), :] for d in range(8)], axis=1)
         gctx[:, cols(i, 256)] = mm_t(gattn[...], w).astype(BF16)
-        r = mm(saved["ctx_t"][...], gattn[:, cols(i, 256)]).astype(BF16)
+        r = mm(saved["ctx_t"][...].reshape(D, ROWS), gattn[:, cols(i, 256)]).astype(BF16)
         send_tile(stage, tile_sem, i + 32, r, [(g_h["wout"].at[2 * i + e], e * 128, 128) for e in range(2)])
 
     for a in ("q", "k", "v", "ctx"):
@@ -503,14 +499,23 @@
             get(pair + 1, 1 - slot).start()
 
         get(pair, slot).wait()
-        attend_back_pair(pair, saved["q"], saved["k"], saved["v"], saved["ctx"], gctx, probs, slot, gmix, sums)
+        here = cols(pair, 128)
+
+        got = attend_back_pair(
+            *(saved[a][:, here] for a in ("q", "k", "v", "ctx")), gctx[:, here], probs.at[slot]
+        )
+        for c in range(3):
+            at = pl.ds(pl.multiple_of(c * 256 + (pair % 2) * 128, 128), 128)
+            gmix[pair // 2, :, at] = got[c].astype(BF16)
+        sums[2:3, here] = jnp.sum(got[0], axis=0, keepdims=True)
+        sums[3:4, here] = jnp.sum(got[2], axis=0, keepdims=True)
 
     load_saved["nin_t"].wait()
 
     @pl.loop(0, 12)
     def _(i):
         t, c = i // 3, i % 3
-        r = mm(saved["nin_t"][...], gmix[t, :, cols(c, 256)]).astype(BF16)
+        r = mm(saved["nin_t"][...].reshape(D, ROWS), gmix[t, :, cols(c, 256)]).astype(BF16)
         send_tile(stage, tile_sem, i + 36, r, [(g_h["wqkv"].at[t, :, cols(c, 256)], 0, 256)])
 
     load["wqkv"].wait()
@@ -609,7 +614,11 @@
 
     def order(self, i):
         t = self.t
-        return (t, t + 1 - 2 * (t % 2), 2 - t // 2, 3 - 3 * (t // 2))[i]
+        near, far = (t, t + 1 - 2 * (t % 2)), (2 - t // 2, 3 - 3 * (t // 2))
+        if isinstance(i, int):
+            return (near + far)[i]
+        half, odd = i // 2, i % 2
+        return (1 - half) * (near[0] + odd * (near[1] - near[0])) + half * (far[0] + odd * (far[1] - far[0]))
 
     def greet(self):
         barrier = pltpu.get_barrier_semaphore()
@@ -662,9 +671,19 @@
         src = half_of(self.own, h) if mine else dst
         return remote(src, dst, self.xy_send.at[s, k], self.xy_recv.at[s, k], to)
 
+    def straight(self, k):
+        p = self.p
+        return remote(
+            self.own, self.at(p.t, p.yx), self.z_send.at[0, k], self.z_recv.at[p.t], p.z_id(lax.rem(p.t + k, 4))
+        )
+
     def open(self):
         s = self.p.t
-        self.z_copies(s, "start", self.own)
+        if self.name == "sv":
+            for k in (1, 2, 3):
+                self.straight(k).start()
+        else:
+            self.z_copies(s, "start", self.own)
         for k in (0, 1):
             self.xy_copy(k, s, True).start()
 
@@ -672,14 +691,15 @@
         s = self.p.order(i)
         here = self.at(s, self.p.yx)
         remote(here, here, self.z_send.at[0, s], self.z_recv.at[s], self.p.c_id).wait_recv()
-        self.z_copies(s, "start")
+        if self.name != "sv":
+            self.z_copies(s, "start")
         for k in (0, 1):
             self.xy_copy(k, s).start()
 
     def second(self, i):
         s = self.p.order(i)
         for got, own, other in ((0, 2, 3), (1, 4, 5)):
-            self.xy_copy(own, s, i == 0).start()
+            self.xy_copy(own, s, isinstance(i, int) and i == 0).start()
             self.xy_copy(got, s).wait_recv()
             self.xy_copy(other, s).start()
 
@@ -699,7 +719,10 @@
 
     def finish(self):
         for s in range(4):
-            self.z_copies(s, "wait")
+            if self.name != "sv":
+                self.z_copies(s, "wait")
+            elif s:
+                self.straight(s).wait_send()
             for k in range(6):
                 self.xy_copy(k, s).wait_send()
             self.core_copy(s).wait_send()
@@ -730,25 +753,40 @@
             self.copy(k).wait_send()
 
 
-class Bounce:
-    def __init__(self, src, buf, dst, sems):
-        self.load = pltpu.make_async_copy(src, buf, sems.at[0])
-        self.store = pltpu.make_async_copy(buf, dst, sems.at[1])
-
-
+class Mail:
+    def __init__(self, place, buf, sem):
+        self.p, self.buf, self.sem, self.depth = place, buf, sem, buf.shape[0]
+
+    def copy(self, slot, dst, recv):
+        return remote(self.buf.at[slot], dst, self.sem.at[slot], recv, self.p.c_id)
+
+    def post(self, i, parts, dst, recv):
+        slot = lax.rem(i, self.depth)
+
+        @pl.when(i >= self.depth)
+        def _():
+            self.copy(slot, dst, recv).wait_send()
+
+        for k, part in enumerate(parts):
+            self.buf[slot, k] = part
+        self.copy(slot, dst, recv).start()
+
+    def finish(self):
+        for slot in range(self.depth):
+            self.copy(slot, self.buf.at[slot], self.sem.at[slot]).wait_send()
+
+
+def column_pair(ref, q, c):
+    return jnp.concatenate([ref[:, cols(q * 4 + c, 128)], ref[:, cols(q * 4 + 2 + c, 128)]], axis=1)
+
+
+ACTS = ("sv", "wqkv", "wout", "w1", "w2", "XS", "CS", "LN1", "Q", "OUT", "F", "D", "END", "K1")
+KINDS = ("", "O", "A", "S", "L")
 SEQUENCE = (
-    ("sv", "O"), ("wout", "O"), ("wqkv", "O"), ("sv", "S", 0), ("wout", "A", 1), ("sv", "A", 1), ("w1", "O"),
-    ("wout", "S", 0), ("wqkv", "A", 1), ("sv", "S", 1), ("wqkv", "S", 0), ("wout", "A", 2), ("w1", "S", 0),
-    ("wout", "A", 3), ("sv", "L", 0), ("sv", "A", 2), ("sv", "A", 3), ("wqkv", "S", 1), ("w1", "A", 1),
-    ("wqkv", "A", 2), ("wqkv", "A", 3), ("XS",), ("sv", "L", 1), ("sv", "S", 2), ("w1", "S", 1),
-    ("wout", "S", 1), ("sv", "S", 3), ("wout", "S", 2), ("sv", "L", 2), ("w2", "O"), ("wout", "S", 3),
-    ("sv", "L", 3), ("wqkv", "S", 2), ("wqkv", "S", 3), ("w1", "A", 2), ("wqkv", "L", 0), ("w2", "S", 0),
-    ("LN1",), ("w1", "A", 3), ("wqkv", "L", 1), ("wqkv", "L", 2), ("wout", "L", 0), ("w1", "L", 0), ("Q", 0),
-    ("w2", "A", 1), ("wout", "L", 1), ("wout", "L", 2), ("w1", "S", 2), ("wqkv", "L", 3), ("w2", "A", 2),
-    ("Q", 1), ("Q", 2), ("w2", "A", 3), ("w1", "S", 3), ("wout", "L", 3), ("w2", "S", 1), ("w1", "L", 1),
-    ("Q", 3), ("CS",), ("OUT",), ("w1", "L", 2), ("F", 0), ("w2", "S", 2), ("w2", "S", 3), ("w2", "L", 0),
-    ("F", 1), ("w1", "L", 3), ("w2", "L", 1), ("F", 2), ("F", 3), ("D", 0), ("w2", "L", 2), ("D", 1),
-    ("w2", "L", 3), ("D", 2), ("D", 3), ("END",),
+    210, 110, 130, 10, 221, 410, 121, 310, 430, 222, 230, 21, 223, 30, 131, 330, 122, 22, 23, 231, 123, 500,
+    132, 31, 32, 33, 140, 321, 232, 421, 240, 331, 133, 40, 41, 141, 322, 42, 43, 241, 233, 700, 323, 242,
+    142, 800, 440, 431, 801, 143, 422, 332, 340, 341, 802, 243, 333, 803, 423, 432, 600, 900, 1000, 342, 433,
+    343, 1001, 1002, 441, 442, 1003, 1300, 1100, 443, 1101, 1102, 1103, 1200,
 )
 
 
@@ -759,14 +797,14 @@
     rest = rest[n + 5 :]
     whole_h, saved_h = dict(zip(WEIGHTS, rest[:4])), dict(zip(SAVED, rest[4 : 4 + m]))
     rest = rest[4 + m :]
-    x, ct, b1 = rest[:3]
-    whole = dict(zip(names, rest[3 : 3 + n]))
-    rest = rest[3 + n :]
+    x, ct, out, b1 = rest[:4]
+    whole = dict(zip(names, rest[4 : 4 + n]))
+    rest = rest[4 + n :]
     local_sem, keep_sem = rest[0], rest[1]
     swap_sems, rest = rest[2:6], rest[6:]
     sems, refs = rest[: 6 * n], rest[6 * n :]
     p = Place()
-    f = Forward(x, whole, vectors, b1, mask, out_h, probs_h, saved_h, refs)
+    f = Forward(x, whole, vectors, b1, mask, out, out_h, probs_h, saved_h, refs)
     gathers = {a: Gather(p, a, own[a], whole[a], sems[6 * i : 6 * i + 6]) for i, a in enumerate(names)}
     swaps = dict(XS=Swap(p, x_in, x, swap_sems[0:2]), CS=Swap(p, ct_in, ct, swap_sems[2:4]))
     local = [
@@ -781,28 +819,30 @@
         c.start()
     p.greet()
     pending = []
-    settled = False
+    settled = []
+    resid_stored = f.stores(("resid",))
 
     def keep(src, dst):
         c = pltpu.make_async_copy(src, dst, keep_sem.at[len(pending)])
         c.start()
         pending.append(c)
 
-    for name, *step in SEQUENCE:
+    def do(code, step):
+        name, kind = ACTS[code // 100], KINDS[code // 10 % 10]
         if name in gathers:
-            g, kind = gathers[name], step[0]
+            g = gathers[name]
             if kind == "O":
                 g.open()
             elif kind == "A":
-                g.arrive(step[1])
+                g.arrive(step)
             elif kind == "S":
-                g.second(step[1])
+                g.second(step)
             else:
                 if not settled:
                     for c in local:
                         c.wait()
-                    settled = True
-                g.last(step[1])
+                    settled.append(True)
+                g.last(step)
         elif name in swaps:
             swaps[name].start()
         elif name == "LN1":
@@ -817,37 +857,51 @@
             keep(x, x_h)
             f.start_norm()
         elif name == "Q":
-            gathers["wqkv"].have(step[0])
-            f.heads(p.order(step[0]), step[0])
+            gathers["wqkv"].have(step)
+            f.heads(p.order(step), step)
         elif name == "OUT":
             for i in range(4):
                 gathers["wout"].have(i)
             keep(whole["wqkv"], whole_h["wqkv"])
             keep(whole["wout"], whole_h["wout"])
             f.middle()
-            for c in f.stores(("q", "k", "v", "ctx", "nin_t", "resid")):
+            f.turn()
+            for c in (*f.stores(("q", "k", "v", "ctx", "nin_t", "ctx_t", "nmid_t")), *resid_stored):
                 c.start()
         elif name == "F":
-            gathers["w1"].have(step[0])
-            f.hidden(p.order(step[0]))
+            gathers["w1"].have(step)
+            f.hidden(p.order(step))
+        elif name == "K1":
+            keep(whole["w1"], whole_h["w1"])
+            for c in f.stores(("slope", "act")):
+                c.start()
+            for c in resid_stored:
+                c.wait()
         elif name == "D":
-            if step[0] == 0:
-                keep(whole["w1"], whole_h["w1"])
-                for c in f.stores(("act_t", "slope")):
-                    c.start()
-            gathers["w2"].have(step[0])
-            f.down(p.order(step[0]))
+            gathers["w2"].have(step)
+            f.down(p.order(step))
         elif name == "END":
             keep(whole["w2"], whole_h["w2"])
             f.finish()
             f.store_out().start()
             swaps["CS"].done()
             keep(ct, ct_h)
-            f.turn()
-            for c in f.stores(("ctx_t", "nmid_t")):
-                c.start()
+    for item in SEQUENCE:
+        if isinstance(item, int):
+            do(item, item % 10)
+            continue
+
+        @pl.loop(0, 4 + max(code % 10 for code in item))
+        def _(m, item=item):
+            for code in item:
+                lag = code % 10
+
+                @pl.when((m >= lag) & (m < lag + 4))
+                def _():
+                    do(code, m - lag)
+
     f.drain_last(p.order(3))
-    for c in [*pending, *f.stores(SAVED), f.store_out()]:
+    for c in [*pending, *f.stores([a for a in SAVED if a != "resid"]), f.store_out()]:
         c.wait()
     for s in swaps.values():
         s.finish()
@@ -864,9 +918,9 @@
         + list(SAVED.values()),
         in_specs=[ANY, ANY, VM] + [ANY] * n,
         out_specs=[ANY] * 4 + [VM] + [ANY] * (4 + m),
-        scratch_shapes=[scratch(IMAGE), scratch(IMAGE), pltpu.VMEM((4, 1, 1024), F32)]
+        scratch_shapes=[scratch(IMAGE), scratch(IMAGE), scratch(IMAGE), pltpu.VMEM((4, 1, 1024), F32)]
         + [scratch(part(a)) for a in names]
-        + [pltpu.SemaphoreType.DMA((n + 2,)), pltpu.SemaphoreType.DMA((6,))]
+        + [pltpu.SemaphoreType.DMA((n + 2,)), pltpu.SemaphoreType.DMA((7,))]
         + Swap.SEMS * 2
         + Gather.SEMS * n
         + Forward.SCRATCH,
@@ -875,152 +929,168 @@
         ),
         name="spread",
     )(x_in, ct_in, mask, *[own[a] for a in names])
-    x, ct, out, probs, vectors = outs[:5]
-    return x, ct, out, probs, vectors, dict(zip(WEIGHTS, outs[5:9])), dict(zip(SAVED, outs[9:]))
+    return outs[:5], dict(zip(WEIGHTS, outs[5:9])), dict(zip(SAVED, outs[9:]))
 
 
 REDUCED = ("w2", "w1", "wout", "wqkv")
 
 
+def turn_of(i):
+    return (1 - i // 2) * (1 - i % 2) * 3 + i // 2 * (2 - i % 2)
+
+
 class Reduce:
-    def __init__(self, place, name, grad, own, got, got1, got2, got3, result, sems):
-        self.p, self.name, self.grad, self.own, self.got = place, name, grad, own, got
-        self.got1, self.got2, self.got3, self.result = got1, got2, got3, result
-        self.send, self.recv, self.local = sems
-
-    def plane(self, c):
-        return self.grad.at[:, c] if self.name in BY_COLUMN else self.grad.at[:, :, c]
+    def __init__(self, place, name, refs):
+        self.p, self.name = place, name
+        self.own, self.got1, self.got2, self.got3 = refs[:4]
+        self.c_recv, self.send, self.recv, self.z_send, self.z_recv = refs[4:]
+
+    @staticmethod
+    def scratch(name):
+        rows, width = PARTS[name][0][3:]
+        return [
+            pltpu.VMEM((4, 4, rows, width), BF16),
+            pltpu.VMEM((4, 4, rows // 2, width), BF16),
+            pltpu.VMEM((2, 4, rows // 2, width), BF16),
+            pltpu.VMEM((5, rows, width), BF16),
+            pltpu.SemaphoreType.DMA((4,)),
+            pltpu.SemaphoreType.DMA((4, 6)),
+            pltpu.SemaphoreType.DMA((4, 6)),
+            pltpu.SemaphoreType.DMA((4,)),
+            pltpu.SemaphoreType.DMA((5,)),
+        ]
 
     def block(self, ref, t, yx):
         return ref.at[yx, t] if self.name in BY_COLUMN else ref.at[t, yx]
 
-    def core_copy(self):
-        return remote(self.plane(1 - self.p.c), self.got, self.send.at[0], self.recv.at[0], self.p.c_id)
-
-    def own_copy(self):
-        return pltpu.make_async_copy(self.plane(self.p.c), self.own, self.local)
+    def wait_bytes(self, ref, sem):
+        remote(ref, ref, self.z_send.at[0], sem, self.p.c_id).wait_recv()
 
     def add(self, dst, *more):
-        rows = dst.shape[0]
-        n = min(64, rows)
+        rows, width = dst.shape
+        n = min(rows, 64 if width > 128 else 512)
 
         @pl.loop(0, rows // n)
         def _(i):
             r = pl.ds(pl.multiple_of(i * n, n), n)
-            total = dst[r, :].astype(F32)
+            total = dst[r, :]
             for ref in more:
-                total += ref[r, :].astype(F32)
-            dst[r, :] = total.astype(BF16)
+                total += ref[r, :]
+            dst[r, :] = total
 
     def first_copy(self, by_y, j, t):
         p = self.p
         yx = (1 - p.y) * 2 + j if by_y else j * 2 + 1 - p.x
         src = half_of(self.block(self.own, t, yx), 0 if by_y else 1)
         k = (0 if by_y else 2) + j
-        n = 1 + k * 4 + t
-        return remote(src, self.got1.at[k, t], self.send.at[n], self.recv.at[n], p.y_id if by_y else p.x_id)
+        return remote(src, self.got1.at[k, t], self.send.at[t, k], self.recv.at[t, k], p.y_id if by_y else p.x_id)
 
     def second_copy(self, j, t):
         p = self.p
         by_x = j == 0
         src = half_of(self.block(self.own, t, p.x_yx if by_x else p.y_yx), j)
-        return remote(src, self.got2.at[j, t], self.send.at[17 + j * 4 + t], self.recv.at[17 + j * 4 + t],
+        return remote(src, self.got2.at[j, t], self.send.at[t, 4 + j], self.recv.at[t, 4 + j],
                       p.x_id if by_x else p.y_id)
 
-    def z_copy(self, k):
+    def other_core(self, t=None):
+        ref = self.own if t is None else self.own.at[:, t] if self.name in BY_COLUMN else self.own.at[t]
+        self.wait_bytes(ref, self.c_recv.at[0 if t is None else t])
+
+    def begin(self, t):
         p = self.p
-        to = lax.rem(p.t + k, 4)
-        src = self.block(self.own, to, p.yx)
-        return remote(src, self.got3.at[k - 1], self.send.at[24 + k], self.recv.at[24 + k], p.z_id(to))
-
-    def stage(self, i):
+        self.first_copy(True, 1 - p.x, t).start()
+        self.first_copy(False, 1 - p.y, t).start()
+        self.first_copy(True, p.x, t).start()
+        self.first_copy(False, p.y, t).start()
+
+    def cross(self, i):
+        p, t = self.p, turn_of(i)
+        for j in range(2):
+            self.first_copy(True, j, t).wait_recv()
+            self.first_copy(False, j, t).wait_recv()
+        self.add(half_of(self.block(self.own, t, p.x_yx), 0), self.got1.at[1 - p.x, t])
+        self.second_copy(0, t).start()
+        self.add(half_of(self.block(self.own, t, p.y_yx), 1), self.got1.at[2 + 1 - p.y, t])
+        self.second_copy(1, t).start()
+        self.add(half_of(self.block(self.own, t, p.yx), 0), self.got1.at[p.x, t])
+        self.add(half_of(self.block(self.own, t, p.yx), 1), self.got1.at[2 + p.y, t])
+
+    def along(self, i):
+        p, t = self.p, turn_of(i)
+        mine = self.block(self.own, t, p.yx)
+        for j in (0, 1):
+            self.second_copy(j, t).wait_recv()
+            self.add(half_of(mine, j), self.got2.at[j, t])
+        for up, ends in ((True, (p.t == 0) & (t > 0)), (False, (p.t == 3) & (t < 3))):
+
+            @pl.when(ends)
+            def _():
+                self.send_z(t, up).start()
+
+    def pass_on(self, i, hop):
+        p, t = self.p, turn_of(i)
+        mine = self.block(self.own, t, p.yx)
+        for up, here in ((True, (p.t == hop) & (t > hop)), (False, (p.t == 3 - hop) & (t < 3 - hop))):
+
+            @pl.when(here)
+            def _():
+                self.wait_bytes(self.got3.at[t], self.z_recv.at[t])
+                self.add(mine, self.got3.at[t])
+                self.send_z(t, up).start()
+
+    def send_z(self, t, up):
         p = self.p
-        if i == 0:
-            self.core_copy().start()
-            self.own_copy().start()
-        if i == 1:
-            self.own_copy().wait()
-            self.core_copy().wait_recv()
-            self.sum_core()
-        if i == 2:
-            self.sum_first()
-        if i == 3:
-            self.sum_second()
-        if i == 4:
-            self.sum_last()
-
-    def sum_core(self):
+        slot = t if up else t + (4 - t) * ((3 + t - p.t) // 2)
+        return remote(self.block(self.own, t, p.yx), self.got3.at[slot], self.z_send.at[t], self.z_recv.at[slot],
+                      p.z_id(p.t + 1 if up else p.t - 1))
+
+    def end(self, result):
         p = self.p
-        for yx, by_y, by_x in ((p.xy_yx, 1 - p.x, 1 - p.y), (p.y_yx, p.x, None), (p.x_yx, None, p.y), (p.yx, None, None)):
-            for t in range(4):
-                self.add(self.block(self.own, t, yx), self.block(self.got, t, yx))
-                if by_y is not None:
-                    self.first_copy(True, by_y, t).start()
-                if by_x is not None:
-                    self.first_copy(False, by_x, t).start()
-
-    def sum_first(self):
+        mine = self.block(self.own, p.t, p.yx)
+        rows, width = mine.shape
+        n = min(rows, 32 if width > 128 else 256)
+
+        def through(ref):
+            @pl.loop(0, rows // n)
+            def _(i):
+                r = pl.ds(pl.multiple_of(i * n, n), n)
+                result[r, :] = (mine if ref is mine else result)[r, :].astype(F32) + (
+                    0.0 if ref is mine else ref[r, :].astype(F32)
+                )
+
+        through(mine)
+        for slot, there in ((p.t, p.t > 0), (4, p.t < 3)):
+
+            @pl.when(there)
+            def _():
+                self.wait_bytes(self.got3.at[slot], self.z_recv.at[slot])
+                through(self.got3.at[slot])
+
+    def finish(self):
         p = self.p
-        for t in range(4):
-            for j in range(2):
-                self.first_copy(True, j, t).wait_recv()
-                self.first_copy(False, j, t).wait_recv()
-        for t in range(4):
-            self.add(half_of(self.block(self.own, t, p.x_yx), 0), self.got1.at[1 - p.x, t])
-            self.second_copy(0, t).start()
-            self.add(half_of(self.block(self.own, t, p.y_yx), 1), self.got1.at[2 + 1 - p.y, t])
-            self.second_copy(1, t).start()
-        for t in range(4):
-            self.add(half_of(self.block(self.own, t, p.yx), 0), self.got1.at[p.x, t])
-            self.add(half_of(self.block(self.own, t, p.yx), 1), self.got1.at[2 + p.y, t])
-
-    def sum_second(self):
-        p = self.p
-        for k in (1, 2, 3, 0):
-            t = lax.rem(p.t + k, 4)
-            for j in (0, 1):
-                self.second_copy(j, t).wait_recv()
-                self.add(half_of(self.block(self.own, t, p.yx), j), self.got2.at[j, t])
-            if k:
-                self.z_copy(k).start()
-
-    def sum_last(self):
-        p = self.p
-        for k in (1, 2, 3):
-            self.z_copy(k).wait_recv()
-        mine = self.block(self.own, p.t, p.yx)
-        rows = mine.shape[0]
-
-        @pl.loop(0, rows // 64)
-        def _(i):
-            r = pl.ds(pl.multiple_of(i * 64, 64), 64)
-            total = mine[r, :].astype(F32)
-            for k in range(3):
-                total += self.got3[k, r, :].astype(F32)
-            self.result[r, :] = total
-
-    def finish(self):
-        self.core_copy().wait_send()
         for t in range(4):
             for j in range(2):
                 self.first_copy(True, j, t).wait_send()
                 self.first_copy(False, j, t).wait_send()
                 self.second_copy(j, t).wait_send()
-        for k in (1, 2, 3):
-            self.z_copy(k).wait_send()
-
-
-def reduce_shapes(name):
-    shape = PARTS[name][0]
-    rows, width = shape[3:]
-    plane = (4, 4, rows, width)
-    return plane, (4, 4, rows // 2, width), (2, 4, rows // 2, width), (3, rows, width), (rows, width)
+
+            @pl.when(p.t != t)
+            def _():
+                block = self.block(self.own, t, p.yx)
+                remote(block, block, self.z_send.at[t], self.z_recv.at[t], p.c_id).wait_send()
 
 
 class Total:
-    def __init__(self, place, acc, sent, got, sems):
-        self.p, self.acc, self.sent, self.got = place, acc, sent, got
-        self.send, self.recv = sems
+    SCRATCH = [
+        pltpu.VMEM((4, 16, D), F32),
+        pltpu.VMEM((6, 16, D), F32),
+        pltpu.SemaphoreType.DMA((6,)),
+        pltpu.SemaphoreType.DMA((6,)),
+    ]
+
+    def __init__(self, place, acc, refs):
+        self.p, self.acc = place, acc
+        self.sent, self.got, self.send, self.recv = refs
 
     def copies(self, i):
         p = self.p
@@ -1043,86 +1113,478 @@
             self.acc[...] += self.got[k]
 
 
-def reduce_kernel(out_in, gtok_in, sums_in, *rest):
-    n = len(REDUCED)
-    grads = dict(zip(REDUCED, rest[:n]))
-    out, gtok, sums = rest[n : n + 3]
-    results = dict(zip(REDUCED, rest[n + 3 : 2 * n + 3]))
-    rest = rest[2 * n + 3 :]
-    out_buf, gtok_buf, sent, got = rest[:4]
-    local_sem, total_send, total_recv = rest[4:7]
-    swap_sems = rest[7:11]
-    rest = rest[11:]
-    place = Place()
-    parts = []
-    for i, a in enumerate(REDUCED):
-        own, got0, got1, got2, got3, send, recv, local = rest[8 * i : 8 * i + 8]
-        parts.append(Reduce(place, a, grads[a], own, got0, got1, got2, got3, results[a], (send, recv, local)))
-    swaps = [Swap(place, out_in, out, swap_sems[0:2]), Swap(place, gtok_in, gtok, swap_sems[2:4])]
-    local = [
-        Bounce(out_in.at[place.t], out_buf, out.at[place.t], local_sem.at[0]),
-        Bounce(gtok_in.at[place.t], gtok_buf, gtok.at[place.t], local_sem.at[1]),
+class Stream:
+    def __init__(self, n, src, buf, sem):
+        self.n, self.src, self.buf, self.sem = n, src, buf, sem
+        self.depth = buf.shape[0]
+
+    def copies(self, i):
+        slot = lax.rem(i, self.depth)
+        return [
+            pltpu.make_async_copy(a, b, self.sem.at[slot, k])
+            for k, (a, b) in enumerate(self.src(i, self.buf.at[slot]))
+        ]
+
+    def start(self):
+        for i in range(min(self.depth - 1, self.n)):
+            for c in self.copies(jnp.int32(i)):
+                c.start()
+
+    def next(self, i):
+        for c in self.copies(i):
+            c.wait()
+
+        @pl.when(i + self.depth - 1 < self.n)
+        def _():
+            for c in self.copies(i + self.depth - 1):
+                c.start()
+
+        return self.buf.at[lax.rem(i, self.depth)]
+
+
+def accumulate(ref, here, value, step):
+    @pl.when(step == 0)
+    def _():
+        ref[:, here] = value
+
+    @pl.when(step > 0)
+    def _():
+        ref[:, here] += value
+
+
+BACK = ("w2", "w1", "wout", "wqkv", "T", "G0", "GS", "GM", "SHARE", "HG", "HS", "HM", "GN", "GR", "OA", "OM", "AT", "AM", "GI", "GT")
+STEPS = ("", "X", "Z", "E", "Y", "W")
+COLLECT = (
+    500, (600, 701,), (900,), 1200, 800, 1300, 1400, 10, 13, 11, 12, 1500, (1600, 1701, 20,), 311, 1800, 211,
+    312, 40, 43, 53, 42, 41, 210, 1900, 213, 313, 310, (1000, 1101,), 212, 220, 51, 110, 223, 323, 50, 111,
+    322, 321, 343, 112, 342, 52, 320, 352, 113, 400, 221, 241, 341, 120, 222, 243, 240, 353, 250, 340, 350,
+    121, 253, 122, 140, 351, 251, 242, 123, 30, 141, 142, 401, 151, 252, 152, 330, 402, 150, 143, 230, 153,
+    403, 130,
+)
+
+
+class Backward:
+    NAMES = (
+        ("image", "gmlp", "slope", "gmix", "gn", "resid", "split", "ctx_t", "b1", "part_sums", "load_sem")
+        + ("col_buf", "col_sem", "row_buf", "row_sem", "head_buf", "head_sem", "probs", "probs_sem")
+        + ("up_mail", "up_mail_sem", "mix_mail", "mix_mail_sem", "out_mail", "out_mail_sem", "down_mail", "down_mail_sem")
+    )
+    SCRATCH = [
+        scratch(IMAGE),
+        scratch(ACT),
+        pltpu.VMEM((ROWS, 4 * D), BF16),
+        pltpu.VMEM((ROWS, 3 * D), BF16),
+        pltpu.VMEM((ROWS, D), F32),
+        pltpu.VMEM((ROWS, D), F32),
+        pltpu.VMEM((2, 4, 128, ROWS), BF16),
+        pltpu.VMEM((4, 2, 128, ROWS), BF16),
+        pltpu.VMEM((4, 1, 1024), F32),
+        pltpu.VMEM((6, 8, D), F32),
+        pltpu.SemaphoreType.DMA((12,)),
+        pltpu.VMEM((3, 4, 2, 2, 256, 128), BF16),
+        pltpu.SemaphoreType.DMA((3, 2)),
+        pltpu.VMEM((3, 2, 2, 128, 1024), BF16),
+        pltpu.SemaphoreType.DMA((3, 1)),
+        pltpu.VMEM((3, 4, ROWS, 128), BF16),
+        pltpu.SemaphoreType.DMA((3, 4)),
+        pltpu.VMEM((2, 2, ROWS, ROWS), BF16),
+        pltpu.SemaphoreType.DMA((2, 1)),
+        pltpu.VMEM((2, 4, 128, 512), BF16),
+        pltpu.SemaphoreType.DMA((2,)),
+        pltpu.VMEM((2, 4, 128, 768), BF16),
+        pltpu.SemaphoreType.DMA((2,)),
+        pltpu.VMEM((2, 2, 4, 256, 128), BF16),
+        pltpu.SemaphoreType.DMA((2,)),
+        pltpu.VMEM((1, 4, 1024, 128), BF16),
+        pltpu.SemaphoreType.DMA((1,)),
     ]
-    for b in local:
-        b.load.start()
-    place.greet()
-    for r in parts:
-        r.stage(0)
-    total = Total(place, sums, sent, got, (total_send, total_recv))
-    sums[...] = sums_in[...]
-    total.start(0)
-    for b in local:
-        b.load.wait()
-        b.store.start()
-    for s in swaps:
-        s.start()
-    small = 0
-    for tick in range(1, n + 4):
-        for i, r in enumerate(parts):
-            if 1 <= tick - i <= 4:
-                r.stage(tick - i)
-        if small < 4:
-            total.end(small)
-            small += 1
-            if small < 4:
-                total.start(small)
-    for b in local:
-        b.store.wait()
-    for s in swaps:
-        s.done()
-        s.finish()
-    for r in parts:
-        r.finish()
-
-
-def reduce(out, gtok, sums, grads):
-    n = len(REDUCED)
-    shapes = [reduce_shapes(a) for a in REDUCED]
+
+    def __init__(self, p, reduces, swaps_of, total, hbm, vectors, sums, refs):
+        for a, b in zip(self.NAMES, refs):
+            setattr(self, a, b)
+        self.p, self.reduces, self.total, self.vectors, self.sums = p, reduces, total, vectors, sums
+        self.hbm = hbm
+        self.out_swap, self.tok_swap = swaps_of(self.image)
+        self.ups_mail = Mail(p, self.up_mail, self.up_mail_sem)
+        self.mixes_mail = Mail(p, self.mix_mail, self.mix_mail_sem)
+        self.downs_mail = Mail(p, self.down_mail, self.down_mail_sem)
+        self.outs_mail = Mail(p, self.out_mail, self.out_mail_sem)
+        h = hbm
+        self.out_buf = self.probs.at[0, 0, :, pl.ds(0, 256)]
+        self.loads = {
+            a: self.load(i, *b)
+            for i, (a, b) in enumerate(
+                dict(
+                    ct=(h["ct"], self.image),
+                    slope=(h["slope"], self.slope),
+                    nin0=(h["nin_t"].at[:, p.c], self.split.at[0]),
+                    nin1=(h["nin_t"].at[:, 1 - p.c], self.split.at[1]),
+                    out=(h["out"].at[p.t], self.out_buf),
+                    resid=(h["resid"], self.resid),
+                    ctx_t=(h["ctx_t"], self.ctx_t),
+                    x=(h["x"], self.image),
+                ).items()
+            )
+        }
+        self.nmid = [
+            self.load(2, h["nmid_t"].at[:, p.c], self.split.at[0]),
+            self.load(3, h["nmid_t"].at[:, 1 - p.c], self.split.at[1]),
+        ]
+        self.out_done = self.load(4, self.out_buf, h["out_o"].at[p.t])
+        self.tok_done = self.load(0, self.image.at[p.t], h["gtok_o"].at[p.t])
+
+        def down_src(i, b):
+            return [
+                (h["w2"].at[:, :, turn_of(i // 2), pl.ds(i % 2 * 512 + k * 256, 256)], b.at[:, :, k]) for k in range(2)
+            ]
+
+        def out_src(i, b):
+            return [(h["wout"].at[:, :, i * 2 + k], b.at[:, :, k]) for k in range(2)]
+
+        def head_src(i, b):
+            at = cols(turn_of(i // 2) * 2 + i % 2, 128)
+            return [(h[a].at[:, at], b.at[k]) for k, a in enumerate(("q", "k", "v", "ctx"))]
+
+        self.downs = Stream(8, down_src, self.col_buf, self.col_sem)
+        self.outs = Stream(2, out_src, self.col_buf, self.col_sem)
+        self.ups = Stream(
+            8, lambda i, b: [(h["w1"].at[i % 4, pl.ds(i // 4 * 2, 2)], b)], self.row_buf, self.row_sem
+        )
+        self.mixes = Stream(
+            8,
+            lambda i, b: [(h["wqkv"].at[i % 4, pl.ds(i // 4 * 2, 2)], b.at[:, :, :, pl.ds(0, 768)])],
+            self.row_buf,
+            self.row_sem,
+        )
+        self.heads = Stream(8, head_src, self.head_buf, self.head_sem)
+        self.heads_p = Stream(
+            8, lambda i, b: [(h["probs"].at[turn_of(i // 2) * 2 + i % 2], b)], self.probs, self.probs_sem
+        )
+
+    def load(self, i, src, dst):
+        return pltpu.make_async_copy(src, dst, self.load_sem.at[i])
+
+    def act_load(self, i):
+        return self.load(8 + i, self.hbm["act"].at[:, cols(turn_of(i), 1024)], self.gmix.at[:, cols(i % 3, 1024)])
+
+    def begin(self):
+        self.loads["ct"].start()
+        for i in range(3):
+            self.act_load(i).start()
+        self.loads["slope"].start()
+        self.downs.start()
+        self.ups.start()
+        for a in ("out", "resid", "ctx_t", "nin0", "nin1"):
+            self.loads[a].start()
+        self.heads.start()
+        self.part_sums[...] = jnp.zeros_like(self.part_sums)
+        self.sums[...] = jnp.zeros_like(self.sums)
+
+    def mask_cotangent(self):
+        self.loads["ct"].wait()
+        mask = self.hbm["mask"]
+
+        @over_rows
+        def _(rows):
+            g = wide(self.image, rows) * jnp.concatenate([mask[...]] * 4, axis=1)
+            self.gmlp[rows, :] = g.astype(BF16)
+            self.part_sums[0] += fold(g)
+
+        self.loads["out"].wait()
+        self.out_done.start()
+
+    def four_columns(self, c):
+        return jnp.concatenate([self.gmlp[:, cols(yx * 2 + c, 128)] for yx in range(4)], axis=1)
+
+    def down_share(self, i):
+        r, t = self.reduces["w2"], turn_of(i)
+        self.act_load(i).wait()
+        g = t_mm(self.gmix[:, cols(i % 3, 1024)], self.four_columns(1 - self.p.c)).astype(BF16)
+        self.downs_mail.post(
+            i, [g[:, k * 128 : k * 128 + 128] for k in range(4)], r.own.at[:, t], r.c_recv.at[t]
+        )
+
+    def down_own(self, i):
+        r, t = self.reduces["w2"], turn_of(i)
+        r.other_core(t)
+        g = t_mm(self.gmix[:, cols(i % 3, 1024)], self.four_columns(self.p.c))
+        for k in range(4):
+            r.own[k, t] = (g[:, k * 128 : k * 128 + 128] + r.own[k, t].astype(F32)).astype(BF16)
+        r.begin(t)
+
+        @pl.when(i == 0)
+        def _():
+            self.act_load(3).start()
+
+    def share(self):
+        self.out_swap.start()
+
+    def whole_rows(self, tile):
+        return jnp.concatenate([tile[d // 2, d % 2].reshape(512, 128) for d in range(8)], axis=1)
+
+    def post_rows(self, mail, n, g, r, t, here):
+        g = g.astype(BF16).reshape(4, 128, -1)
+        mail.post(n, [g[k] for k in range(4)], r.own.at[t, :, :, here], r.c_recv.at[t])
+
+    def hidden(self, i):
+        t = turn_of(i)
+
+        @pl.when(i == 0)
+        def _():
+            self.loads["slope"].wait()
+
+        @pl.loop(0, 2)
+        def _(j):
+            w = self.whole_rows(self.downs.next(2 * i + j))
+            here = cols(t * 2 + j, 512)
+            gpre = mm_t(self.gmlp[...], w) * self.slope[:, here].astype(F32)
+            self.slope[:, here] = gpre.astype(BF16)
+            self.b1[t, :, cols(j, 512)] = jnp.sum(gpre, axis=0, keepdims=True)
+
+    def hidden_share(self, i):
+        r, t = self.reduces["w1"], turn_of(i)
+
+        @pl.loop(0, 2)
+        def _(j):
+            g = mm(self.split[1].reshape(512, ROWS), self.slope[:, cols(t * 2 + j, 512)])
+            self.post_rows(self.ups_mail, 2 * i + j, g, r, t, cols(j, 512))
+
+    def add_own(self, r, t, here, value):
+        width = value.shape[1]
+        had = r.own[t, :, :, here].astype(F32)
+        r.own[t, :, :, here] = (value.reshape(4, 128, width) + had).astype(BF16)
+
+    def hidden_own(self, i):
+        r, t = self.reduces["w1"], turn_of(i)
+        r.other_core(t)
+
+        @pl.loop(0, 2)
+        def _(j):
+            g = mm(self.split[0].reshape(512, ROWS), self.slope[:, cols(t * 2 + j, 512)])
+            self.add_own(r, t, cols(j, 512), g)
+
+        r.begin(t)
+
+    def through_up(self):
+        self.outs.start()
+
+        @pl.loop(0, 8)
+        def _(i):
+            w = self.ups.next(i)
+            g = mm_t(self.slope[:, cols(i % 4, 1024)], w[...].reshape(512, D))
+            accumulate(self.gn, cols(i // 4, 512), g, i % 4)
+
+        self.mixes.start()
+
+    def norm_mid(self):
+        self.loads["resid"].wait()
+        gain = vec(self.vectors, 5)
+
+        @over_rows
+        def _(rows):
+            normed = self.gn[rows, :]
+            g, scaled = grad_norm_rows(self.resid[rows, :], gain, normed)
+            g = g + self.gmlp[rows, :].astype(F32)
+            self.part_sums[1] += fold(normed)
+            self.part_sums[2] += fold(scaled)
+            self.part_sums[3] += fold(g)
+            self.gn[rows, :] = g
+            self.gmlp[rows, :] = g.astype(BF16)
+
+    def attn_out(self):
+        r, p = self.reduces["wout"], self.p
+        self.loads["ctx_t"].wait()
+        self.out_done.wait()
+        self.heads_p.start()
+
+        @pl.loop(0, 2)
+        def _(q):
+            g = mm(self.ctx_t[...].reshape(D, ROWS), column_pair(self.gmlp, q, 1 - p.c)).astype(BF16)
+            self.outs_mail.post(
+                q,
+                [g[:, k * 128 : k * 128 + 128].reshape(4, 256, 128) for k in range(2)],
+                r.own.at[pl.ds(q * 2, 2)],
+                r.c_recv.at[0],
+            )
+
+        @pl.loop(0, 2)
+        def _(i):
+            g = mm_t(self.gmlp[...], self.whole_rows(self.outs.next(i))).astype(BF16)
+            for k in range(2):
+                self.image[i * 2 + k] = g[:, k * 256 : k * 256 + 256]
+
+    def attn_out_own(self):
+        r, p = self.reduces["wout"], self.p
+        r.other_core()
+
+        @pl.loop(0, 2)
+        def _(q):
+            g = mm(self.ctx_t[...].reshape(D, ROWS), column_pair(self.gmlp, q, p.c))
+            for k in range(2):
+                had = r.own[q * 2 + k].astype(F32)
+                r.own[q * 2 + k] = (g[:, k * 128 : k * 128 + 128].reshape(4, 256, 128) + had).astype(BF16)
+
+        for i in range(4):
+            r.begin(turn_of(i))
+        for a in ("nin0", "nin1"):
+            self.loads[a].wait()
+
+    def attend(self, i):
+        r, t = self.reduces["wqkv"], turn_of(i)
+
+        @pl.loop(0, 2)
+        def _(h):
+            ins = self.heads.next(2 * i + h)
+            probs = self.heads_p.next(2 * i + h)
+            got = attend_back_pair(*(ins[k] for k in range(4)), self.image[t, :, cols(h, 128)], probs)
+            for c in range(3):
+                self.gmix[:, pl.ds(pl.multiple_of(t * 768 + c * 256 + h * 128, 128), 128)] = got[c].astype(BF16)
+            here = cols(t * 2 + h, 128)
+            self.sums[2:3, here] = jnp.sum(got[0], axis=0, keepdims=True)
+            self.sums[3:4, here] = jnp.sum(got[2], axis=0, keepdims=True)
+
+        g = mm(self.split[1].reshape(512, ROWS), self.gmix[:, cols(t, 768)])
+        self.post_rows(self.mixes_mail, i, g, r, t, pl.ds(0, 768))
+
+    def attend_own(self, i):
+        r, t = self.reduces["wqkv"], turn_of(i)
+        r.other_core(t)
+        self.add_own(r, t, slice(None), mm(self.split[0].reshape(512, ROWS), self.gmix[:, cols(t, 768)]))
+        r.begin(t)
+
+    def through_mix(self):
+        self.loads["x"].start()
+        for c in self.nmid:
+            c.start()
+
+        @pl.loop(0, 8)
+        def _(i):
+            w = self.mixes.next(i)
+            g = mm_t(self.gmix[:, cols(i % 4, 768)], w[:, :, :, 0:768].reshape(512, 768))
+            accumulate(self.resid, cols(i // 4, 512), g, i % 4)
+
+    def norm_in(self):
+        self.loads["x"].wait()
+        gain = vec(self.vectors, 0)
+
+        @over_rows
+        def _(rows):
+            normed = self.resid[rows, :]
+            g, scaled = grad_norm_rows(wide(self.image, rows), gain, normed)
+            g = g + self.gn[rows, :]
+            self.part_sums[4] += fold(normed)
+            self.part_sums[5] += fold(scaled)
+            for t in range(4):
+                self.image[t, rows, :] = g[:, t * 256 : t * 256 + 256].astype(BF16)
+
+        self.tok_swap.start()
+        self.tok_done.start()
+        sums = self.sums
+        for row, i in ((7, 0), (6, 1), (5, 2), (4, 3), (1, 4), (0, 5)):
+            sums[row : row + 1, :] = jnp.sum(self.part_sums[i], axis=0, keepdims=True)
+        for t in range(4):
+            sums[8 + t : 9 + t, :] = self.b1[t]
+        self.total.start(0)
+        for c in self.nmid:
+            c.wait()
+
+    def finish(self):
+        self.tok_done.wait()
+        for m in (self.ups_mail, self.mixes_mail, self.outs_mail, self.downs_mail):
+            m.finish()
+        for s in (self.out_swap, self.tok_swap):
+            s.done()
+            s.finish()
+        for r in self.reduces.values():
+            r.finish()
+
+
+HBM = ("x", "out", "ct", "probs") + WEIGHTS
+
+
+def collect_kernel(vectors, mask, *rest):
+    names = HBM + tuple(SAVED)
+    n = len(names)
+    hbm = dict(zip(names, rest[:n]), mask=mask)
+    out_o, gtok_o, sums = rest[n : n + 3]
+    hbm |= dict(out_o=out_o, gtok_o=gtok_o)
+    results = dict(zip(REDUCED, rest[n + 3 : n + 7]))
+    rest = rest[n + 7 :]
+    m = len(Backward.SCRATCH)
+    refs, rest = rest[:m], rest[m:]
+    out_sems, tok_sems, total_refs, rest = rest[0:2], rest[2:4], rest[4:8], rest[8:]
+    p = Place()
+    reduces = {a: Reduce(p, a, rest[9 * i : 9 * i + 9]) for i, a in enumerate(REDUCED)}
+    total = Total(p, sums, total_refs)
+
+    def swaps_of(image):
+        return Swap(p, hbm["out"], out_o, out_sems), Swap(p, image, gtok_o, tok_sems)
+
+    b = Backward(p, reduces, swaps_of, total, hbm, vectors, sums, refs)
+    acts = dict(
+        G0=b.mask_cotangent, GS=b.down_share, GM=b.down_own, SHARE=b.share, HG=b.hidden, HS=b.hidden_share, HM=b.hidden_own, GN=b.through_up, GR=b.norm_mid, OA=b.attn_out,
+        OM=b.attn_out_own, AT=b.attend, AM=b.attend_own, GI=b.through_mix, GT=b.norm_in,
+    )
+    counted = ("GS", "GM", "HG", "HS", "HM", "AT", "AM")
+
+    def act(code, i):
+        name, kind = BACK[code // 100], STEPS[code // 10 % 10]
+        if name in reduces:
+            r = reduces[name]
+            if kind == "E":
+                r.end(results[name])
+            elif kind in ("Y", "W"):
+                r.pass_on(i, 1 if kind == "Y" else 2)
+            else:
+                (r.cross if kind == "X" else r.along)(i)
+        elif name == "T":
+            total.end(i)
+            if i < 3:
+                total.start(i + 1)
+        elif name in counted:
+            acts[name](i)
+        else:
+            acts[name]()
+
+    b.begin()
+    p.greet()
+    for step in COLLECT:
+        if isinstance(step, int):
+            act(step, step % 10)
+            continue
+
+        @pl.loop(0, 4 + max(code % 10 for code in step))
+        def _(m, step=step):
+            for code in step:
+                lag = code % 10
+
+                @pl.when((m >= lag) & (m < lag + 4))
+                def _():
+                    act(code, m - lag)
+
+    b.finish()
+
+
+def collect(vectors, mask, hbm):
+    names = HBM + tuple(SAVED)
     outs = pl.pallas_call(
-        reduce_kernel,
+        collect_kernel,
         out_shape=[IMAGE, IMAGE, jax.ShapeDtypeStruct((16, D), F32)]
-        + [jax.ShapeDtypeStruct(s[4], F32) for s in shapes],
-        in_specs=[ANY, ANY, VM] + [ANY] * n,
-        out_specs=[ANY, ANY, VM] + [VM] * n,
-        scratch_shapes=[pltpu.VMEM((ROWS, 256), BF16)] * 2
-        + [pltpu.VMEM((4, 16, D), F32), pltpu.VMEM((6, 16, D), F32)]
-        + [pltpu.SemaphoreType.DMA((2, 2)), pltpu.SemaphoreType.DMA((6,)), pltpu.SemaphoreType.DMA((6,))]
+        + [jax.ShapeDtypeStruct(PARTS[a][0][3:], F32) for a in REDUCED],
+        in_specs=[VM, VM] + [ANY] * len(names),
+        out_specs=[ANY, ANY, VM] + [VM] * 4,
+        scratch_shapes=Backward.SCRATCH
         + Swap.SEMS * 2
-        + sum(
-            (
-                [pltpu.VMEM(s[0], BF16)] * 2
-                + [pltpu.VMEM(s[k], BF16) for k in (1, 2, 3)]
-                + [pltpu.SemaphoreType.DMA((28,)), pltpu.SemaphoreType.DMA((28,)), pltpu.SemaphoreType.DMA]
-                for s in shapes
-            ),
-            [],
-        ),
+        + Total.SCRATCH
+        + sum((Reduce.scratch(a) for a in REDUCED), []),
         compiler_params=pltpu.CompilerParams(
             collective_id=1, has_side_effects=True, vmem_limit_bytes=VMEM_BYTES
         ),
-        name="reduce",
-    )(out, gtok, sums, *[grads[a].reshape(PARTS[a][0]) for a in REDUCED])
+        name="collect",
+    )(vectors, mask, *[hbm[a] for a in names])
     return outs[0], outs[1], outs[2], dict(zip(REDUCED, outs[3:]))
+
+
 def gather_plain(w_qkv, w_out, w_fc1, w_fc2):
     def all_of(shard, axis):
         return lax.all_gather(
@@ -1189,7 +1651,10 @@
             w1=w_fc1.astype(BF16),
             w2=w_fc2.astype(BF16),
         )
-        x, ct, out, probs, vectors, weights, saved = spread(images(tokens_in), images(cotangent), mask, own)
+        first, weights, saved = spread(images(tokens_in), images(cotangent), mask, own)
+        x, ct, out, probs, vectors = first
+        hbm = dict(x=x, out=out, ct=ct, probs=probs, **weights, **saved)
+        out, gtok, sums, got = collect(vectors, mask, hbm)
     else:
         vectors = lax.all_gather(
             lax.all_gather(small, "dp", axis=1, tiled=True), "tensor", axis=0
@@ -1202,14 +1667,13 @@
         plain = gather_plain(w_qkv, w_out, w_fc1, w_fc2)
         weights = {a: b.reshape(PARTS[a][0]) for a, b in zip(WEIGHTS, plain)}
         out, probs, saved = forward(x, weights, vectors, hidden_bias, mask)
-    flat = [weights[a].reshape(GRADS[a].shape) for a in GRADS]
-    gtok, sums, grads = backward(x, ct, *flat, vectors, mask, probs, saved)
     if dp == 8:
-        out, gtok, sums, got = reduce(out, gtok, jnp.pad(sums, ((0, 4), (0, 0))), grads)
         g_qkv, g_out, g_fc1, g_fc2 = (got[a] for a in GRADS)
         g_small = lax.dynamic_slice(sums, (0, t * 256 + d * 32), (8, 32))
         g_hidden = lax.dynamic_slice(sums, (8 + t, d * 128), (1, 128))
     else:
+        flat = [weights[a].reshape(GRADS[a].shape) for a in GRADS]
+        gtok, sums, grads = backward(x, ct, *flat, vectors, mask, probs, saved)
         g_qkv, g_out, g_fc1, g_fc2 = scatter_plain(grads)
         out, gtok = exchange(out), exchange(gtok)
 

time: 379 us -> 304 us (0.80)
  Pallas kernels: 348 us -> 273 us
    pallas_call x2 -> x1, Pallas kernels: 227 us -> 150 us  [collect(): pl.pallas_call(collect_kernel, out_shape=[IMAGE, IMAGE, jax.ShapeDtypeStr...]
where the time goes in v4:
time: 304 us; the launch traced here: 303 us
  Pallas kernels  273 us (90%)
  local copies, waits for them, and re-layouts  19.6 us (6%)
  other arithmetic  8.29 us (3%)
    pallas_call x1, Pallas kernels, collect(): pl.pallas_call(collect_kernel, out_shape=[IMAGE, IMAGE, jax.ShapeDtypeStr...  150 us
    pallas_call x1, Pallas kernels, spread(): pl.pallas_call(spread_kernel, out_shape=[IMAGE, IMAGE, IMAGE, PROBS, jax....  124 us

profile of v4, /device:TPU:10, one launch (start us, length us, event | category | flops | bytes accessed | tf_op | source)
XLA Modules:
  0.0 302.8 jit_solution(6627623223402399747)
XLA Ops:
  0.6 0.0 copy-start.4
  0.7 0.0 copy-start.3
  0.7 1.3 dynamic_slice.10
  2.7 0.6 broadcast_in_dim.11.mask
  3.2 0.7 convert.26
  3.9 0.7 convert.27
  4.5 0.7 convert.29
  5.2 0.7 convert.30
  5.8 0.7 convert.31
  6.5 0.7 convert_convert_fusion
  7.2 0.7 convert.32
  7.8 0.7 convert.28
  8.6 0.7 dynamic_update_slice.3
  9.2 0.2 scatter.4.rest_0_
  9.5 0.0 copy-start.9
  9.5 0.6 copy-done.9
  10.1 1.5 convert_element_type.41.rest_2_
  11.6 0.0 copy-start
  11.6 1.2 copy.32
  12.9 0.8 copy.33.rest_1_
  13.7 0.0 copy-done.3
  13.7 0.7 convert_element_type.42.rest_3_
  14.5 0.0 copy-done.4
  14.5 0.7 convert_element_type.43.rest_4_
  15.2 0.0 copy-done
  15.2 0.3 reshape.77
  15.5 0.0 copy-start.1
  15.5 1.1 pad.10.x_in
  16.6 0.6 copy-done.1
  17.2 0.3 reshape.78
  17.5 1.1 pad.11.ct_in
  18.7 123.5 %spread.1 = (bf16[4,592,256]{2,1,0:T(8,128)(2,1)}, bf16[4,592,256]{2,1,0:T(8,128)(2,1)}, bf16[4,592,256]{2,1,0:T(8,128)(2,1)}, bf16[8,2,592,592]{3,2,1,0:T(8,128...) custom-call(bf16[4,592,256]{2,1,0:T(8,128)(2,1)} %pad.10.x_in, ...), custom_call_target="tpu_custom_call" | custom-call | tf_op jit(solution)/shard_map/spread/pallas_call | solution.py:914
  142.2 149.9 %collect.1 = (bf16[4,592,256]{2,1,0:T(8,128)(2,1)}, bf16[4,592,256]{2,1,0:T(8,128)(2,1)}, f32[16,1024]{1,0:T(8,128)}, f32[1024,128]{1,0:T(8,128)}, f32[128,1024]...) custom-call(f32[4,8,256]{2,1,0:T(8,128)} %get-tuple-element.52.vectors, f32[1,256]{1,0:T(1,128)} %broadcast_in_dim.11.mask, ...), custom_call_target="tpu_custom_call" | custom-call | tf_op jit(solution)/shard_map/collect/pallas_call | solution.py:1570
  292.1 1.3 dynamic_slice.12
  293.4 1.4 slice.56
  294.7 0.0 copy-start.7
  294.7 1.3 reshape.79
  296.1 0.0 copy-start.2
  296.1 0.9 constant_dynamic-slice_fusion
  296.9 0.6 slice.60
  297.5 0.5 fusion
  298.0 0.0 copy-done.7
  298.0 0.2 copy.34
  298.2 0.9 copy.35
  299.1 0.0 copy-done.2
  299.1 0.1 slice.57
  299.2 0.0 copy-start.8
  299.2 0.0 copy-start.6
  299.2 1.3 reshape.80
  300.5 0.0 copy-done.8
  300.5 0.0 copy-start.5
  300.5 0.7 copy.42
  301.2 0.0 copy-done.6
  301.2 0.8 copy.43
  302.0 0.0 copy-done.5
  302.0 0.8 copy.44
  (4 shorter events, 0.1 us)
Async XLA Ops:
  0.6 13.8 %copy-start.4 = (f32[1024,128]{1,0:T(8,128)S(1)}, f32[1024,128]{1,0:T(8,128)}, u32[]{:S(2)}) copy-start(f32[1024,128]{1,0:T(8,128)} %param.30) | copy-start | bytes 1572868
  0.7 13.1 %copy-start.3 = (f32[128,1024]{1,0:T(8,128)S(1)}, f32[128,1024]{1,0:T(8,128)}, u32[]{:S(2)}) copy-start(f32[128,1024]{1,0:T(8,128)} %param.28) | copy-start | bytes 1572868
  9.5 0.6 copy-start.9
  11.6 3.6 %copy-start = (bf16[2308,256]{1,0:T(8,128)(2,1)S(1)}, bf16[2308,256]{1,0:T(8,128)(2,1)}, u32[]{:S(2)}) copy-start(bf16[2308,256]{1,0:T(8,128)(2,1)} %param.17) | copy-start | bytes 3545092
  15.5 1.7 copy-start.1
  294.7 3.3 %copy-start.7 = (f32[128,768]{1,0:T(8,128)S(1)}, f32[128,768]{1,0:T(8,128)}, u32[]{:S(2)}) copy-start(f32[128,768]{1,0:T(8,128)} %get-tuple-element.74) | copy-start | bytes 1179652
  296.1 3.0 %copy-start.2 = (bf16[4,592,256]{2,1,0:T(8,128)(2,1)S(1)}, bf16[4,592,256]{2,1,0:T(8,128)(2,1)}, u32[]{:S(2)}) copy-start(bf16[4,592,256]{2,1,0:T(8,128)(2,1)} %get-tuple-element.72) | copy-start | bytes 3637252
  299.2 1.3 copy-start.8
  299.2 2.0 copy-start.6
  300.5 1.5 copy-start.5

commit v5 on v4

--- a/solution.py
+++ b/solution.py
@@ -10,7 +10,7 @@
 HD = 64
 SEQ = 577
 ROWS = 592
-CHUNK = 32
+CHUNK = 96
 F32 = jnp.float32
 BF16 = jnp.bfloat16
 LAST = (((1,), (1,)), ((), ()))
@@ -790,33 +790,44 @@
 )
 
 
-def spread_kernel(x_in, ct_in, mask, *rest):
+def spread_kernel(slot_mask, x_in, ct_in, *rest):
     names, n, m = list(PARTS), len(PARTS), len(SAVED)
-    own = dict(zip(names, rest[:n]))
+    small, (w_qkv, w_out, w_fc1, w_fc2), rest = rest[:8], rest[8:12], rest[12 - n :]
     x_h, ct_h, out_h, probs_h, vectors = rest[n : n + 5]
     rest = rest[n + 5 :]
     whole_h, saved_h = dict(zip(WEIGHTS, rest[:4])), dict(zip(SAVED, rest[4 : 4 + m]))
     rest = rest[4 + m :]
-    x, ct, out, b1 = rest[:4]
-    whole = dict(zip(names, rest[4 : 4 + n]))
-    rest = rest[4 + n :]
+    x, ct, out, b1, mask, stack = rest[:6]
+    whole = dict(zip(names, rest[6 : 6 + n]))
+    rest = rest[6 + n :]
     local_sem, keep_sem = rest[0], rest[1]
     swap_sems, rest = rest[2:6], rest[6:]
     sems, refs = rest[: 6 * n], rest[6 * n :]
     p = Place()
+    own = {a: block_of(a, whole[a], p.t, p.yx, p.c) for a in names}
     f = Forward(x, whole, vectors, b1, mask, out, out_h, probs_h, saved_h, refs)
     gathers = {a: Gather(p, a, own[a], whole[a], sems[6 * i : 6 * i + 6]) for i, a in enumerate(names)}
     swaps = dict(XS=Swap(p, x_in, x, swap_sems[0:2]), CS=Swap(p, ct_in, ct, swap_sems[2:4]))
     local = [
-        pltpu.make_async_copy(own[a], block_of(a, whole[a], p.t, p.yx, p.c), local_sem.at[i])
-        for i, a in enumerate(names)
-    ]
-    local += [
-        pltpu.make_async_copy(x_in.at[p.t], x.at[p.t], local_sem.at[n]),
-        pltpu.make_async_copy(ct_in.at[p.t], ct.at[p.t], local_sem.at[n + 1]),
+        pltpu.make_async_copy(x_in.at[p.t], x.at[p.t], local_sem.at[0]),
+        pltpu.make_async_copy(ct_in.at[p.t], ct.at[p.t], local_sem.at[1]),
     ]
     for c in local:
         c.start()
+    mask[...] = jnp.full((1, 256), slot_mask[p.t].astype(F32))
+    for i in range(3):
+        own["wqkv"][:, i * 256 : i * 256 + 256] = w_qkv[i].astype(BF16)
+    own["wout"][...] = w_out[...].astype(BF16)
+    own["w1"][...] = w_fc1[...].astype(BF16)
+    own["w2"][...] = w_fc2[...].astype(BF16)
+    for row, ref in enumerate((small[0], small[1], small[2].at[0], small[2].at[1], *small[3:7])):
+        stack[row : row + 1, :] = ref[...]
+    lane = lax.broadcasted_iota(jnp.int32, (32, 256), 1)
+    row = lax.broadcasted_iota(jnp.int32, (32, 256), 0)
+    place = jnp.where(lane == row + p.d * 32, 1.0, 0.0).astype(BF16)
+    own["sv"][8:16, :] = jnp.zeros((8, 256), F32)
+    own["sv"][0:8, :] = mm(stack[...].astype(BF16), place)
+    own["sv"][8:9, 0:128] = small[7][...].astype(BF16).astype(F32)
     p.greet()
     pending = []
     settled = []
@@ -909,18 +920,19 @@
         g.finish()
 
 
-def spread(x_in, ct_in, mask, own):
+def spread(slot_mask, x_in, ct_in, small, big):
     names, n, m = list(PARTS), len(PARTS), len(SAVED)
     outs = pl.pallas_call(
         spread_kernel,
         out_shape=[IMAGE, IMAGE, IMAGE, PROBS, jax.ShapeDtypeStruct((4, 8, 256), F32)]
         + [part(a) for a in WEIGHTS]
         + list(SAVED.values()),
-        in_specs=[ANY, ANY, VM] + [ANY] * n,
+        in_specs=[pl.BlockSpec(memory_space=pltpu.SMEM), ANY, ANY] + [VM] * (len(small) + len(big)),
         out_specs=[ANY] * 4 + [VM] + [ANY] * (4 + m),
         scratch_shapes=[scratch(IMAGE), scratch(IMAGE), scratch(IMAGE), pltpu.VMEM((4, 1, 1024), F32)]
+        + [pltpu.VMEM((1, 256), F32), pltpu.VMEM((8, 32), F32)]
         + [scratch(part(a)) for a in names]
-        + [pltpu.SemaphoreType.DMA((n + 2,)), pltpu.SemaphoreType.DMA((7,))]
+        + [pltpu.SemaphoreType.DMA((2,)), pltpu.SemaphoreType.DMA((7,))]
         + Swap.SEMS * 2
         + Gather.SEMS * n
         + Forward.SCRATCH,
@@ -928,7 +940,7 @@
             collective_id=0, has_side_effects=True, vmem_limit_bytes=VMEM_BYTES
         ),
         name="spread",
-    )(x_in, ct_in, mask, *[own[a] for a in names])
+    )(slot_mask, x_in, ct_in, *small, *big)
     return outs[:5], dict(zip(WEIGHTS, outs[5:9])), dict(zip(SAVED, outs[9:]))
 
 
@@ -1050,13 +1062,17 @@
         rows, width = mine.shape
         n = min(rows, 32 if width > 128 else 256)
 
+        pieces = [(result, slice(None))]
+        if self.name == "wqkv":
+            pieces = [(result.at[i], slice(i * 256, i * 256 + 256)) for i in range(3)]
+
         def through(ref):
             @pl.loop(0, rows // n)
             def _(i):
                 r = pl.ds(pl.multiple_of(i * n, n), n)
-                result[r, :] = (mine if ref is mine else result)[r, :].astype(F32) + (
-                    0.0 if ref is mine else ref[r, :].astype(F32)
-                )
+                for to, lanes in pieces:
+                    more = ref[r, lanes].astype(F32)
+                    to[r, :] = more if ref is mine else to[r, :] + more
 
         through(mine)
         for slot, there in ((p.t, p.t > 0), (4, p.t < 3)):
@@ -1502,14 +1518,17 @@
 HBM = ("x", "out", "ct", "probs") + WEIGHTS
 
 
-def collect_kernel(vectors, mask, *rest):
+def collect_kernel(slot_mask, vectors, *rest):
     names = HBM + tuple(SAVED)
     n = len(names)
-    hbm = dict(zip(names, rest[:n]), mask=mask)
-    out_o, gtok_o, sums = rest[n : n + 3]
+    hbm = dict(zip(names, rest[:n]))
+    out_o, gtok_o = rest[n : n + 2]
     hbm |= dict(out_o=out_o, gtok_o=gtok_o)
-    results = dict(zip(REDUCED, rest[n + 3 : n + 7]))
-    rest = rest[n + 7 :]
+    results = dict(zip(REDUCED, rest[n + 2 : n + 6]))
+    small, rest = rest[n + 6 : n + 14], rest[n + 14 :]
+    mask, sums, rest = rest[0], rest[1], rest[2:]
+    mask[...] = jnp.full((1, 256), slot_mask[lax.axis_index("tensor")].astype(F32))
+    hbm["mask"] = mask
     m = len(Backward.SCRATCH)
     refs, rest = rest[:m], rest[m:]
     out_sems, tok_sems, total_refs, rest = rest[0:2], rest[2:4], rest[4:8], rest[8:]
@@ -1562,18 +1581,30 @@
                 def _():
                     act(code, m - lag)
 
+    here = pl.ds(pl.multiple_of(p.t * 256 + p.d // 4 * 128, 128), 128)
+    four = sums[0:8, here]
+    mine = sum(jnp.where(p.d % 4 == k, four[:, k * 32 : k * 32 + 32], 0.0) for k in range(4))
+    for i, row in enumerate((0, 1, None, 4, 5, 6, 7)):
+        if row is None:
+            small[i][...] = mine[2:4]
+        else:
+            small[i][...] = mine[row : row + 1]
+    hidden = sums[8:12, pl.ds(pl.multiple_of(p.d * 128, 128), 128)]
+    small[7][...] = sum(jnp.where(p.t == k, hidden[k : k + 1], 0.0) for k in range(4))
     b.finish()
 
 
-def collect(vectors, mask, hbm):
+def collect(slot_mask, vectors, hbm):
     names = HBM + tuple(SAVED)
     outs = pl.pallas_call(
         collect_kernel,
-        out_shape=[IMAGE, IMAGE, jax.ShapeDtypeStruct((16, D), F32)]
-        + [jax.ShapeDtypeStruct(PARTS[a][0][3:], F32) for a in REDUCED],
-        in_specs=[VM, VM] + [ANY] * len(names),
-        out_specs=[ANY, ANY, VM] + [VM] * 4,
-        scratch_shapes=Backward.SCRATCH
+        out_shape=[IMAGE, IMAGE]
+        + [jax.ShapeDtypeStruct((3, 128, 256) if a == "wqkv" else PARTS[a][0][3:], F32) for a in REDUCED]
+        + [jax.ShapeDtypeStruct((2 if i == 2 else 1, 128 if i == 7 else 32), F32) for i in range(8)],
+        in_specs=[pl.BlockSpec(memory_space=pltpu.SMEM), VM] + [ANY] * len(names),
+        out_specs=[ANY, ANY] + [VM] * 12,
+        scratch_shapes=[pltpu.VMEM((1, 256), F32), pltpu.VMEM((16, D), F32)]
+        + Backward.SCRATCH
         + Swap.SEMS * 2
         + Total.SCRATCH
         + sum((Reduce.scratch(a) for a in REDUCED), []),
@@ -1581,8 +1612,8 @@
             collective_id=1, has_side_effects=True, vmem_limit_bytes=VMEM_BYTES
         ),
         name="collect",
-    )(vectors, mask, *[hbm[a] for a in names])
-    return outs[0], outs[1], outs[2], dict(zip(REDUCED, outs[3:]))
+    )(slot_mask, vectors, *[hbm[a] for a in names])
+    return outs[0], outs[1], dict(zip(REDUCED, outs[2:6])), outs[6:]
 
 
 def gather_plain(w_qkv, w_out, w_fc1, w_fc2):
@@ -1634,28 +1665,20 @@
     def exchange(pieces):
         return lax.all_to_all(pieces, "tensor", split_axis=0, concat_axis=0, tiled=True)
 
-    mask = jnp.broadcast_to(
-        lax.dynamic_index_in_dim(slot_mask, lax.axis_index("tensor"), 0).astype(F32), (1, 256)
-    )
-    small = jnp.concatenate(
-        (norm1_gain, norm1_bias, b_qkv[0], b_qkv[1], b_out, norm2_gain, norm2_bias, b_fc2)
-    ).astype(BF16)
-    d, t = lax.axis_index("dp"), lax.axis_index("tensor")
     if dp == 8:
-        sv = lax.dynamic_update_slice(jnp.zeros((16, 256), F32), small.astype(F32), (0, d * 32))
-        sv = sv.at[8, 0:128].set(b_fc1[0].astype(BF16).astype(F32))
-        own = dict(
-            sv=sv,
-            wqkv=w_qkv.reshape(128, 768).astype(BF16),
-            wout=w_out.astype(BF16),
-            w1=w_fc1.astype(BF16),
-            w2=w_fc2.astype(BF16),
-        )
-        first, weights, saved = spread(images(tokens_in), images(cotangent), mask, own)
+        small = (norm1_gain, norm1_bias, b_qkv, b_out, norm2_gain, norm2_bias, b_fc2, b_fc1)
+        big = (w_qkv.transpose(1, 0, 2), w_out, w_fc1, w_fc2)
+        first, weights, saved = spread(slot_mask, images(tokens_in), images(cotangent), small, big)
         x, ct, out, probs, vectors = first
         hbm = dict(x=x, out=out, ct=ct, probs=probs, **weights, **saved)
-        out, gtok, sums, got = collect(vectors, mask, hbm)
+        out, gtok, got, g_small = collect(slot_mask, vectors, hbm)
     else:
+        mask = jnp.broadcast_to(
+            lax.dynamic_index_in_dim(slot_mask, lax.axis_index("tensor"), 0).astype(F32), (1, 256)
+        )
+        small = jnp.concatenate(
+            (norm1_gain, norm1_bias, b_qkv[0], b_qkv[1], b_out, norm2_gain, norm2_bias, b_fc2)
+        ).astype(BF16)
         vectors = lax.all_gather(
             lax.all_gather(small, "dp", axis=1, tiled=True), "tensor", axis=0
         ).astype(F32)
@@ -1669,8 +1692,7 @@
         out, probs, saved = forward(x, weights, vectors, hidden_bias, mask)
     if dp == 8:
         g_qkv, g_out, g_fc1, g_fc2 = (got[a] for a in GRADS)
-        g_small = lax.dynamic_slice(sums, (0, t * 256 + d * 32), (8, 32))
-        g_hidden = lax.dynamic_slice(sums, (8 + t, d * 128), (1, 128))
+        g_qkv = g_qkv.transpose(1, 0, 2)
     else:
         flat = [weights[a].reshape(GRADS[a].shape) for a in GRADS]
         gtok, sums, grads = backward(x, ct, *flat, vectors, mask, probs, saved)
@@ -1681,8 +1703,8 @@
             part = lax.psum_scatter(part, "tensor", scatter_dimension=0, tiled=True)
             return lax.psum_scatter(part, "dp", scatter_dimension=axis, tiled=True)
 
-        g_small = total(sums[0:8].reshape(8, 4, 256).transpose(1, 0, 2), 2)[0]
-        g_hidden = total(sums[8:12], 1)
+        s = total(sums[0:8].reshape(8, 4, 256).transpose(1, 0, 2), 2)[0]
+        g_small = (s[0:1], s[1:2], s[2:4], s[4:5], s[5:6], s[6:7], s[7:8], total(sums[8:12], 1))
 
     def rows(pieces):
         return pieces[:, :SEQ].reshape(4 * SEQ, 256)
@@ -1690,18 +1712,18 @@
     return (
         rows(out),
         rows(gtok),
-        g_small[0:1],
-        g_small[1:2],
+        g_small[0],
+        g_small[1],
         g_qkv.reshape(w_qkv.shape),
-        g_small[2:4][:, None],
+        g_small[2][:, None],
         g_out,
-        g_small[4:5],
-        g_small[5:6],
-        g_small[6:7],
+        g_small[3],
+        g_small[4],
+        g_small[5],
         g_fc1,
-        g_hidden,
+        g_small[7],
         g_fc2,
-        g_small[7:8],
+        g_small[6],
     )
 
 

time: 304 us -> 289 us (0.951)
  other arithmetic: 8.29 us -> 0 us
  local copies, waits for them, and re-layouts: 19.6 us -> 16 us
    another operation x7 -> x0, other arithmetic: 4.62 us -> none
    convert_element_type x5 -> x0, other arithmetic: 3.67 us -> none  [the longest x1 1.54 us: on_device(): w_out.astype(BF16)]
    dynamic_slice x3 -> x0, local copies, waits for them, and re-layouts: 3.44 us -> none  [the longest x1 1.33 us: on_device(): lax.dynamic_index_in_dim(slot_mask, lax.axis_index('tensor'), 0).astype(F32)]
    unnamed x25 -> x40, local copies, waits for them, and re-layouts: 5.63 us -> 7.78 us
where the time goes in v5:
time: 289 us
  Pallas kernels  272 us (94%)
  local copies, waits for them, and re-layouts  16 us (6%)
    pallas_call x1, Pallas kernels, collect(): pl.pallas_call(collect_kernel, out_shape=[IMAGE, IMAGE] + [jax.ShapeDtype...  148 us
    pallas_call x1, Pallas kernels, spread(): pl.pallas_call(spread_kernel, out_shape=[IMAGE, IMAGE, IMAGE, PROBS, jax....  124 us
    unnamed x40, local copies, waits for them, and re-layouts  7.78 us

profile of v5, /device:TPU:10, one launch (start us, length us, event | category | flops | bytes accessed | tf_op | source)
XLA Modules:
  0.0 288.6 jit_solution(5483418697022731711)
XLA Ops:
  0.6 1.6 reshape.40
  2.2 0.0 copy-start
  2.2 1.1 pad.7.x_in
  3.4 0.6 copy-done
  3.9 0.3 reshape.41
  4.3 1.1 pad.8.ct_in
  5.4 124.0 %spread.1 = (bf16[4,592,256]{2,1,0:T(8,128)(2,1)}, bf16[4,592,256]{2,1,0:T(8,128)(2,1)}, bf16[4,592,256]{2,1,0:T(8,128)(2,1)}, bf16[8,2,592,592]{3,2,1,0:T(8,128...) custom-call(s32[4]{0:T(128)} %slot_mask.3, ...), custom_call_target="tpu_custom_call" | custom-call | tf_op jit(solution)/shard_map/spread/pallas_call | solution.py:925
  129.4 147.8 %collect.1 = (bf16[4,592,256]{2,1,0:T(8,128)(2,1)}, bf16[4,592,256]{2,1,0:T(8,128)(2,1)}, f32[1024,128]{1,0:T(8,128)}, f32[128,1024]{1,0:T(8,128)}, f32[256,128]...) custom-call(s32[4]{0:T(128)} %slot_mask.3, ...), custom_call_target="tpu_custom_call" | custom-call | tf_op jit(solution)/shard_map/collect/pallas_call | solution.py:1599
  277.2 1.4 slice.6
  278.6 0.0 copy-start.1
  278.6 1.3 reshape.42
  279.9 0.0 copy-done.1
  279.9 0.1 slice.7
  280.0 0.0 copy-start.13
  280.0 0.0 copy-start.12
  280.0 0.0 copy-start.4
  280.1 0.0 copy-start.6
  280.1 0.0 copy-start.5
  280.1 0.0 copy-start.11
  280.1 0.0 copy-start.10
  280.1 0.0 copy-start.9
  280.1 0.0 copy-start.3
  280.1 1.3 reshape.43
  281.4 0.0 copy-done.13
  281.4 0.0 copy-start.8
  281.4 0.0 copy-start.2
  281.4 0.5 copy.43
  282.0 0.0 copy-done.12
  282.0 0.5 copy.44
  282.5 0.0 copy-done.4
  282.5 0.7 copy.45
  283.2 0.0 copy-done.6
  283.2 0.0 copy-start.7
  283.2 0.6 copy.46
  283.8 0.0 copy-done.5
  283.8 0.7 copy.47
  284.4 0.0 copy-done.11
  284.4 0.5 copy.48
  285.0 0.0 copy-done.10
  285.0 0.5 copy.49
  285.5 0.0 copy-done.9
  285.5 0.5 copy.50
  286.0 0.0 copy-done.3
  286.0 0.8 copy.51
  286.8 0.0 copy-done.8
  286.8 0.5 copy.52
  287.3 0.0 copy-done.2
  287.3 0.8 copy.53
  288.1 0.0 copy-done.7
  288.1 0.5 copy.54
Async XLA Ops:
  2.2 1.7 copy-start
  278.6 1.4 copy-start.1
  280.0 1.4 copy-start.13
  280.0 1.9 copy-start.12
  280.0 2.4 copy-start.4
  280.1 3.2 %copy-start.6 = (f32[2,32]{1,0:T(2,128)S(1)}, f32[2,32]{1,0:T(2,128)}, u32[]{:S(2)}) copy-start(f32[2,32]{1,0:T(2,128)} %get-tuple-element.71) | copy-start | bytes 772
  280.1 3.7 %copy-start.5 = (f32[256,128]{1,0:T(8,128)S(1)}, f32[256,128]{1,0:T(8,128)}, u32[]{:S(2)}) copy-start(f32[256,128]{1,0:T(8,128)} %get-tuple-element.128) | copy-start | bytes 393220
  280.1 4.4 %copy-start.11 = (f32[1,32]{1,0:T(1,128)S(1)}, f32[1,32]{1,0:T(1,128)}, u32[]{:S(2)}) copy-start(f32[1,32]{1,0:T(1,128)} %get-tuple-element.129) | copy-start | bytes 388
  280.1 4.9 %copy-start.10 = (f32[1,32]{1,0:T(1,128)S(1)}, f32[1,32]{1,0:T(1,128)}, u32[]{:S(2)}) copy-start(f32[1,32]{1,0:T(1,128)} %get-tuple-element.130) | copy-start | bytes 388
  280.1 5.4 %copy-start.9 = (f32[1,32]{1,0:T(1,128)S(1)}, f32[1,32]{1,0:T(1,128)}, u32[]{:S(2)}) copy-start(f32[1,32]{1,0:T(1,128)} %get-tuple-element.131) | copy-start | bytes 388
  280.1 5.9 %copy-start.3 = (f32[128,1024]{1,0:T(8,128)S(1)}, f32[128,1024]{1,0:T(8,128)}, u32[]{:S(2)}) copy-start(f32[128,1024]{1,0:T(8,128)} %get-tuple-element.132) | copy-start | bytes 1572868
  281.4 5.3 %copy-start.8 = (f32[1,128]{1,0:T(1,128)S(1)}, f32[1,128]{1,0:T(1,128)}, u32[]{:S(2)}) copy-start(f32[1,128]{1,0:T(1,128)} %get-tuple-element.133) | copy-start | bytes 1540
  281.4 5.9 %copy-start.2 = (f32[1024,128]{1,0:T(8,128)S(1)}, f32[1024,128]{1,0:T(8,128)}, u32[]{:S(2)}) copy-start(f32[1024,128]{1,0:T(8,128)} %get-tuple-element.134) | copy-start | bytes 1572868
  283.2 4.9 %copy-start.7 = (f32[1,32]{1,0:T(1,128)S(1)}, f32[1,32]{1,0:T(1,128)}, u32[]{:S(2)}) copy-start(f32[1,32]{1,0:T(1,128)} %get-tuple-element.135) | copy-start | bytes 388

commit v6 on v5

--- a/solution.py
+++ b/solution.py
@@ -790,16 +790,24 @@
 )
 
 
-def spread_kernel(slot_mask, x_in, ct_in, *rest):
+def cut(raw, pieces):
+    for i in range(4):
+        pieces[i, 576:ROWS, :] = jnp.zeros((ROWS - 576, 256), BF16)
+        for r in (*range(0, 576, CHUNK), 576):
+            n = min(CHUNK, SEQ - r)
+            pieces[i, r : r + n, :] = raw[SEQ * i + r : SEQ * i + r + n, :]
+
+
+def spread_kernel(slot_mask, x_raw, ct_raw, *rest):
     names, n, m = list(PARTS), len(PARTS), len(SAVED)
     small, (w_qkv, w_out, w_fc1, w_fc2), rest = rest[:8], rest[8:12], rest[12 - n :]
     x_h, ct_h, out_h, probs_h, vectors = rest[n : n + 5]
     rest = rest[n + 5 :]
     whole_h, saved_h = dict(zip(WEIGHTS, rest[:4])), dict(zip(SAVED, rest[4 : 4 + m]))
     rest = rest[4 + m :]
-    x, ct, out, b1, mask, stack = rest[:6]
-    whole = dict(zip(names, rest[6 : 6 + n]))
-    rest = rest[6 + n :]
+    x, ct, out, b1, mask, stack, raw, x_in, ct_in = rest[:9]
+    whole = dict(zip(names, rest[9 : 9 + n]))
+    rest = rest[9 + n :]
     local_sem, keep_sem = rest[0], rest[1]
     swap_sems, rest = rest[2:6], rest[6:]
     sems, refs = rest[: 6 * n], rest[6 * n :]
@@ -812,14 +820,9 @@
         pltpu.make_async_copy(x_in.at[p.t], x.at[p.t], local_sem.at[0]),
         pltpu.make_async_copy(ct_in.at[p.t], ct.at[p.t], local_sem.at[1]),
     ]
-    for c in local:
-        c.start()
+    raw_loads = [pltpu.make_async_copy(a, raw, local_sem.at[2 + i]) for i, a in enumerate((x_raw, ct_raw))]
+    raw_loads[0].start()
     mask[...] = jnp.full((1, 256), slot_mask[p.t].astype(F32))
-    for i in range(3):
-        own["wqkv"][:, i * 256 : i * 256 + 256] = w_qkv[i].astype(BF16)
-    own["wout"][...] = w_out[...].astype(BF16)
-    own["w1"][...] = w_fc1[...].astype(BF16)
-    own["w2"][...] = w_fc2[...].astype(BF16)
     for row, ref in enumerate((small[0], small[1], small[2].at[0], small[2].at[1], *small[3:7])):
         stack[row : row + 1, :] = ref[...]
     lane = lax.broadcasted_iota(jnp.int32, (32, 256), 1)
@@ -828,6 +831,10 @@
     own["sv"][8:16, :] = jnp.zeros((8, 256), F32)
     own["sv"][0:8, :] = mm(stack[...].astype(BF16), place)
     own["sv"][8:9, 0:128] = small[7][...].astype(BF16).astype(F32)
+    raw_loads[0].wait()
+    cut(raw, x_in)
+    raw_loads[1].start()
+    local[0].start()
     p.greet()
     pending = []
     settled = []
@@ -837,12 +844,20 @@
         c = pltpu.make_async_copy(src, dst, keep_sem.at[len(pending)])
         c.start()
         pending.append(c)
+
+    def ready(name):
+        if name == "wqkv":
+            for i in range(3):
+                own[name][:, i * 256 : i * 256 + 256] = w_qkv[i].astype(BF16)
+        elif name != "sv":
+            own[name][...] = dict(wout=w_out, w1=w_fc1, w2=w_fc2)[name][...].astype(BF16)
 
     def do(code, step):
         name, kind = ACTS[code // 100], KINDS[code // 10 % 10]
         if name in gathers:
             g = gathers[name]
             if kind == "O":
+                ready(name)
                 g.open()
             elif kind == "A":
                 g.arrive(step)
@@ -850,11 +865,14 @@
                 g.second(step)
             else:
                 if not settled:
-                    for c in local:
-                        c.wait()
+                    local[0].wait()
                     settled.append(True)
                 g.last(step)
         elif name in swaps:
+            if name == "CS":
+                raw_loads[1].wait()
+                cut(raw, ct_in)
+                local[1].start()
             swaps[name].start()
         elif name == "LN1":
             for i in range(4):
@@ -896,6 +914,7 @@
             f.finish()
             f.store_out().start()
             swaps["CS"].done()
+            local[1].wait()
             keep(ct, ct_h)
     for item in SEQUENCE:
         if isinstance(item, int):
@@ -920,7 +939,7 @@
         g.finish()
 
 
-def spread(slot_mask, x_in, ct_in, small, big):
+def spread(slot_mask, x_raw, ct_raw, small, big):
     names, n, m = list(PARTS), len(PARTS), len(SAVED)
     outs = pl.pallas_call(
         spread_kernel,
@@ -930,9 +949,9 @@
         in_specs=[pl.BlockSpec(memory_space=pltpu.SMEM), ANY, ANY] + [VM] * (len(small) + len(big)),
         out_specs=[ANY] * 4 + [VM] + [ANY] * (4 + m),
         scratch_shapes=[scratch(IMAGE), scratch(IMAGE), scratch(IMAGE), pltpu.VMEM((4, 1, 1024), F32)]
-        + [pltpu.VMEM((1, 256), F32), pltpu.VMEM((8, 32), F32)]
+        + [pltpu.VMEM((1, 256), F32), pltpu.VMEM((8, 32), F32), scratch(x_raw), scratch(IMAGE), scratch(IMAGE)]
         + [scratch(part(a)) for a in names]
-        + [pltpu.SemaphoreType.DMA((2,)), pltpu.SemaphoreType.DMA((7,))]
+        + [pltpu.SemaphoreType.DMA((4,)), pltpu.SemaphoreType.DMA((7,))]
         + Swap.SEMS * 2
         + Gather.SEMS * n
         + Forward.SCRATCH,
@@ -940,7 +959,7 @@
             collective_id=0, has_side_effects=True, vmem_limit_bytes=VMEM_BYTES
         ),
         name="spread",
-    )(slot_mask, x_in, ct_in, *small, *big)
+    )(slot_mask, x_raw, ct_raw, *small, *big)
     return outs[:5], dict(zip(WEIGHTS, outs[5:9])), dict(zip(SAVED, outs[9:]))
 
 
@@ -1668,7 +1687,7 @@
     if dp == 8:
         small = (norm1_gain, norm1_bias, b_qkv, b_out, norm2_gain, norm2_bias, b_fc2, b_fc1)
         big = (w_qkv.transpose(1, 0, 2), w_out, w_fc1, w_fc2)
-        first, weights, saved = spread(slot_mask, images(tokens_in), images(cotangent), small, big)
+        first, weights, saved = spread(slot_mask, tokens_in, cotangent, small, big)
         x, ct, out, probs, vectors = first
         hbm = dict(x=x, out=out, ct=ct, probs=probs, **weights, **saved)
         out, gtok, got, g_small = collect(slot_mask, vectors, hbm)

time: 289 us -> 286 us (0.990)
  local copies, waits for them, and re-layouts: 16 us -> 11.3 us
    unnamed x40 -> x38, local copies, waits for them, and re-layouts: 7.78 us -> 7.19 us
where the time goes in v6:
time: 286 us
  Pallas kernels  274 us (96%)
  local copies, waits for them, and re-layouts  11.3 us (4%)
    pallas_call x1, Pallas kernels, collect(): pl.pallas_call(collect_kernel, out_shape=[IMAGE, IMAGE] + [jax.ShapeDtype...  148 us
    pallas_call x1, Pallas kernels, spread(): pl.pallas_call(spread_kernel, out_shape=[IMAGE, IMAGE, IMAGE, PROBS, jax....  126 us
    unnamed x38, local copies, waits for them, and re-layouts  7.19 us

profile of v6, /device:TPU:10, one launch (start us, length us, event | category | flops | bytes accessed | tf_op | source)
XLA Modules:
  0.0 285.7 jit_solution(746855133623202958)
XLA Ops:
  0.7 125.5 %spread.1 = (bf16[4,592,256]{2,1,0:T(8,128)(2,1)}, bf16[4,592,256]{2,1,0:T(8,128)(2,1)}, bf16[4,592,256]{2,1,0:T(8,128)(2,1)}, bf16[8,2,592,592]{3,2,1,0:T(8,128...) custom-call(s32[4]{0:T(128)} %slot_mask.3, ...), custom_call_target="tpu_custom_call" | custom-call | tf_op jit(solution)/shard_map/spread/pallas_call | solution.py:944
  126.2 148.1 %collect.1 = (bf16[4,592,256]{2,1,0:T(8,128)(2,1)}, bf16[4,592,256]{2,1,0:T(8,128)(2,1)}, f32[1024,128]{1,0:T(8,128)}, f32[128,1024]{1,0:T(8,128)}, f32[256,128]...) custom-call(s32[4]{0:T(128)} %slot_mask.3, ...), custom_call_target="tpu_custom_call" | custom-call | tf_op jit(solution)/shard_map/collect/pallas_call | solution.py:1618
  274.3 1.4 slice.6
  275.7 0.0 copy-start
  275.7 1.3 reshape.34
  277.0 0.0 copy-done
  277.0 0.1 slice.7
  277.1 0.0 copy-start.12
  277.1 0.0 copy-start.11
  277.1 0.0 copy-start.3
  277.1 0.0 copy-start.5
  277.1 0.0 copy-start.4
  277.1 0.0 copy-start.10
  277.1 0.0 copy-start.9
  277.2 0.0 copy-start.8
  277.2 0.0 copy-start.2
  277.2 1.3 reshape.35
  278.5 0.0 copy-done.12
  278.5 0.0 copy-start.7
  278.5 0.0 copy-start.1
  278.5 0.5 copy.43
  279.0 0.0 copy-done.11
  279.0 0.5 copy.44
  279.5 0.0 copy-done.3
  279.5 0.7 copy.45
  280.3 0.0 copy-done.5
  280.3 0.0 copy-start.6
  280.3 0.6 copy.46
  280.9 0.0 copy-done.4
  280.9 0.7 copy.47
  281.5 0.0 copy-done.10
  281.5 0.5 copy.48
  282.0 0.0 copy-done.9
  282.0 0.5 copy.49
  282.5 0.0 copy-done.8
  282.5 0.5 copy.50
  283.1 0.0 copy-done.2
  283.1 0.8 copy.51
  283.8 0.0 copy-done.7
  283.9 0.5 copy.52
  284.4 0.0 copy-done.1
  284.4 0.8 copy.53
  285.2 0.0 copy-done.6
  285.2 0.5 copy.54
Async XLA Ops:
  275.7 1.4 copy-start
  277.1 1.4 copy-start.12
  277.1 1.9 copy-start.11
  277.1 2.4 copy-start.3
  277.1 3.2 %copy-start.5 = (f32[2,32]{1,0:T(2,128)S(1)}, f32[2,32]{1,0:T(2,128)}, u32[]{:S(2)}) copy-start(f32[2,32]{1,0:T(2,128)} %get-tuple-element.71) | copy-start | bytes 772
  277.1 3.7 %copy-start.4 = (f32[256,128]{1,0:T(8,128)S(1)}, f32[256,128]{1,0:T(8,128)}, u32[]{:S(2)}) copy-start(f32[256,128]{1,0:T(8,128)} %get-tuple-element.128) | copy-start | bytes 393220
  277.1 4.4 %copy-start.10 = (f32[1,32]{1,0:T(1,128)S(1)}, f32[1,32]{1,0:T(1,128)}, u32[]{:S(2)}) copy-start(f32[1,32]{1,0:T(1,128)} %get-tuple-element.129) | copy-start | bytes 388
  277.1 4.9 %copy-start.9 = (f32[1,32]{1,0:T(1,128)S(1)}, f32[1,32]{1,0:T(1,128)}, u32[]{:S(2)}) copy-start(f32[1,32]{1,0:T(1,128)} %get-tuple-element.130) | copy-start | bytes 388
  277.2 5.4 %copy-start.8 = (f32[1,32]{1,0:T(1,128)S(1)}, f32[1,32]{1,0:T(1,128)}, u32[]{:S(2)}) copy-start(f32[1,32]{1,0:T(1,128)} %get-tuple-element.131) | copy-start | bytes 388
  277.2 5.9 %copy-start.2 = (f32[128,1024]{1,0:T(8,128)S(1)}, f32[128,1024]{1,0:T(8,128)}, u32[]{:S(2)}) copy-start(f32[128,1024]{1,0:T(8,128)} %get-tuple-element.132) | copy-start | bytes 1572868
  278.5 5.3 %copy-start.7 = (f32[1,128]{1,0:T(1,128)S(1)}, f32[1,128]{1,0:T(1,128)}, u32[]{:S(2)}) copy-start(f32[1,128]{1,0:T(1,128)} %get-tuple-element.133) | copy-start | bytes 1540
  278.5 5.9 %copy-start.1 = (f32[1024,128]{1,0:T(8,128)S(1)}, f32[1024,128]{1,0:T(8,128)}, u32[]{:S(2)}) copy-start(f32[1024,128]{1,0:T(8,128)} %get-tuple-element.134) | copy-start | bytes 1572868
  280.3 4.9 %copy-start.6 = (f32[1,32]{1,0:T(1,128)S(1)}, f32[1,32]{1,0:T(1,128)}, u32[]{:S(2)}) copy-start(f32[1,32]{1,0:T(1,128)} %get-tuple-element.135) | copy-start | bytes 388

commit v7 on v6

--- a/solution.py
+++ b/solution.py
@@ -831,13 +831,8 @@
     own["sv"][8:16, :] = jnp.zeros((8, 256), F32)
     own["sv"][0:8, :] = mm(stack[...].astype(BF16), place)
     own["sv"][8:9, 0:128] = small[7][...].astype(BF16).astype(F32)
-    raw_loads[0].wait()
-    cut(raw, x_in)
-    raw_loads[1].start()
-    local[0].start()
     p.greet()
     pending = []
-    settled = []
     resid_stored = f.stores(("resid",))
 
     def keep(src, dst):
@@ -864,12 +859,14 @@
             elif kind == "S":
                 g.second(step)
             else:
-                if not settled:
-                    local[0].wait()
-                    settled.append(True)
                 g.last(step)
         elif name in swaps:
-            if name == "CS":
+            if name == "XS":
+                raw_loads[0].wait()
+                cut(raw, x_in)
+                raw_loads[1].start()
+                local[0].start()
+            else:
                 raw_loads[1].wait()
                 cut(raw, ct_in)
                 local[1].start()
@@ -883,6 +880,7 @@
                 for d in range(8):
                     b1[t, :, d * 128 : d * 128 + 128] = sv[t, d // 2, d % 2, 8:9, 0:128]
             swaps["XS"].done()
+            local[0].wait()
             keep(x, x_h)
             f.start_norm()
         elif name == "Q":

time: 286 us -> 284 us (level)
  no operation moved by 1% of the time
where the time goes in v7:
time: 284 us
  Pallas kernels  272 us (96%)
  local copies, waits for them, and re-layouts  11.3 us (4%)
    pallas_call x1, Pallas kernels, collect(): pl.pallas_call(collect_kernel, out_shape=[IMAGE, IMAGE] + [jax.ShapeDtype...  148 us
    pallas_call x1, Pallas kernels, spread(): pl.pallas_call(spread_kernel, out_shape=[IMAGE, IMAGE, IMAGE, PROBS, jax....  124 us
    unnamed x38, local copies, waits for them, and re-layouts  7.19 us

profile of v7, /device:TPU:10, one launch (start us, length us, event | category | flops | bytes accessed | tf_op | source)
XLA Modules:
  0.0 284.2 jit_solution(3019387773598234607)
XLA Ops:
  0.7 124.0 %spread.1 = (bf16[4,592,256]{2,1,0:T(8,128)(2,1)}, bf16[4,592,256]{2,1,0:T(8,128)(2,1)}, bf16[4,592,256]{2,1,0:T(8,128)(2,1)}, bf16[8,2,592,592]{3,2,1,0:T(8,128...) custom-call(s32[4]{0:T(128)} %slot_mask.3, ...), custom_call_target="tpu_custom_call" | custom-call | tf_op jit(solution)/shard_map/spread/pallas_call | solution.py:942
  124.7 148.1 %collect.1 = (bf16[4,592,256]{2,1,0:T(8,128)(2,1)}, bf16[4,592,256]{2,1,0:T(8,128)(2,1)}, f32[1024,128]{1,0:T(8,128)}, f32[128,1024]{1,0:T(8,128)}, f32[256,128]...) custom-call(s32[4]{0:T(128)} %slot_mask.3, ...), custom_call_target="tpu_custom_call" | custom-call | tf_op jit(solution)/shard_map/collect/pallas_call | solution.py:1616
  272.8 1.4 slice.6
  274.1 0.0 copy-start
  274.1 1.3 reshape.34
  275.5 0.0 copy-done
  275.5 0.1 slice.7
  275.6 0.0 copy-start.12
  275.6 0.0 copy-start.11
  275.6 0.0 copy-start.3
  275.6 0.0 copy-start.5
  275.6 0.0 copy-start.4
  275.6 0.0 copy-start.10
  275.6 0.0 copy-start.9
  275.6 0.0 copy-start.8
  275.7 0.0 copy-start.2
  275.7 1.3 reshape.35
  277.0 0.0 copy-done.12
  277.0 0.0 copy-start.7
  277.0 0.0 copy-start.1
  277.0 0.5 copy.43
  277.5 0.0 copy-done.11
  277.5 0.5 copy.44
  278.0 0.0 copy-done.3
  278.0 0.7 copy.45
  278.8 0.0 copy-done.5
  278.8 0.0 copy-start.6
  278.8 0.6 copy.46
  279.3 0.0 copy-done.4
  279.3 0.7 copy.47
  280.0 0.0 copy-done.10
  280.0 0.5 copy.48
  280.5 0.0 copy-done.9
  280.5 0.5 copy.49
  281.0 0.0 copy-done.8
  281.0 0.5 copy.50
  281.5 0.0 copy-done.2
  281.5 0.8 copy.51
  282.3 0.0 copy-done.7
  282.3 0.5 copy.52
  282.8 0.0 copy-done.1
  282.8 0.8 copy.53
  283.6 0.0 copy-done.6
  283.6 0.5 copy.54
Async XLA Ops:
  274.1 1.4 copy-start
  275.6 1.4 copy-start.12
  275.6 1.9 copy-start.11
  275.6 2.4 copy-start.3
  275.6 3.2 %copy-start.5 = (f32[2,32]{1,0:T(2,128)S(1)}, f32[2,32]{1,0:T(2,128)}, u32[]{:S(2)}) copy-start(f32[2,32]{1,0:T(2,128)} %get-tuple-element.71) | copy-start | bytes 772
  275.6 3.7 %copy-start.4 = (f32[256,128]{1,0:T(8,128)S(1)}, f32[256,128]{1,0:T(8,128)}, u32[]{:S(2)}) copy-start(f32[256,128]{1,0:T(8,128)} %get-tuple-element.128) | copy-start | bytes 393220
  275.6 4.4 %copy-start.10 = (f32[1,32]{1,0:T(1,128)S(1)}, f32[1,32]{1,0:T(1,128)}, u32[]{:S(2)}) copy-start(f32[1,32]{1,0:T(1,128)} %get-tuple-element.129) | copy-start | bytes 388
  275.6 4.9 %copy-start.9 = (f32[1,32]{1,0:T(1,128)S(1)}, f32[1,32]{1,0:T(1,128)}, u32[]{:S(2)}) copy-start(f32[1,32]{1,0:T(1,128)} %get-tuple-element.130) | copy-start | bytes 388
  275.6 5.4 %copy-start.8 = (f32[1,32]{1,0:T(1,128)S(1)}, f32[1,32]{1,0:T(1,128)}, u32[]{:S(2)}) copy-start(f32[1,32]{1,0:T(1,128)} %get-tuple-element.131) | copy-start | bytes 388
  275.7 5.9 %copy-start.2 = (f32[128,1024]{1,0:T(8,128)S(1)}, f32[128,1024]{1,0:T(8,128)}, u32[]{:S(2)}) copy-start(f32[128,1024]{1,0:T(8,128)} %get-tuple-element.132) | copy-start | bytes 1572868
  277.0 5.3 %copy-start.7 = (f32[1,128]{1,0:T(1,128)S(1)}, f32[1,128]{1,0:T(1,128)}, u32[]{:S(2)}) copy-start(f32[1,128]{1,0:T(1,128)} %get-tuple-element.133) | copy-start | bytes 1540
  277.0 5.9 %copy-start.1 = (f32[1024,128]{1,0:T(8,128)S(1)}, f32[1024,128]{1,0:T(8,128)}, u32[]{:S(2)}) copy-start(f32[1024,128]{1,0:T(8,128)} %get-tuple-element.134) | copy-start | bytes 1572868
  278.8 4.9 %copy-start.6 = (f32[1,32]{1,0:T(1,128)S(1)}, f32[1,32]{1,0:T(1,128)}, u32[]{:S(2)}) copy-start(f32[1,32]{1,0:T(1,128)} %get-tuple-element.135) | copy-start | bytes 388
